TPU v7x, 512 devices: a whole 4x4x16 slice. The times are simulated.
512 devices in a mesh: band: 8 (over y, z_hi), chan: 64 (over z_lo, x, core).
Axes of the slice: x: 4, y: 4, z: 16 (z_hi: 2, z_lo: 8; z = z_hi * 8 + z_lo), core: 2. Of those that a mesh axis runs over, the one named last changes fastest.
Arguments:
- field: bfloat16 [256, 16, 128, 360], P('chan', None, 'band'), may hold values from -6 to 6
- noise_level: int32 [16], replicated, may hold values from 0 to 19
- conv_kernel: float32 [2, 256, 7, 7], P(None, 'chan'), may hold values from -0.875 to 0.875
- conv_bias: float32 [2, 256], P(None, 'chan'), may hold values from -3 to 3
- modulation: float32 [2, 20, 2, 256], replicated, may hold values from -3 to 3
- expand_weight: bfloat16 [2, 256, 1024], replicated, may hold values from -0.375 to 0.375
- expand_bias: float32 [2, 1024], replicated, may hold values from -3 to 3
- project_weight: bfloat16 [2, 1024, 256], replicated, may hold values from -0.1875 to 0.1875
- project_bias: float32 [2, 256], replicated, may hold values from -3 to 3
- layer_scale: float32 [2, 256], replicated, may hold values from 0.3 to 1.5
Outputs:
- updated: bfloat16 [256, 16, 128, 360], P('chan', None, 'band')
All inputs are finite; a program needn't handle non-finite values.
Results may differ from a plain program's by a relative error of at most 0.0069.
Values may be sent and summed in bfloat16 or wider, within the bound.
No kernel may reach another device: no remote copies, remote signals or barrier semaphores. Data moves between devices by JAX's collectives and lax.ppermute only.
A program may use at most 64 MiB of HBM per device.

v0:
```python
import jax
import jax.numpy as jnp
from jax import lax
from jax.experimental import pallas as pl
from jax.experimental.pallas import tpu as pltpu
from jax.sharding import Mesh, PartitionSpec as P

EPS = 1e-06
LANES = 128
TAPS = 7
REACH = 3
LEFT = 8


def lane_iota(rows):
    return lax.broadcasted_iota(jnp.int32, (rows, LANES), 1)


def moved_lanes(load, spans, rows):
    lanes = lane_iota(rows)
    tile = jnp.zeros((rows, LANES), jnp.float32)
    for source, src, dst, width in spans:
        done = 0
        while done < width:
            part, lane = divmod(src + done, LANES)
            take = min(width - done, LANES - lane)
            value = load(source, part)
            shift = (dst + done - lane) % LANES
            if shift:
                value = pltpu.roll(value, shift, 1)
            lo, hi = dst + done, dst + done + take
            tile = jnp.where((lanes >= lo) & (lanes < hi), value, tile)
            done += take
    return tile


def spans_of(total, count, stride, width, tile_index, start_of):
    spans = []
    for item in range(count):
        lo = max(item * stride, tile_index * LANES)
        hi = min(item * stride + width, (tile_index + 1) * LANES)
        if lo < hi:
            spans.append((item, start_of(item) + lo - item * stride, lo - tile_index * LANES, hi - lo))
    return spans


def cut_kernel(field_ref, out_ref, wide, cut, *, seg, slot):
    chans, members, lats, lons = field_ref.shape
    rows = chans * members
    parts = -(-lons // LANES)
    segs = lons // seg
    tiles = lats * slot // LANES
    for a in range(parts):
        lo, hi = a * LANES, min((a + 1) * LANES, lons)
        piece = field_ref[:, :, :, lo:hi].astype(jnp.float32).reshape(rows * lats, hi - lo)
        wide[a, :, 0 : hi - lo] = piece
    for s in range(segs):
        for t in range(tiles):
            spans = spans_of(0, lats, slot, seg, t, lambda item: s * seg)

            def load(lat, part):
                return wide[part, pl.ds(lat, rows, stride=lats), :]

            tile = moved_lanes(load, spans, rows)
            for c in range(chans):
                start = s * chans * tiles + c * tiles + t
                cut[pl.ds(start, members, stride=segs * chans * tiles), :] = tile[
                    c * members : (c + 1) * members
                ]
    out_ref[...] = cut[...].astype(jnp.bfloat16)


def paste_kernel(in_ref, out_ref, cut, wide, *, seg, slot):
    chans, members, lats, lons = out_ref.shape
    rows = chans * members
    parts = -(-lons // LANES)
    segs = lons // seg
    tiles = lats * slot // LANES
    cut[...] = in_ref[...].astype(jnp.float32)
    for lat in range(lats):
        for a in range(parts):
            spans = spans_of(0, segs, seg, seg, a, lambda item: lat * slot)

            def load(s, part):
                return jnp.concatenate(
                    [
                        cut[
                            pl.ds(
                                s * chans * tiles + c * tiles + part,
                                members,
                                stride=segs * chans * tiles,
                            ),
                            :,
                        ]
                        for c in range(chans)
                    ],
                    axis=0,
                )

            wide[a, pl.ds(lat, rows, stride=lats), :] = moved_lanes(load, spans, rows)
    for a in range(parts):
        lo, hi = a * LANES, min((a + 1) * LANES, lons)
        out_ref[:, :, :, lo:hi] = (
            wide[a, :, 0 : hi - lo].reshape(chans, members, lats, hi - lo).astype(jnp.bfloat16)
        )


def to_cells_kernel(in_ref, out_ref, rows32, *, tiles):
    channels = out_ref.shape[1]
    halves = in_ref.shape[0] // (channels * tiles)
    rows32[...] = in_ref[...].astype(jnp.float32)
    for half in range(halves):
        for t in range(tiles):
            block = rows32[pl.ds(half * channels * tiles + t, channels, stride=tiles), :]
            start = (half * tiles + t) * LANES
            out_ref[start : start + LANES, :] = block.T.astype(jnp.bfloat16)


def to_channels_kernel(in_ref, out_ref, rows32, *, tiles):
    channels = in_ref.shape[1]
    halves = out_ref.shape[0] // (channels * tiles)
    for half in range(halves):
        for t in range(tiles):
            start = (half * tiles + t) * LANES
            block = in_ref[start : start + LANES, :].astype(jnp.float32)
            rows32[pl.ds(half * channels * tiles + t, channels, stride=tiles), :] = block.T
    out_ref[...] = rows32[...].astype(jnp.bfloat16)


def block_kernel(
    x_ref, top_ref, bottom_ref, left_ref, right_ref, taps_ref, mod_ref,
    up_ref, up_bias_ref, down_ref, down_bias_ref, scale_ref,
    out_ref, padded, spread, mixed,
):
    lats, slot, channels = x_ref.shape
    groups = channels // LANES
    col_tiles = slot // 8
    row_block = 8
    for g in range(groups):
        ch = slice(g * LANES, (g + 1) * LANES)
        padded[g, 0:REACH, LEFT : LEFT + slot, :] = top_ref[:, :, ch].astype(jnp.float32)
        padded[g, REACH : REACH + lats, LEFT : LEFT + slot, :] = x_ref[:, :, ch].astype(jnp.float32)
        padded[g, REACH + lats :, LEFT : LEFT + slot, :] = bottom_ref[:, :, ch].astype(jnp.float32)
        padded[g, :, LEFT + slot :, :] = jnp.zeros(
            (lats + 2 * REACH, padded.shape[2] - LEFT - slot, LANES), jnp.float32
        )
        padded[g, :, LEFT - REACH : LEFT, :] = left_ref[:, :, ch].astype(jnp.float32)
        right_at = LEFT + slot - REACH
        padded[g, :, right_at : right_at + REACH, :] = right_ref[:, :, ch].astype(jnp.float32)
        for k in range(TAPS * TAPS + 1):
            spread[g, k] = jnp.broadcast_to(taps_ref[k : k + 1, ch], (8, LANES))

    def conv_step(step, carry):
        g = step // (lats // row_block)
        row = (step % (lats // row_block)) * row_block
        for k in range(col_tiles):
            sums = [spread[g, TAPS * TAPS]] * row_block
            for j in range(TAPS):
                col = LEFT - REACH + j + 8 * k
                weights = [spread[g, i * TAPS + j] for i in range(TAPS)]
                for r in range(row_block + TAPS - 1):
                    value = padded[g, row + r, col : col + 8, :]
                    for i in range(TAPS):
                        if 0 <= r - i < row_block:
                            sums[r - i] = sums[r - i] + weights[i] * value
            for r in range(row_block):
                mixed[g, row + r, 8 * k : 8 * k + 8, :] = sums[r]
        return carry

    lax.fori_loop(0, groups * (lats // row_block), conv_step, 0)
    mlp_rows = 8
    cells = mlp_rows * slot
    average_matrix = jnp.full((channels, channels), 1.0 / channels, jnp.bfloat16)

    def mlp_step(step, carry):
        row = step * mlp_rows
        parts = [
            mixed[g, pl.ds(row, mlp_rows), :, :].reshape(cells, LANES) for g in range(groups)
        ]
        rounded = jnp.concatenate(parts, axis=1).astype(jnp.bfloat16)
        average = jnp.dot(rounded, average_matrix, preferred_element_type=jnp.float32)
        centered = rounded.astype(jnp.float32) - average
        variance = jnp.dot(
            (centered * centered).astype(jnp.bfloat16),
            average_matrix,
            preferred_element_type=jnp.float32,
        )
        normed = centered * lax.rsqrt(variance + EPS) * (1.0 + mod_ref[0:1, :]) + mod_ref[1:2, :]
        hidden = (
            jnp.dot(normed.astype(jnp.bfloat16), up_ref[0], preferred_element_type=jnp.float32)
            + up_bias_ref[...]
        )
        active = (0.5 * hidden * (1.0 + lax.erf(hidden * 0.7071067811865476))).astype(jnp.bfloat16)
        result = (
            jnp.dot(active, down_ref[0], preferred_element_type=jnp.float32) + down_bias_ref[...]
        )
        branch = (scale_ref[...] * result).astype(jnp.bfloat16).astype(jnp.float32)
        current = x_ref[pl.ds(row, mlp_rows), :, :].astype(jnp.float32)
        out_ref[pl.ds(row, mlp_rows), :, :] = (
            current + branch.reshape(mlp_rows, slot, channels)
        ).astype(jnp.bfloat16)
        return carry

    lax.fori_loop(0, lats // mlp_rows, mlp_step, 0)


def whole(shape):
    return pl.BlockSpec(shape, lambda *_: (0,) * len(shape))


def run_cut(field, seg, slot):
    chans, members, lats, lons = field.shape
    tiles = lats * slot // LANES
    rows = members * (lons // seg) * chans * tiles
    return pl.pallas_call(
        lambda *refs: cut_kernel(*refs, seg=seg, slot=slot),
        out_shape=jax.ShapeDtypeStruct((rows, LANES), jnp.bfloat16),
        scratch_shapes=[
            pltpu.VMEM((-(-lons // LANES), chans * members * lats, LANES), jnp.float32),
            pltpu.VMEM((rows, LANES), jnp.float32),
        ],
        name="cut",
    )(field)


def run_paste(pieces, shape, seg, slot):
    chans, members, lats, lons = shape
    return pl.pallas_call(
        lambda *refs: paste_kernel(*refs, seg=seg, slot=slot),
        out_shape=jax.ShapeDtypeStruct(shape, jnp.bfloat16),
        scratch_shapes=[
            pltpu.VMEM(pieces.shape, jnp.float32),
            pltpu.VMEM((-(-lons // LANES), chans * members * lats, LANES), jnp.float32),
        ],
        name="paste",
    )(pieces)


def run_to_cells(pieces, cells, channels, tiles):
    return pl.pallas_call(
        lambda *refs: to_cells_kernel(*refs, tiles=tiles),
        out_shape=jax.ShapeDtypeStruct((cells, channels), jnp.bfloat16),
        scratch_shapes=[pltpu.VMEM(pieces.shape, jnp.float32)],
        name="to_cells",
    )(pieces)


def run_to_channels(x, tiles):
    rows = x.shape[0] * x.shape[1] // LANES
    return pl.pallas_call(
        lambda *refs: to_channels_kernel(*refs, tiles=tiles),
        out_shape=jax.ShapeDtypeStruct((rows, LANES), jnp.bfloat16),
        scratch_shapes=[pltpu.VMEM((rows, LANES), jnp.float32)],
        name="to_channels",
    )(x)


def run_block(x, halos, taps, mod, layer, up, up_bias, down, down_bias, scale):
    lats, slot, channels = x.shape
    groups = channels // LANES
    hidden = up.shape[2]
    arrays = (x, *halos, taps, mod)
    return pl.pallas_call(
        block_kernel,
        grid=(1,),
        out_shape=jax.ShapeDtypeStruct(x.shape, jnp.bfloat16),
        in_specs=[whole(a.shape) for a in arrays]
        + [
            pl.BlockSpec((1, channels, hidden), lambda _: (layer, 0, 0)),
            whole((1, hidden)),
            pl.BlockSpec((1, hidden, channels), lambda _: (layer, 0, 0)),
            whole((1, channels)),
            whole((1, channels)),
        ],
        out_specs=whole(x.shape),
        scratch_shapes=[
            pltpu.VMEM((groups, lats + 2 * REACH, LEFT + slot + 8, LANES), jnp.float32),
            pltpu.VMEM((groups, TAPS * TAPS + 1, 8, LANES), jnp.float32),
            pltpu.VMEM((groups, lats, slot, LANES), jnp.float32),
        ],
        name="block",
    )(
        *arrays,
        up, up_bias[layer][None], down, down_bias[layer][None], scale[layer][None],
    )


def halo_of(x, seg):
    rows, segs = lax.axis_size("y"), lax.axis_size("xc")
    down = [(i, i + 1) for i in range(rows - 1)]
    up = [(j, i) for i, j in down]
    top = lax.ppermute(x[-REACH:], "y", down)
    bottom = lax.ppermute(x[:REACH], "y", up)
    east = [(i, (i + 1) % segs) for i in range(segs)]
    west = [(j, i) for i, j in east]

    def columns(lo):
        return jnp.concatenate(
            [part[:, lo : lo + REACH] for part in (top, x, bottom)], axis=0
        )

    left = lax.ppermute(columns(seg - REACH), "xc", east)
    right = lax.ppermute(columns(0), "xc", west)
    return top, bottom, left, right


def on_device(
    field, noise_level, conv_kernel, conv_bias, modulation,
    expand_weight, expand_bias, project_weight, project_bias, layer_scale,
):
    chans, members, lats, lons = field.shape
    layers = conv_kernel.shape[0]
    halves = lax.axis_size("zh")
    segs = lax.axis_size("xc")
    peers = halves * lax.axis_size("zl") * segs
    channels = chans * lax.axis_size("zl") * segs
    seg = lons // segs
    slot = -(-seg // 8) * 8
    tiles = lats * slot // LANES
    member = lax.axis_index("zh") * lax.axis_size("zl") + lax.axis_index("zl")
    mods = modulation[:, noise_level[member]]

    filters = jnp.concatenate(
        [conv_kernel.reshape(layers, chans, TAPS * TAPS), conv_bias[:, :, None]], axis=2
    )
    filters = jnp.broadcast_to(filters.reshape(1, -1), (channels // chans, filters.size))
    filters = lax.all_to_all(filters, ("zl", "xc"), 0, 0, tiled=True)
    filters = filters.reshape(channels // chans, layers, chans, TAPS * TAPS + 1)
    filters = filters.transpose(1, 3, 0, 2).reshape(layers, TAPS * TAPS + 1, channels)

    pieces = run_cut(field, seg, slot)
    shape = (peers, chans * tiles, LANES)
    around = ("zh", "zl", "xc")
    pieces = lax.all_to_all(pieces.reshape(shape), around, 0, 0, tiled=True).reshape(-1, LANES)
    x = run_to_cells(pieces, halves * lats * slot, channels, tiles)
    x = x.reshape(halves * lats, slot, channels)
    for layer in range(layers):
        halos = halo_of(x, seg)
        x = run_block(
            x, halos, filters[layer], mods[layer], layer,
            expand_weight, expand_bias, project_weight, project_bias, layer_scale,
        )
    pieces = run_to_channels(x.reshape(-1, channels), tiles)
    pieces = lax.all_to_all(pieces.reshape(shape), around, 0, 0, tiled=True).reshape(-1, LANES)
    return run_paste(pieces, field.shape, seg, slot)


def solution(mesh):
    bands, chan = mesh.shape["band"], mesh.shape["chan"]
    split = Mesh(mesh.devices.reshape(bands // 2, 2, chan // 8, 8), ("y", "zh", "zl", "xc"))
    band, group = ("y", "zh"), ("zl", "xc")
    return jax.shard_map(
        on_device,
        mesh=split,
        in_specs=(
            P(group, None, band, None),
            P(),
            P(None, group, None, None),
            P(None, group),
            P(), P(), P(), P(), P(), P(),
        ),
        out_specs=P(group, None, band, None),
        check_vma=False,
    )
```

profile of v0, /device:TPU:41, one launch (start us, length us, event | category | flops | bytes accessed | tf_op | source)
XLA Modules:
  0.0 214.2 jit_solution(10442143981374369741)
XLA Ops:
  0.0 0.7 copy-done.12
  0.7 0.1 copy.17
  0.8 0.8 copy.16
  1.5 0.1 reshape.48
  1.6 0.1 pad_maximum_fusion.4
  1.7 0.1 broadcast_in_dim.11
  1.8 0.7 broadcast_in_dim.12
  2.5 16.0 %all-to-all-start.1 = ((f32[64,1,400]{2,1,0:T(1,128)}), f32[64,1,400]{2,1,0:T(1,128)S(1)}, u32[]{:S(2)}, u32[]{:S(2)}) async-start(f32[64,1,400]{2,1,0:T(1,128)} %broadcast_in_dim.12), calls=%async_computation.1 | async-start | bytes 262144 | tf_op jit(solution)/shard_map/all_to_all | solution.py:327
  18.5 5.0 %cut.1 = bf16[3072,128]{1,0:T(8,128)(2,1)} custom-call(bf16[4,16,16,360]{3,2,1,0:T(8,128)(2,1)} %refs_0_.1), custom_call_target="tpu_custom_call" | custom-call | tf_op jit(solution)/shard_map/cut/pallas_call | solution.py:215
  23.4 8.5 %all-to-all-done.1 = f32[64,1,400]{2,1,0:T(1,128)S(1)} async-done(((f32[64,1,400]{2,1,0:T(1,128)}), f32[64,1,400]{2,1,0:T(1,128)S(1)}, u32[]{:S(2)}, u32[]{:S(2)}) %all-to-all-start.1) | async-done | bytes 102432 | tf_op jit(solution)/shard_map/all_to_all | solution.py:327
  32.0 11.0 %all-to-all-start = ((bf16[128,24,128]{2,1,0:T(8,128)(2,1)}), bf16[128,24,128]{2,1,0:T(8,128)(2,1)S(1)}, u32[]{:S(2)}, u32[]{:S(2)}) async-start(bf16[128,24,128]{2,1,0:T(8,128)(2,1)} %bitcast.19), calls=%async_computation | async-start | bytes 1572864 | tf_op jit(solution)/shard_map/all_to_all | solution.py:334
  43.0 0.0 copy-start.10
  43.0 0.0 copy-start.11
  43.0 0.0 copy-start.13
  43.0 0.6 copy-done.13
  43.6 0.6 dynamic_slice.6
  45.9 0.0 copy-start.9
  45.9 1.3 dynamic-slice_bitcast_fusion
  47.2 0.0 copy-done.10
  47.2 0.0 copy-done.11
  47.2 0.6 fusion.10
  47.8 0.6 fusion.9
  48.4 0.3 reduce
  48.7 0.3 reshape.49
  49.0 38.5 %all-to-all-done = bf16[128,24,128]{2,1,0:T(8,128)(2,1)S(1)} async-done(((bf16[128,24,128]{2,1,0:T(8,128)(2,1)}), bf16[128,24,128]{2,1,0:T(8,128)(2,1)S(1)}, u32[]{:S(2)}, u32[]{:S(2)}) %all-to-all-start) | async-done | bytes 786464 | tf_op jit(solution)/shard_map/all_to_all | solution.py:334
  87.5 0.9 copy-done
  88.4 2.3 %to_cells.1 = bf16[1536,256]{1,0:T(8,128)(2,1)} custom-call(bf16[3072,128]{1,0:T(8,128)(2,1)} %bitcast.20), custom_call_target="tpu_custom_call" | custom-call | tf_op jit(solution)/shard_map/to_cells/pallas_call | solution.py:240
  90.8 0.9 fusion.3
  91.7 3.2 %collective-permute-start = (bf16[3,48,256]{2,1,0:T(8,128)(2,1)S(1)}, bf16[3,48,256]{2,1,0:T(8,128)(2,1)S(1)}, u32[]{:S(2)}, u32[]{:S(2)}) collective-permute-start(bf16[3,48,256]{2,1,0:T(8,128)(2,1)S(1)} %bitcast.28), channel_id=1, source_target_pairs={{0,128},{128,256},{256,384},{1,129},{129,257},{257,385},{2,130},{1... | collective-permute-start | bytes 221192 | tf_op jit(solution)/shard_map/ppermute | solution.py:292
  94.9 1.0 fusion.2
  95.9 2.1 collective-permute-start.1
  98.0 0.0 collective-permute-done.top_ref
  98.1 3.4 %collective-permute-done.1.bottom_ref = bf16[3,48,256]{2,1,0:T(8,128)(2,1)S(1)} collective-permute-done((bf16[3,48,256]{2,1,0:T(8,128)(2,1)S(1)}, bf16[3,48,256]{2,1,0:T(8,128)(2,1)S(1)}, u32[]{:S(2)}, u32[]{:S(2)}) %collective-permute-start.1) | collective-permute-done | bytes 73760 | tf_op jit(solution)/shard_map/ppermute | solution.py:293
  101.4 0.1 pad_maximum_fusion
  101.5 0.5 copy-done.3
  102.0 1.3 collective-permute-start.2
  103.3 0.1 pad_maximum_fusion.1
  103.4 0.0 collective-permute-start.3
  103.5 0.7 copy.18.taps_ref
  104.2 0.6 collective-permute-done.2.left_ref
  104.8 2.7 %collective-permute-done.3.right_ref = bf16[38,3,256]{2,1,0:T(4,128)(2,1)S(1)} collective-permute-done((bf16[38,3,256]{2,1,0:T(4,128)(2,1)S(1)}, bf16[38,3,256]{2,1,0:T(4,128)(2,1)S(1)}, u32[]{:S(2)}, u32[]{:S(2)}) %collective-permute-start.3) | collective-permute-done | bytes 58400 | tf_op jit(solution)/shard_map/ppermute | solution.py:303
  107.5 0.6 copy-done.7
  108.2 13.8 %block.2.x_ref = bf16[32,48,256]{2,1,0:T(8,128)(2,1)} custom-call(bf16[32,48,256]{2,1,0:T(8,128)(2,1)} %bitcast.18, bf16[3,48,256]{2,1,0:T(8,128)(2,1)} %copy-done.1, bf16[3,48,256]{2,1,0:T(8,128)(2,1)} %copy-done.3, bf16[38,3,256]{2,1,0:T(4,128)(2,1)} %copy-done.5, bf16[38,3,256]{2,1,0:T(4,128)(2,1)} %copy-done.7, f32[50,256]{1,0:T(8,128)} %copy.18.taps_ref, ...), custom_call_target="tpu_custom_call" | custom-call | tf_op jit(solution)/shard_map/block/pallas_call | solution.py:263
  122.0 0.9 fusion.1
  122.9 2.1 collective-permute-start.5
  125.0 1.0 fusion
  126.0 3.4 %collective-permute-start.4 = (bf16[3,48,256]{2,1,0:T(8,128)(2,1)S(1)}, bf16[3,48,256]{2,1,0:T(8,128)(2,1)S(1)}, u32[]{:S(2)}, u32[]{:S(2)}) collective-permute-start(bf16[3,48,256]{2,1,0:T(8,128)(2,1)S(1)} %get-tuple-element.8), channel_id=1, source_target_pairs={{0,128},{128,256},{256,384},{1,129},{129,257},{257,385},{2,130},{1... | collective-permute-start | bytes 221192 | tf_op jit(solution)/shard_map/ppermute | solution.py:292
  129.4 0.0 collective-permute-done.5.bottom_ref
  129.4 0.0 copy-start.2
  129.4 1.7 collective-permute-done.4.top_ref
  131.1 0.1 pad_maximum_fusion.2
  131.2 0.5 copy-done.4
  131.7 1.1 collective-permute-start.6
  132.9 0.1 pad_maximum_fusion.3
  132.9 1.0 collective-permute-start.7
  133.9 0.7 copy.19.taps_ref
  134.6 0.0 collective-permute-done.6.left_ref
  134.6 2.1 collective-permute-done.7.right_ref
  136.8 0.0 copy-done.6
  136.8 0.6 copy-done.8
  137.4 13.8 %block.3 = bf16[32,48,256]{2,1,0:T(8,128)(2,1)} custom-call(bf16[32,48,256]{2,1,0:T(8,128)(2,1)} %block.2.x_ref, bf16[3,48,256]{2,1,0:T(8,128)(2,1)} %copy-done.4, bf16[3,48,256]{2,1,0:T(8,128)(2,1)} %copy-done.2, bf16[38,3,256]{2,1,0:T(4,128)(2,1)} %copy-done.6, bf16[38,3,256]{2,1,0:T(4,128)(2,1)} %copy-done.8, f32[50,256]{1,0:T(8,128)} %copy.19.taps_ref, ...), custom_call_target="tpu_custom_call" | custom-call | tf_op jit(solution)/shard_map/block/pallas_call | solution.py:263
  151.2 2.3 %to_channels.1 = bf16[3072,128]{1,0:T(8,128)(2,1)} custom-call(bf16[1536,256]{1,0:T(8,128)(2,1)} %bitcast.23), custom_call_target="tpu_custom_call" | custom-call | tf_op jit(solution)/shard_map/to_channels/pallas_call | solution.py:250
  153.5 55.1 %all_to_all.16 = bf16[128,24,128]{2,1,0:T(8,128)(2,1)} all-to-all(bf16[128,24,128]{2,1,0:T(8,128)(2,1)} %bitcast.21), channel_id=1, replica_groups=mesh['y'=4,'zh'=2,'zl'=8,'xc'=8] {'zh','zl','xc'}, dimensions={0} | all-to-all | bytes 1572864 | tf_op jit(solution)/shard_map/all_to_all | solution.py:344
  208.7 5.6 %paste.1 = bf16[4,16,16,360]{3,2,1,0:T(8,128)(2,1)} custom-call(bf16[3072,128]{1,0:T(8,128)(2,1)} %bitcast.22), custom_call_target="tpu_custom_call" | custom-call | tf_op jit(solution)/shard_map/paste/pallas_call | solution.py:228
  (18 shorter events, 0.1 us)
Async XLA Ops:
  0.0 0.7 copy-start.12
  2.5 29.5 %all-to-all-start.1 = ((f32[64,1,400]{2,1,0:T(1,128)}), f32[64,1,400]{2,1,0:T(1,128)S(1)}, u32[]{:S(2)}, u32[]{:S(2)}) async-start(f32[64,1,400]{2,1,0:T(1,128)} %broadcast_in_dim.12), calls=%async_computation.1 | async-start | bytes 262144 | tf_op jit(solution)/shard_map/all_to_all | solution.py:327
  32.0 55.6 %all-to-all-start = ((bf16[128,24,128]{2,1,0:T(8,128)(2,1)}), bf16[128,24,128]{2,1,0:T(8,128)(2,1)S(1)}, u32[]{:S(2)}, u32[]{:S(2)}) async-start(bf16[128,24,128]{2,1,0:T(8,128)(2,1)} %bitcast.19), calls=%async_computation | async-start | bytes 1572864 | tf_op jit(solution)/shard_map/all_to_all | solution.py:334
  43.0 4.3 %copy-start.10 = (f32[2,256]{1,0:T(2,128)S(1)}, f32[2,256]{1,0:T(2,128)}, u32[]{:S(2)}) copy-start(f32[2,256]{1,0:T(2,128)} %param.19) | copy-start | bytes 6148
  43.0 4.3 %copy-start.11 = (f32[2,256]{1,0:T(2,128)S(1)}, f32[2,256]{1,0:T(2,128)}, u32[]{:S(2)}) copy-start(f32[2,256]{1,0:T(2,128)} %param.18) | copy-start | bytes 6148
  43.0 0.7 copy-start.13
  45.9 1.9 copy-start.9
  87.5 0.9 copy-start
  91.7 6.3 %collective-permute-start = (bf16[3,48,256]{2,1,0:T(8,128)(2,1)S(1)}, bf16[3,48,256]{2,1,0:T(8,128)(2,1)S(1)}, u32[]{:S(2)}, u32[]{:S(2)}) collective-permute-start(bf16[3,48,256]{2,1,0:T(8,128)(2,1)S(1)} %bitcast.28), channel_id=1, source_target_pairs={{0,128},{128,256},{256,384},{1,129},{129,257},{257,385},{2,130},{1... | collective-permute-start | bytes 221192 | tf_op jit(solution)/shard_map/ppermute | solution.py:292
  95.9 5.5 %collective-permute-start.1 = (bf16[3,48,256]{2,1,0:T(8,128)(2,1)S(1)}, bf16[3,48,256]{2,1,0:T(8,128)(2,1)S(1)}, u32[]{:S(2)}, u32[]{:S(2)}) collective-permute-start(bf16[3,48,256]{2,1,0:T(8,128)(2,1)S(1)} %bitcast.27), channel_id=1, source_target_pairs={{128,0},{256,128},{384,256},{129,1},{257,129},{385,257},{130,2},{2... | collective-permute-start | bytes 221192 | tf_op jit(solution)/shard_map/ppermute | solution.py:293
  98.0 3.5 %copy-start.1 = (bf16[3,48,256]{2,1,0:T(8,128)(2,1)}, bf16[3,48,256]{2,1,0:T(8,128)(2,1)S(1)}, u32[]{:S(2)}) copy-start(bf16[3,48,256]{2,1,0:T(8,128)(2,1)S(1)} %collective-permute-done.top_ref) | copy-start | bytes 221188
  101.4 0.6 copy-start.3
  102.0 2.7 %collective-permute-start.2 = (bf16[38,3,256]{2,1,0:T(4,128)(2,1)S(1)}, bf16[38,3,256]{2,1,0:T(4,128)(2,1)S(1)}, u32[]{:S(2)}, u32[]{:S(2)}) collective-permute-start(bf16[38,3,256]{2,1,0:T(4,128)(2,1)S(1)} %pad_maximum_fusion), channel_id=1, source_target_pairs={{0,1},{1,2},{2,3},{3,4},{4,5},{5,6},{6,7},{7,0},{8,9},{9,10},{10,1... | collective-permute-start | bytes 175112 | tf_op jit(solution)/shard_map/ppermute | solution.py:302
  103.4 4.1 %collective-permute-start.3 = (bf16[38,3,256]{2,1,0:T(4,128)(2,1)S(1)}, bf16[38,3,256]{2,1,0:T(4,128)(2,1)S(1)}, u32[]{:S(2)}, u32[]{:S(2)}) collective-permute-start(bf16[38,3,256]{2,1,0:T(4,128)(2,1)S(1)} %pad_maximum_fusion.1), channel_id=1, source_target_pairs={{1,0},{2,1},{3,2},{4,3},{5,4},{6,5},{7,6},{0,7},{9,8},{10,9},{11,1... | collective-permute-start | bytes 175112 | tf_op jit(solution)/shard_map/ppermute | solution.py:303
  104.8 2.7 %copy-start.5 = (bf16[38,3,256]{2,1,0:T(4,128)(2,1)}, bf16[38,3,256]{2,1,0:T(4,128)(2,1)S(1)}, u32[]{:S(2)}) copy-start(bf16[38,3,256]{2,1,0:T(4,128)(2,1)S(1)} %collective-permute-done.2.left_ref) | copy-start | bytes 175108
  107.5 0.6 copy-start.7
  122.9 6.5 %collective-permute-start.5 = (bf16[3,48,256]{2,1,0:T(8,128)(2,1)S(1)}, bf16[3,48,256]{2,1,0:T(8,128)(2,1)S(1)}, u32[]{:S(2)}, u32[]{:S(2)}) collective-permute-start(bf16[3,48,256]{2,1,0:T(8,128)(2,1)S(1)} %get-tuple-element.7), channel_id=1, source_target_pairs={{128,0},{256,128},{384,256},{129,1},{257,129},{385,257},{130,2},{2... | collective-permute-start | bytes 221192 | tf_op jit(solution)/shard_map/ppermute | solution.py:293
  126.0 5.1 %collective-permute-start.4 = (bf16[3,48,256]{2,1,0:T(8,128)(2,1)S(1)}, bf16[3,48,256]{2,1,0:T(8,128)(2,1)S(1)}, u32[]{:S(2)}, u32[]{:S(2)}) collective-permute-start(bf16[3,48,256]{2,1,0:T(8,128)(2,1)S(1)} %get-tuple-element.8), channel_id=1, source_target_pairs={{0,128},{128,256},{256,384},{1,129},{129,257},{257,385},{2,130},{1... | collective-permute-start | bytes 221192 | tf_op jit(solution)/shard_map/ppermute | solution.py:292
  129.4 1.8 copy-start.2
  131.1 0.6 copy-start.4
  131.7 2.9 %collective-permute-start.6 = (bf16[38,3,256]{2,1,0:T(4,128)(2,1)S(1)}, bf16[38,3,256]{2,1,0:T(4,128)(2,1)S(1)}, u32[]{:S(2)}, u32[]{:S(2)}) collective-permute-start(bf16[38,3,256]{2,1,0:T(4,128)(2,1)S(1)} %pad_maximum_fusion.2), channel_id=1, source_target_pairs={{0,1},{1,2},{2,3},{3,4},{4,5},{5,6},{6,7},{7,0},{8,9},{9,10},{10,1... | collective-permute-start | bytes 175112 | tf_op jit(solution)/shard_map/ppermute | solution.py:302
  132.9 3.8 %collective-permute-start.7 = (bf16[38,3,256]{2,1,0:T(4,128)(2,1)S(1)}, bf16[38,3,256]{2,1,0:T(4,128)(2,1)S(1)}, u32[]{:S(2)}, u32[]{:S(2)}) collective-permute-start(bf16[38,3,256]{2,1,0:T(4,128)(2,1)S(1)} %pad_maximum_fusion.3), channel_id=1, source_target_pairs={{1,0},{2,1},{3,2},{4,3},{5,4},{6,5},{7,6},{0,7},{9,8},{10,9},{11,1... | collective-permute-start | bytes 175112 | tf_op jit(solution)/shard_map/ppermute | solution.py:303
  134.6 2.1 %copy-start.6 = (bf16[38,3,256]{2,1,0:T(4,128)(2,1)}, bf16[38,3,256]{2,1,0:T(4,128)(2,1)S(1)}, u32[]{:S(2)}) copy-start(bf16[38,3,256]{2,1,0:T(4,128)(2,1)S(1)} %collective-permute-done.6.left_ref) | copy-start | bytes 175108
  136.8 0.6 copy-start.8
where the time goes:
time: 215 us; the launch traced here: 214 us
  waiting for transfers between devices  57.6 us (27%)
  blocking collectives  55.1 us (26%)
  Pallas kernels  42.8 us (20%)
  starting transfers between devices  41.1 us (19%)
  local copies, waits for them, and re-layouts  15 us (7%)
    all_to_all x1, blocking collectives, on_device(): lax.all_to_all(pieces.reshape(shape), around, 0, 0, tiled=True)  55.1 us
    all_to_all x1, waiting for transfers between devices, on_device(): lax.all_to_all(pieces.reshape(shape), around, 0, 0, tiled=True)  38.5 us
    pallas_call x2, Pallas kernels, run_block(): pl.pallas_call(block_kernel, grid=(1,), out_shape=jax.ShapeDtypeStruct(x....  27.6 us
    all_to_all x1, starting transfers between devices, on_device(): filters = lax.all_to_all(filters, ('zl', 'xc'), 0, 0, tiled=True)  16 us
    all_to_all x1, starting transfers between devices, on_device(): lax.all_to_all(pieces.reshape(shape), around, 0, 0, tiled=True)  11 us
    all_to_all x1, waiting for transfers between devices, on_device(): filters = lax.all_to_all(filters, ('zl', 'xc'), 0, 0, tiled=True)  8.54 us
    ppermute x2, starting transfers between devices, halo_of(): top = lax.ppermute(x[-REACH:], 'y', down)  6.59 us
    pallas_call x1, Pallas kernels, run_paste(): pl.pallas_call(lambda *refs: paste_kernel(*refs, seg=seg, slot=slot), out...  5.57 us
  transfers between devices with their start and end apart: 10, of which 7 were waited for; matrix products, arithmetic and copies ran while one was open for 3% of the time, Pallas kernels for 2%

commit v1 on v0

--- a/solution.py
+++ b/solution.py
@@ -10,6 +10,7 @@
 TAPS = 7
 REACH = 3
 LEFT = 8
+ROWS = 8
 
 
 def lane_iota(rows):
@@ -116,67 +117,49 @@
             out_ref[start : start + LANES, :] = block.T.astype(jnp.bfloat16)
 
 
-def to_channels_kernel(in_ref, out_ref, rows32, *, tiles):
-    channels = in_ref.shape[1]
-    halves = out_ref.shape[0] // (channels * tiles)
-    for half in range(halves):
-        for t in range(tiles):
-            start = (half * tiles + t) * LANES
-            block = in_ref[start : start + LANES, :].astype(jnp.float32)
-            rows32[pl.ds(half * channels * tiles + t, channels, stride=tiles), :] = block.T
-    out_ref[...] = rows32[...].astype(jnp.bfloat16)
-
-
-def block_kernel(
-    x_ref, top_ref, bottom_ref, left_ref, right_ref, taps_ref, mod_ref,
-    up_ref, up_bias_ref, down_ref, down_bias_ref, scale_ref,
-    out_ref, padded, spread, mixed,
-):
-    lats, slot, channels = x_ref.shape
-    groups = channels // LANES
-    col_tiles = slot // 8
-    row_block = 8
-    for g in range(groups):
-        ch = slice(g * LANES, (g + 1) * LANES)
-        padded[g, 0:REACH, LEFT : LEFT + slot, :] = top_ref[:, :, ch].astype(jnp.float32)
-        padded[g, REACH : REACH + lats, LEFT : LEFT + slot, :] = x_ref[:, :, ch].astype(jnp.float32)
-        padded[g, REACH + lats :, LEFT : LEFT + slot, :] = bottom_ref[:, :, ch].astype(jnp.float32)
-        padded[g, :, LEFT + slot :, :] = jnp.zeros(
-            (lats + 2 * REACH, padded.shape[2] - LEFT - slot, LANES), jnp.float32
-        )
-        padded[g, :, LEFT - REACH : LEFT, :] = left_ref[:, :, ch].astype(jnp.float32)
-        right_at = LEFT + slot - REACH
-        padded[g, :, right_at : right_at + REACH, :] = right_ref[:, :, ch].astype(jnp.float32)
-        for k in range(TAPS * TAPS + 1):
-            spread[g, k] = jnp.broadcast_to(taps_ref[k : k + 1, ch], (8, LANES))
-
-    def conv_step(step, carry):
-        g = step // (lats // row_block)
-        row = (step % (lats // row_block)) * row_block
+def taps_over(load, spread, layer, group, cols, sums):
+    rows = len(sums)
+    for j in range(TAPS):
+        weights = [spread[layer, group, i * TAPS + j] for i in range(TAPS)]
+        for r in range(rows + TAPS - 1):
+            value = load(r, cols + j)
+            for i in range(TAPS):
+                if 0 <= r - i < rows:
+                    sums[r - i] = sums[r - i] + weights[i] * value
+    return sums
+
+
+def depthwise(source, spread, mixed, layer, lats, col_tiles, first_col):
+    groups = source.shape[0]
+    steps = -(-lats // ROWS)
+
+    def step_of(step, carry):
+        g = step // steps
+        row = jnp.minimum((step % steps) * ROWS, lats - ROWS)
         for k in range(col_tiles):
-            sums = [spread[g, TAPS * TAPS]] * row_block
-            for j in range(TAPS):
-                col = LEFT - REACH + j + 8 * k
-                weights = [spread[g, i * TAPS + j] for i in range(TAPS)]
-                for r in range(row_block + TAPS - 1):
-                    value = padded[g, row + r, col : col + 8, :]
-                    for i in range(TAPS):
-                        if 0 <= r - i < row_block:
-                            sums[r - i] = sums[r - i] + weights[i] * value
-            for r in range(row_block):
+            sums = [spread[layer, g, TAPS * TAPS]] * ROWS
+            sums = taps_over(
+                lambda r, col: source[g, row + r, col : col + 8, :],
+                spread, layer, g, first_col + 8 * k, sums,
+            )
+            for r in range(ROWS):
                 mixed[g, row + r, 8 * k : 8 * k + 8, :] = sums[r]
         return carry
 
-    lax.fori_loop(0, groups * (lats // row_block), conv_step, 0)
-    mlp_rows = 8
-    cells = mlp_rows * slot
+    lax.fori_loop(0, groups * steps, step_of, 0)
+
+
+def pointwise(mixed, layer, lats, slot, residual, store, weights):
+    mod_ref, up_ref, up_bias_ref, down_ref, down_bias_ref, scale_ref = weights
+    groups = mixed.shape[0]
+    channels = groups * LANES
+    cells = ROWS * slot
+    steps = -(-lats // ROWS)
     average_matrix = jnp.full((channels, channels), 1.0 / channels, jnp.bfloat16)
 
-    def mlp_step(step, carry):
-        row = step * mlp_rows
-        parts = [
-            mixed[g, pl.ds(row, mlp_rows), :, :].reshape(cells, LANES) for g in range(groups)
-        ]
+    def step_of(step, carry):
+        row = jnp.minimum(step * ROWS, lats - ROWS)
+        parts = [mixed[g, pl.ds(row, ROWS), 0:slot, :].reshape(cells, LANES) for g in range(groups)]
         rounded = jnp.concatenate(parts, axis=1).astype(jnp.bfloat16)
         average = jnp.dot(rounded, average_matrix, preferred_element_type=jnp.float32)
         centered = rounded.astype(jnp.float32) - average
@@ -185,27 +168,95 @@
             average_matrix,
             preferred_element_type=jnp.float32,
         )
-        normed = centered * lax.rsqrt(variance + EPS) * (1.0 + mod_ref[0:1, :]) + mod_ref[1:2, :]
+        gain = 1.0 + mod_ref[2 * layer : 2 * layer + 1, :]
+        shift = mod_ref[2 * layer + 1 : 2 * layer + 2, :]
+        normed = (centered * lax.rsqrt(variance + EPS) * gain + shift).astype(jnp.bfloat16)
         hidden = (
-            jnp.dot(normed.astype(jnp.bfloat16), up_ref[0], preferred_element_type=jnp.float32)
-            + up_bias_ref[...]
+            jnp.dot(normed, up_ref[layer], preferred_element_type=jnp.float32)
+            + up_bias_ref[layer : layer + 1, :]
         )
         active = (0.5 * hidden * (1.0 + lax.erf(hidden * 0.7071067811865476))).astype(jnp.bfloat16)
         result = (
-            jnp.dot(active, down_ref[0], preferred_element_type=jnp.float32) + down_bias_ref[...]
-        )
-        branch = (scale_ref[...] * result).astype(jnp.bfloat16).astype(jnp.float32)
-        current = x_ref[pl.ds(row, mlp_rows), :, :].astype(jnp.float32)
-        out_ref[pl.ds(row, mlp_rows), :, :] = (
-            current + branch.reshape(mlp_rows, slot, channels)
-        ).astype(jnp.bfloat16)
+            jnp.dot(active, down_ref[layer], preferred_element_type=jnp.float32)
+            + down_bias_ref[layer : layer + 1, :]
+        )
+        branch = (scale_ref[layer : layer + 1, :] * result).astype(jnp.bfloat16).astype(jnp.float32)
+        for g in range(groups):
+            part = branch[:, g * LANES : (g + 1) * LANES].reshape(ROWS, slot, LANES)
+            store(g, row, (residual(g, row) + part).astype(jnp.bfloat16).astype(jnp.float32))
         return carry
 
-    lax.fori_loop(0, lats // mlp_rows, mlp_step, 0)
-
-
-def whole(shape):
-    return pl.BlockSpec(shape, lambda *_: (0,) * len(shape))
+    lax.fori_loop(0, steps, step_of, 0)
+
+
+def blocks_kernel(
+    edge_ref, x_ref, top_ref, bottom_ref, left_ref, right_ref, taps_ref, mod_ref,
+    up_ref, up_bias_ref, down_ref, down_bias_ref, scale_ref,
+    out_ref, first, second, spread, mixed, final, rows32, *, tiles,
+):
+    lats, slot, channels = x_ref.shape
+    groups = channels // LANES
+    reach = 2 * REACH
+    wide = lats + reach
+    right_at = LEFT + slot - REACH
+    for g in range(groups):
+        ch = slice(g * LANES, (g + 1) * LANES)
+        first[g, 0:reach, LEFT : LEFT + slot, :] = top_ref[:, :, ch].astype(jnp.float32)
+        first[g, reach : reach + lats, LEFT : LEFT + slot, :] = x_ref[:, :, ch].astype(jnp.float32)
+        first[g, reach + lats :, LEFT : LEFT + slot, :] = bottom_ref[:, :, ch].astype(jnp.float32)
+        first[g, :, LEFT + slot :, :] = jnp.zeros(
+            (lats + 2 * reach, first.shape[2] - LEFT - slot, LANES), jnp.float32
+        )
+        first[g, :, LEFT - reach : LEFT, :] = left_ref[:, :, ch].astype(jnp.float32)
+        first[g, :, right_at : right_at + reach, :] = right_ref[:, :, ch].astype(jnp.float32)
+        for layer in range(taps_ref.shape[0]):
+            for k in range(TAPS * TAPS + 1):
+                spread[layer, g, k] = jnp.broadcast_to(taps_ref[layer, k : k + 1, ch], (8, LANES))
+    weights = (mod_ref, up_ref, up_bias_ref, down_ref, down_bias_ref, scale_ref)
+
+    wide_slot = slot + 8
+    depthwise(first, spread, mixed, 0, wide, wide_slot // 8, LEFT - reach)
+
+    def first_store(g, row, value):
+        second[g, pl.ds(row, ROWS), :, :] = value
+
+    pointwise(
+        mixed, 0, wide, wide_slot,
+        lambda g, row: first[g, pl.ds(row + REACH, ROWS), LEFT - REACH : LEFT - REACH + wide_slot, :],
+        first_store, weights,
+    )
+
+    @pl.when(edge_ref[0] == 1)
+    def _():
+        second[:, 0:REACH, :, :] = jnp.zeros((groups, REACH, wide_slot, LANES), jnp.float32)
+
+    @pl.when(edge_ref[1] == 1)
+    def _():
+        second[:, REACH + lats :, :, :] = jnp.zeros((groups, REACH, wide_slot, LANES), jnp.float32)
+
+    depthwise(second, spread, mixed, 1, lats, slot // 8, 0)
+
+    def final_store(g, row, value):
+        final[g, pl.ds(row, ROWS), :, :] = value
+
+    pointwise(
+        mixed, 1, lats, slot,
+        lambda g, row: second[g, pl.ds(row + REACH, ROWS), REACH : REACH + slot, :],
+        final_store, weights,
+    )
+    flat = lats * slot // tiles // LANES
+    rows_per = LANES * 3 // slot
+    for half in range(flat):
+        for g in range(groups):
+            for part in range(tiles // 3):
+                lat = (half * tiles + part * 3) * LANES // slot
+                block = final[g, lat : lat + rows_per, :, :].reshape(rows_per * slot, LANES)
+                for t in range(3):
+                    start = half * channels * tiles + g * LANES * tiles + part * 3 + t
+                    rows32[pl.ds(start, LANES, stride=tiles), :] = block[
+                        t * LANES : (t + 1) * LANES
+                    ].T
+    out_ref[...] = rows32[...].astype(jnp.bfloat16)
 
 
 def run_cut(field, seg, slot):
@@ -245,61 +296,45 @@
     )(pieces)
 
 
-def run_to_channels(x, tiles):
-    rows = x.shape[0] * x.shape[1] // LANES
-    return pl.pallas_call(
-        lambda *refs: to_channels_kernel(*refs, tiles=tiles),
-        out_shape=jax.ShapeDtypeStruct((rows, LANES), jnp.bfloat16),
-        scratch_shapes=[pltpu.VMEM((rows, LANES), jnp.float32)],
-        name="to_channels",
-    )(x)
-
-
-def run_block(x, halos, taps, mod, layer, up, up_bias, down, down_bias, scale):
+def run_blocks(edges, x, halos, taps, mods, up, up_bias, down, down_bias, scale, tiles):
     lats, slot, channels = x.shape
     groups = channels // LANES
-    hidden = up.shape[2]
-    arrays = (x, *halos, taps, mod)
+    rows = lats * slot * channels // LANES
+    vmem = pl.BlockSpec(memory_space=pltpu.VMEM)
+    arrays = (x, *halos, taps, mods, up, up_bias, down, down_bias, scale)
+    wide_slot = slot + 8
     return pl.pallas_call(
-        block_kernel,
-        grid=(1,),
-        out_shape=jax.ShapeDtypeStruct(x.shape, jnp.bfloat16),
-        in_specs=[whole(a.shape) for a in arrays]
-        + [
-            pl.BlockSpec((1, channels, hidden), lambda _: (layer, 0, 0)),
-            whole((1, hidden)),
-            pl.BlockSpec((1, hidden, channels), lambda _: (layer, 0, 0)),
-            whole((1, channels)),
-            whole((1, channels)),
+        lambda *refs: blocks_kernel(*refs, tiles=tiles),
+        out_shape=jax.ShapeDtypeStruct((rows, LANES), jnp.bfloat16),
+        in_specs=[pl.BlockSpec(memory_space=pltpu.SMEM)] + [vmem] * len(arrays),
+        scratch_shapes=[
+            pltpu.VMEM((groups, lats + 4 * REACH, LEFT + wide_slot, LANES), jnp.float32),
+            pltpu.VMEM((groups, lats + 2 * REACH, wide_slot, LANES), jnp.float32),
+            pltpu.VMEM((taps.shape[0], groups, TAPS * TAPS + 1, 8, LANES), jnp.float32),
+            pltpu.VMEM((groups, lats + 2 * REACH, wide_slot, LANES), jnp.float32),
+            pltpu.VMEM((groups, lats, slot, LANES), jnp.float32),
+            pltpu.VMEM((rows, LANES), jnp.float32),
         ],
-        out_specs=whole(x.shape),
-        scratch_shapes=[
-            pltpu.VMEM((groups, lats + 2 * REACH, LEFT + slot + 8, LANES), jnp.float32),
-            pltpu.VMEM((groups, TAPS * TAPS + 1, 8, LANES), jnp.float32),
-            pltpu.VMEM((groups, lats, slot, LANES), jnp.float32),
-        ],
-        name="block",
-    )(
-        *arrays,
-        up, up_bias[layer][None], down, down_bias[layer][None], scale[layer][None],
-    )
+        name="blocks",
+    )(edges, *arrays)
 
 
 def halo_of(x, seg):
     rows, segs = lax.axis_size("y"), lax.axis_size("xc")
+    reach = 2 * REACH
     down = [(i, i + 1) for i in range(rows - 1)]
     up = [(j, i) for i, j in down]
-    top = lax.ppermute(x[-REACH:], "y", down)
-    bottom = lax.ppermute(x[:REACH], "y", up)
+    top = lax.ppermute(x[-reach:], "y", down)
+    bottom = lax.ppermute(x[:reach], "y", up)
     east = [(i, (i + 1) % segs) for i in range(segs)]
     west = [(j, i) for i, j in east]
 
     def columns(lo):
         return jnp.concatenate(
-            [part[:, lo : lo + REACH] for part in (top, x, bottom)], axis=0
-        )
-
-    left = lax.ppermute(columns(seg - REACH), "xc", east)
+            [part[:, lo : lo + reach] for part in (top, x, bottom)], axis=0
+        )
+
+    left = lax.ppermute(columns(seg - reach), "xc", east)
     right = lax.ppermute(columns(0), "xc", west)
     return top, bottom, left, right
 
@@ -318,29 +353,30 @@
     slot = -(-seg // 8) * 8
     tiles = lats * slot // LANES
     member = lax.axis_index("zh") * lax.axis_size("zl") + lax.axis_index("zl")
-    mods = modulation[:, noise_level[member]]
-
+    mods = modulation[:, noise_level[member]].reshape(2 * layers, channels)
+    band = lax.axis_index("y")
+    edges = jnp.stack([band == 0, band == lax.axis_size("y") - 1]).astype(jnp.int32)
+
+    pieces = run_cut(field, seg, slot)
     filters = jnp.concatenate(
         [conv_kernel.reshape(layers, chans, TAPS * TAPS), conv_bias[:, :, None]], axis=2
     )
+    pieces, filters = lax.optimization_barrier((pieces, filters))
+    shape = (peers, chans * tiles, LANES)
+    around = ("zh", "zl", "xc")
+    pieces = lax.all_to_all(pieces.reshape(shape), around, 0, 0, tiled=True).reshape(-1, LANES)
+
     filters = jnp.broadcast_to(filters.reshape(1, -1), (channels // chans, filters.size))
     filters = lax.all_to_all(filters, ("zl", "xc"), 0, 0, tiled=True)
     filters = filters.reshape(channels // chans, layers, chans, TAPS * TAPS + 1)
     filters = filters.transpose(1, 3, 0, 2).reshape(layers, TAPS * TAPS + 1, channels)
 
-    pieces = run_cut(field, seg, slot)
-    shape = (peers, chans * tiles, LANES)
-    around = ("zh", "zl", "xc")
-    pieces = lax.all_to_all(pieces.reshape(shape), around, 0, 0, tiled=True).reshape(-1, LANES)
     x = run_to_cells(pieces, halves * lats * slot, channels, tiles)
     x = x.reshape(halves * lats, slot, channels)
-    for layer in range(layers):
-        halos = halo_of(x, seg)
-        x = run_block(
-            x, halos, filters[layer], mods[layer], layer,
-            expand_weight, expand_bias, project_weight, project_bias, layer_scale,
-        )
-    pieces = run_to_channels(x.reshape(-1, channels), tiles)
+    pieces = run_blocks(
+        edges, x, halo_of(x, seg), filters, mods,
+        expand_weight, expand_bias, project_weight, project_bias, layer_scale, tiles,
+    )
     pieces = lax.all_to_all(pieces.reshape(shape), around, 0, 0, tiled=True).reshape(-1, LANES)
     return run_paste(pieces, field.shape, seg, slot)
 

time: 215 us -> 194 us (0.902)
  waiting for transfers between devices: 57.6 us -> 47.3 us
  starting transfers between devices: 41.1 us -> 32.7 us
  local copies, waits for them, and re-layouts: 15 us -> 8.83 us
  blocking collectives: 55.1 us -> 58.6 us
    all_to_all x1, starting transfers between devices: 16 us -> 5.48 us  [on_device(): filters = lax.all_to_all(filters, ('zl', 'xc'), 0, 0, tiled=True)]
    all_to_all x1, waiting for transfers between devices: 8.54 us -> 0.01 us  [on_device(): filters = lax.all_to_all(filters, ('zl', 'xc'), 0, 0, tiled=True)]
    all_to_all x1, starting transfers between devices: 11 us -> 19.3 us  [on_device(): lax.all_to_all(pieces.reshape(shape), around, 0, 0, tiled=True)]
    ppermute x6 -> x3, starting transfers between devices: 13.2 us -> 7.86 us  [the longest x1 3.2 us: halo_of(): top = lax.ppermute(x[-reach:], 'y', down)]
    all_to_all x1, blocking collectives: 55.1 us -> 58.6 us  [on_device(): lax.all_to_all(pieces.reshape(shape), around, 0, 0, tiled=True)]
    slice x11 -> x4, local copies, waits for them, and re-layouts: 5.2 us -> 2.09 us  [the longest x3 1.09 us: columns(): part[:, lo:lo + reach]]
    all_to_all x1, waiting for transfers between devices: 38.5 us -> 41.6 us  [on_device(): lax.all_to_all(pieces.reshape(shape), around, 0, 0, tiled=True)]
    squeeze x3 -> x0, local copies, waits for them, and re-layouts: 2.71 us -> none  [the longest x2 1.41 us: on_device(): filters[layer]]
  transfers between devices with their start and end apart: 10 -> 6, of which waited for: 7 -> 4; matrix products, arithmetic and copies ran while one was open for 3% -> 3% of each run, Pallas kernels for 2% -> 1%
where the time goes in v1:
time: 194 us; the launch traced here: 193 us
  blocking collectives  58.6 us (30%)
  waiting for transfers between devices  47.3 us (24%)
  Pallas kernels  42.9 us (22%)
  starting transfers between devices  32.7 us (17%)
  local copies, waits for them, and re-layouts  8.83 us (5%)
    all_to_all x1, blocking collectives, on_device(): lax.all_to_all(pieces.reshape(shape), around, 0, 0, tiled=True)  58.6 us
    all_to_all x1, waiting for transfers between devices, on_device(): lax.all_to_all(pieces.reshape(shape), around, 0, 0, tiled=True)  41.6 us
    pallas_call x1, Pallas kernels, run_blocks(): pl.pallas_call(lambda *refs: blocks_kernel(*refs, tiles=tiles), out_shape...  30 us
    all_to_all x1, starting transfers between devices, on_device(): lax.all_to_all(pieces.reshape(shape), around, 0, 0, tiled=True)  19.3 us
    pallas_call x1, Pallas kernels, run_paste(): pl.pallas_call(lambda *refs: paste_kernel(*refs, seg=seg, slot=slot), out...  5.57 us
    all_to_all x1, starting transfers between devices, on_device(): filters = lax.all_to_all(filters, ('zl', 'xc'), 0, 0, tiled=True)  5.48 us
    pallas_call x1, Pallas kernels, run_cut(): pl.pallas_call(lambda *refs: cut_kernel(*refs, seg=seg, slot=slot), out_s...  4.97 us
  transfers between devices with their start and end apart: 6, of which 4 were waited for; matrix products, arithmetic and copies ran while one was open for 3% of the time, Pallas kernels for 1%

profile of v1, /device:TPU:41, one launch (start us, length us, event | category | flops | bytes accessed | tf_op | source)
XLA Modules:
  0.0 193.2 jit_solution(1196724849448144625)
XLA Ops:
  0.0 0.0 copy-start
  0.0 0.0 copy-start.6
  0.0 0.7 copy-done.6
  0.7 0.1 copy.17
  0.8 0.8 copy.16
  1.6 0.1 reshape.36
  1.6 5.0 %cut.1 = bf16[3072,128]{1,0:T(8,128)(2,1)} custom-call(bf16[4,16,16,360]{3,2,1,0:T(8,128)(2,1)} %refs_0_.1), custom_call_target="tpu_custom_call" | custom-call | tf_op jit(solution)/shard_map/cut/pallas_call | solution.py:266
  6.6 0.1 pad_maximum_fusion.2
  6.7 19.3 %all-to-all-start = ((bf16[128,24,128]{2,1,0:T(8,128)(2,1)}), bf16[128,24,128]{2,1,0:T(8,128)(2,1)S(1)}, u32[]{:S(2)}, u32[]{:S(2)}) async-start(bf16[128,24,128]{2,1,0:T(8,128)(2,1)} %bitcast.17), calls=%async_computation | async-start | bytes 1572864 | tf_op jit(solution)/shard_map/all_to_all | solution.py:367
  26.0 0.0 copy-start.7
  26.0 0.6 copy-done.7
  26.7 0.6 dynamic_slice.6
  28.3 0.1 broadcast_in_dim.11
  29.0 41.6 %all-to-all-done = bf16[128,24,128]{2,1,0:T(8,128)(2,1)S(1)} async-done(((bf16[128,24,128]{2,1,0:T(8,128)(2,1)}), bf16[128,24,128]{2,1,0:T(8,128)(2,1)S(1)}, u32[]{:S(2)}, u32[]{:S(2)}) %all-to-all-start) | async-done | bytes 786464 | tf_op jit(solution)/shard_map/all_to_all | solution.py:367
  70.6 0.0 copy-start.1
  70.6 0.9 broadcast_in_dim.12
  71.5 5.5 %all-to-all-start.1 = ((f32[64,1,400]{2,1,0:T(1,128)}), f32[64,1,400]{2,1,0:T(1,128)S(1)}, u32[]{:S(2)}, u32[]{:S(2)}) async-start(f32[64,1,400]{2,1,0:T(1,128)} %broadcast_in_dim.12), calls=%async_computation.1 | async-start | bytes 262144 | tf_op jit(solution)/shard_map/all_to_all | solution.py:370
  76.9 0.0 copy-done.1
  77.0 2.3 %to_cells.1 = bf16[1536,256]{1,0:T(8,128)(2,1)} custom-call(bf16[3072,128]{1,0:T(8,128)(2,1)} %bitcast.16), custom_call_target="tpu_custom_call" | custom-call | tf_op jit(solution)/shard_map/to_cells/pallas_call | solution.py:291
  79.3 1.0 fusion.1
  80.3 3.2 %collective-permute-start = (bf16[6,48,256]{2,1,0:T(8,128)(2,1)S(1)}, bf16[6,48,256]{2,1,0:T(8,128)(2,1)S(1)}, u32[]{:S(2)}, u32[]{:S(2)}) collective-permute-start(bf16[6,48,256]{2,1,0:T(8,128)(2,1)S(1)} %bitcast.22), channel_id=1, source_target_pairs={{0,128},{128,256},{256,384},{1,129},{129,257},{257,385},{2,130},{1... | collective-permute-start | bytes 442376 | tf_op jit(solution)/shard_map/ppermute | solution.py:327
  83.5 2.1 %collective-permute-start.1 = (bf16[6,48,256]{2,1,0:T(8,128)(2,1)S(1)}, bf16[6,48,256]{2,1,0:T(8,128)(2,1)S(1)}, u32[]{:S(2)}, u32[]{:S(2)}) collective-permute-start(bf16[6,48,256]{2,1,0:T(8,128)(2,1)S(1)} %bitcast.21), channel_id=1, source_target_pairs={{128,0},{256,128},{384,256},{129,1},{257,129},{385,257},{130,2},{2... | collective-permute-start | bytes 442376 | tf_op jit(solution)/shard_map/ppermute | solution.py:328
  85.6 1.1 fusion
  86.7 0.6 collective-permute-done.refs_2_
  87.3 0.0 copy-start.2
  87.3 2.9 %collective-permute-done.1.refs_3_ = bf16[6,48,256]{2,1,0:T(8,128)(2,1)S(1)} collective-permute-done((bf16[6,48,256]{2,1,0:T(8,128)(2,1)S(1)}, bf16[6,48,256]{2,1,0:T(8,128)(2,1)S(1)}, u32[]{:S(2)}, u32[]{:S(2)}) %collective-permute-start.1) | collective-permute-done | bytes 147488 | tf_op jit(solution)/shard_map/ppermute | solution.py:328
  90.2 0.0 copy-start.3
  90.2 0.0 copy-done.2
  90.3 0.6 copy-done.3
  90.8 2.6 %collective-permute-start.2 = (bf16[44,6,256]{2,1,0:T(8,128)(2,1)S(1)}, bf16[44,6,256]{2,1,0:T(8,128)(2,1)S(1)}, u32[]{:S(2)}, u32[]{:S(2)}) collective-permute-start(bf16[44,6,256]{2,1,0:T(8,128)(2,1)S(1)} %pad_maximum_fusion), channel_id=1, source_target_pairs={{0,1},{1,2},{2,3},{3,4},{4,5},{5,6},{6,7},{7,0},{8,9},{9,10},{10,1... | collective-permute-start | bytes 405512 | tf_op jit(solution)/shard_map/ppermute | solution.py:337
  93.5 0.0 collective-permute-start.3
  93.5 0.0 copy-done
  93.5 0.6 reshape_squeeze.3.refs_7_
  94.1 0.7 add_convert_fusion.refs_0_
  94.8 0.0 all-to-all-done.1
  94.8 0.3 reduce
  95.1 0.3 reshape.40
  95.4 0.8 copy.19.refs_6_
  96.2 0.0 collective-permute-done.2.refs_4_
  96.2 0.0 copy-start.4
  96.2 2.2 %collective-permute-done.3.refs_5_ = bf16[44,6,256]{2,1,0:T(8,128)(2,1)S(1)} collective-permute-done((bf16[44,6,256]{2,1,0:T(8,128)(2,1)S(1)}, bf16[44,6,256]{2,1,0:T(8,128)(2,1)S(1)}, u32[]{:S(2)}, u32[]{:S(2)}) %collective-permute-start.3) | collective-permute-done | bytes 135200 | tf_op jit(solution)/shard_map/ppermute | solution.py:338
  98.4 0.0 copy-done.4
  98.4 0.0 copy-start.5
  98.4 0.7 copy-done.5
  99.1 30.0 %blocks.1 = bf16[3072,128]{1,0:T(8,128)(2,1)} custom-call(s32[2]{0:T(128)} %add_convert_fusion.refs_0_, bf16[32,48,256]{2,1,0:T(8,128)(2,1)} %bitcast.14, bf16[6,48,256]{2,1,0:T(8,128)(2,1)} %copy-done.2, bf16[6,48,256]{2,1,0:T(8,128)(2,1)} %copy-done.3, bf16[44,6,256]{2,1,0:T(8,128)(2,1)} %copy-done.4, bf16[44,6,256]{2,1,0:T(8,128)(2,1)} %copy-done.5, ...), custom_call_target="tpu_custom_call" | custom-call | tf_op jit(solution)/shard_map/blocks/pallas_call | solution.py:306
  129.0 58.6 %all_to_all.16 = bf16[128,24,128]{2,1,0:T(8,128)(2,1)} all-to-all(bf16[128,24,128]{2,1,0:T(8,128)(2,1)} %bitcast.15), channel_id=1, replica_groups=mesh['y'=4,'zh'=2,'zl'=8,'xc'=8] {'zh','zl','xc'}, dimensions={0} | all-to-all | bytes 1572864 | tf_op jit(solution)/shard_map/all_to_all | solution.py:380
  187.6 5.6 %paste.1 = bf16[4,16,16,360]{3,2,1,0:T(8,128)(2,1)} custom-call(bf16[3072,128]{1,0:T(8,128)(2,1)} %bitcast.18), custom_call_target="tpu_custom_call" | custom-call | tf_op jit(solution)/shard_map/paste/pallas_call | solution.py:279
  (6 shorter events, 0.2 us)
Async XLA Ops:
  0.0 93.5 %copy-start = (f32[2,20,2,256]{3,2,1,0:T(2,128)S(1)}, f32[2,20,2,256]{3,2,1,0:T(2,128)}, u32[]{:S(2)}) copy-start(f32[2,20,2,256]{3,2,1,0:T(2,128)} %param.14) | copy-start | bytes 245764
  0.0 0.7 copy-start.6
  6.7 63.9 %all-to-all-start = ((bf16[128,24,128]{2,1,0:T(8,128)(2,1)}), bf16[128,24,128]{2,1,0:T(8,128)(2,1)S(1)}, u32[]{:S(2)}, u32[]{:S(2)}) async-start(bf16[128,24,128]{2,1,0:T(8,128)(2,1)} %bitcast.17), calls=%async_computation | async-start | bytes 1572864 | tf_op jit(solution)/shard_map/all_to_all | solution.py:367
  26.0 0.7 copy-start.7
  70.6 6.3 %copy-start.1 = (bf16[128,24,128]{2,1,0:T(8,128)(2,1)}, bf16[128,24,128]{2,1,0:T(8,128)(2,1)S(1)}, u32[]{:S(2)}) copy-start(bf16[128,24,128]{2,1,0:T(8,128)(2,1)S(1)} %all-to-all-done) | copy-start | bytes 2359300
  71.5 23.3 %all-to-all-start.1 = ((f32[64,1,400]{2,1,0:T(1,128)}), f32[64,1,400]{2,1,0:T(1,128)S(1)}, u32[]{:S(2)}, u32[]{:S(2)}) async-start(f32[64,1,400]{2,1,0:T(1,128)} %broadcast_in_dim.12), calls=%async_computation.1 | async-start | bytes 262144 | tf_op jit(solution)/shard_map/all_to_all | solution.py:370
  80.3 7.0 %collective-permute-start = (bf16[6,48,256]{2,1,0:T(8,128)(2,1)S(1)}, bf16[6,48,256]{2,1,0:T(8,128)(2,1)S(1)}, u32[]{:S(2)}, u32[]{:S(2)}) collective-permute-start(bf16[6,48,256]{2,1,0:T(8,128)(2,1)S(1)} %bitcast.22), channel_id=1, source_target_pairs={{0,128},{128,256},{256,384},{1,129},{129,257},{257,385},{2,130},{1... | collective-permute-start | bytes 442376 | tf_op jit(solution)/shard_map/ppermute | solution.py:327
  83.5 6.6 %collective-permute-start.1 = (bf16[6,48,256]{2,1,0:T(8,128)(2,1)S(1)}, bf16[6,48,256]{2,1,0:T(8,128)(2,1)S(1)}, u32[]{:S(2)}, u32[]{:S(2)}) collective-permute-start(bf16[6,48,256]{2,1,0:T(8,128)(2,1)S(1)} %bitcast.21), channel_id=1, source_target_pairs={{128,0},{256,128},{384,256},{129,1},{257,129},{385,257},{130,2},{2... | collective-permute-start | bytes 442376 | tf_op jit(solution)/shard_map/ppermute | solution.py:328
  87.3 3.0 %copy-start.2 = (bf16[6,48,256]{2,1,0:T(8,128)(2,1)}, bf16[6,48,256]{2,1,0:T(8,128)(2,1)S(1)}, u32[]{:S(2)}) copy-start(bf16[6,48,256]{2,1,0:T(8,128)(2,1)S(1)} %collective-permute-done.refs_2_) | copy-start | bytes 442372
  90.2 0.7 copy-start.3
  90.8 5.4 %collective-permute-start.2 = (bf16[44,6,256]{2,1,0:T(8,128)(2,1)S(1)}, bf16[44,6,256]{2,1,0:T(8,128)(2,1)S(1)}, u32[]{:S(2)}, u32[]{:S(2)}) collective-permute-start(bf16[44,6,256]{2,1,0:T(8,128)(2,1)S(1)} %pad_maximum_fusion), channel_id=1, source_target_pairs={{0,1},{1,2},{2,3},{3,4},{4,5},{5,6},{6,7},{7,0},{8,9},{9,10},{10,1... | collective-permute-start | bytes 405512 | tf_op jit(solution)/shard_map/ppermute | solution.py:337
  93.5 4.9 %collective-permute-start.3 = (bf16[44,6,256]{2,1,0:T(8,128)(2,1)S(1)}, bf16[44,6,256]{2,1,0:T(8,128)(2,1)S(1)}, u32[]{:S(2)}, u32[]{:S(2)}) collective-permute-start(bf16[44,6,256]{2,1,0:T(8,128)(2,1)S(1)} %pad_maximum_fusion.1), channel_id=1, source_target_pairs={{1,0},{2,1},{3,2},{4,3},{5,4},{6,5},{7,6},{0,7},{9,8},{10,9},{11,1... | collective-permute-start | bytes 405512 | tf_op jit(solution)/shard_map/ppermute | solution.py:338
  96.2 2.2 %copy-start.4 = (bf16[44,6,256]{2,1,0:T(8,128)(2,1)}, bf16[44,6,256]{2,1,0:T(8,128)(2,1)S(1)}, u32[]{:S(2)}) copy-start(bf16[44,6,256]{2,1,0:T(8,128)(2,1)S(1)} %collective-permute-done.2.refs_4_) | copy-start | bytes 405508
  98.4 0.7 copy-start.5

commit v2 on v1

--- a/solution.py
+++ b/solution.py
@@ -17,25 +17,26 @@
     return lax.broadcasted_iota(jnp.int32, (rows, LANES), 1)
 
 
-def moved_lanes(load, spans, rows):
+def moved_lanes(load, spans, rows, rolled):
     lanes = lane_iota(rows)
-    tile = jnp.zeros((rows, LANES), jnp.float32)
+    tile = None
     for source, src, dst, width in spans:
         done = 0
         while done < width:
             part, lane = divmod(src + done, LANES)
             take = min(width - done, LANES - lane)
-            value = load(source, part)
             shift = (dst + done - lane) % LANES
-            if shift:
-                value = pltpu.roll(value, shift, 1)
-            lo, hi = dst + done, dst + done + take
-            tile = jnp.where((lanes >= lo) & (lanes < hi), value, tile)
+            key = (source, part, shift)
+            if key not in rolled:
+                value = load(source, part)
+                rolled[key] = pltpu.roll(value, shift, 1) if shift else value
+            value = rolled[key]
+            tile = value if tile is None else jnp.where(lanes >= dst + done, value, tile)
             done += take
     return tile
 
 
-def spans_of(total, count, stride, width, tile_index, start_of):
+def spans_of(count, stride, width, tile_index, start_of):
     spans = []
     for item in range(count):
         lo = max(item * stride, tile_index * LANES)
@@ -55,14 +56,17 @@
         lo, hi = a * LANES, min((a + 1) * LANES, lons)
         piece = field_ref[:, :, :, lo:hi].astype(jnp.float32).reshape(rows * lats, hi - lo)
         wide[a, :, 0 : hi - lo] = piece
+        if hi - lo < LANES:
+            wide[a, :, hi - lo :] = jnp.zeros((rows * lats, LANES - hi + lo), jnp.float32)
     for s in range(segs):
+        rolled = {}
         for t in range(tiles):
-            spans = spans_of(0, lats, slot, seg, t, lambda item: s * seg)
+            spans = spans_of(lats, slot, seg, t, lambda item: s * seg)
 
             def load(lat, part):
                 return wide[part, pl.ds(lat, rows, stride=lats), :]
 
-            tile = moved_lanes(load, spans, rows)
+            tile = moved_lanes(load, spans, rows, rolled)
             for c in range(chans):
                 start = s * chans * tiles + c * tiles + t
                 cut[pl.ds(start, members, stride=segs * chans * tiles), :] = tile[
@@ -79,8 +83,9 @@
     tiles = lats * slot // LANES
     cut[...] = in_ref[...].astype(jnp.float32)
     for lat in range(lats):
+        rolled = {}
         for a in range(parts):
-            spans = spans_of(0, segs, seg, seg, a, lambda item: lat * slot)
+            spans = spans_of(segs, seg, seg, a, lambda item: lat * slot)
 
             def load(s, part):
                 return jnp.concatenate(
@@ -98,7 +103,7 @@
                     axis=0,
                 )
 
-            wide[a, pl.ds(lat, rows, stride=lats), :] = moved_lanes(load, spans, rows)
+            wide[a, pl.ds(lat, rows, stride=lats), :] = moved_lanes(load, spans, rows, rolled)
     for a in range(parts):
         lo, hi = a * LANES, min((a + 1) * LANES, lons)
         out_ref[:, :, :, lo:hi] = (
@@ -106,8 +111,8 @@
         )
 
 
-def to_cells_kernel(in_ref, out_ref, rows32, *, tiles):
-    channels = out_ref.shape[1]
+def to_cells_kernel(in_ref, out_ref, north_ref, south_ref, rows32, *, tiles):
+    cells, channels = out_ref.shape
     halves = in_ref.shape[0] // (channels * tiles)
     rows32[...] = in_ref[...].astype(jnp.float32)
     for half in range(halves):
@@ -115,38 +120,33 @@
             block = rows32[pl.ds(half * channels * tiles + t, channels, stride=tiles), :]
             start = (half * tiles + t) * LANES
             out_ref[start : start + LANES, :] = block.T.astype(jnp.bfloat16)
-
-
-def taps_over(load, spread, layer, group, cols, sums):
-    rows = len(sums)
-    for j in range(TAPS):
-        weights = [spread[layer, group, i * TAPS + j] for i in range(TAPS)]
-        for r in range(rows + TAPS - 1):
-            value = load(r, cols + j)
-            for i in range(TAPS):
-                if 0 <= r - i < rows:
-                    sums[r - i] = sums[r - i] + weights[i] * value
-    return sums
-
-
-def depthwise(source, spread, mixed, layer, lats, col_tiles, first_col):
+    edge = north_ref.shape[0]
+    north_ref[...] = out_ref[0:edge, :]
+    south_ref[...] = out_ref[cells - edge :, :]
+
+
+def depthwise(source, spread, mixed, layer, lats, rows, col_tiles, first_col):
     groups = source.shape[0]
-    steps = -(-lats // ROWS)
-
-    def step_of(step, carry):
-        g = step // steps
-        row = jnp.minimum((step % steps) * ROWS, lats - ROWS)
-        for k in range(col_tiles):
-            sums = [spread[layer, g, TAPS * TAPS]] * ROWS
-            sums = taps_over(
-                lambda r, col: source[g, row + r, col : col + 8, :],
-                spread, layer, g, first_col + 8 * k, sums,
-            )
-            for r in range(ROWS):
+    steps = -(-lats // rows)
+    for k in range(col_tiles):
+
+        def step_of(step, carry):
+            g = step // steps
+            row = jnp.minimum((step % steps) * rows, lats - rows)
+            sums = [spread[layer, g, TAPS * TAPS]] * rows
+            for j in range(TAPS):
+                col = first_col + 8 * k + j
+                weights = [spread[layer, g, i * TAPS + j] for i in range(TAPS)]
+                for r in range(rows + TAPS - 1):
+                    value = source[g, row + r, col : col + 8, :]
+                    for i in range(TAPS):
+                        if 0 <= r - i < rows:
+                            sums[r - i] = sums[r - i] + weights[i] * value
+            for r in range(rows):
                 mixed[g, row + r, 8 * k : 8 * k + 8, :] = sums[r]
-        return carry
-
-    lax.fori_loop(0, groups * steps, step_of, 0)
+            return carry
+
+        lax.fori_loop(0, groups * steps, step_of, 0)
 
 
 def pointwise(mixed, layer, lats, slot, residual, store, weights):
@@ -215,7 +215,7 @@
     weights = (mod_ref, up_ref, up_bias_ref, down_ref, down_bias_ref, scale_ref)
 
     wide_slot = slot + 8
-    depthwise(first, spread, mixed, 0, wide, wide_slot // 8, LEFT - reach)
+    depthwise(first, spread, mixed, 0, wide, 13, wide_slot // 8, LEFT - reach)
 
     def first_store(g, row, value):
         second[g, pl.ds(row, ROWS), :, :] = value
@@ -234,7 +234,7 @@
     def _():
         second[:, REACH + lats :, :, :] = jnp.zeros((groups, REACH, wide_slot, LANES), jnp.float32)
 
-    depthwise(second, spread, mixed, 1, lats, slot // 8, 0)
+    depthwise(second, spread, mixed, 1, lats, 16, slot // 8, 0)
 
     def final_store(g, row, value):
         final[g, pl.ds(row, ROWS), :, :] = value
@@ -287,10 +287,11 @@
     )(pieces)
 
 
-def run_to_cells(pieces, cells, channels, tiles):
+def run_to_cells(pieces, cells, channels, tiles, edge):
+    outs = [(cells, channels), (edge, channels), (edge, channels)]
     return pl.pallas_call(
         lambda *refs: to_cells_kernel(*refs, tiles=tiles),
-        out_shape=jax.ShapeDtypeStruct((cells, channels), jnp.bfloat16),
+        out_shape=[jax.ShapeDtypeStruct(out, jnp.bfloat16) for out in outs],
         scratch_shapes=[pltpu.VMEM(pieces.shape, jnp.float32)],
         name="to_cells",
     )(pieces)
@@ -319,13 +320,13 @@
     )(edges, *arrays)
 
 
-def halo_of(x, seg):
+def halo_of(x, north, south, seg):
     rows, segs = lax.axis_size("y"), lax.axis_size("xc")
     reach = 2 * REACH
     down = [(i, i + 1) for i in range(rows - 1)]
     up = [(j, i) for i, j in down]
-    top = lax.ppermute(x[-reach:], "y", down)
-    bottom = lax.ppermute(x[:reach], "y", up)
+    top = lax.ppermute(south, "y", down)
+    bottom = lax.ppermute(north, "y", up)
     east = [(i, (i + 1) % segs) for i in range(segs)]
     west = [(j, i) for i, j in east]
 
@@ -337,6 +338,11 @@
     left = lax.ppermute(columns(seg - reach), "xc", east)
     right = lax.ppermute(columns(0), "xc", west)
     return top, bottom, left, right
+
+
+def gathered(row, axis):
+    copies = jnp.broadcast_to(row, (lax.axis_size(axis), row.shape[1]))
+    return lax.all_to_all(copies, axis, 0, 0, tiled=True)
 
 
 def on_device(
@@ -357,24 +363,23 @@
     band = lax.axis_index("y")
     edges = jnp.stack([band == 0, band == lax.axis_size("y") - 1]).astype(jnp.int32)
 
-    pieces = run_cut(field, seg, slot)
     filters = jnp.concatenate(
         [conv_kernel.reshape(layers, chans, TAPS * TAPS), conv_bias[:, :, None]], axis=2
     )
-    pieces, filters = lax.optimization_barrier((pieces, filters))
+    filters = gathered(filters.reshape(1, -1), "xc")
+    pieces = run_cut(field, seg, slot)
     shape = (peers, chans * tiles, LANES)
     around = ("zh", "zl", "xc")
     pieces = lax.all_to_all(pieces.reshape(shape), around, 0, 0, tiled=True).reshape(-1, LANES)
-
-    filters = jnp.broadcast_to(filters.reshape(1, -1), (channels // chans, filters.size))
-    filters = lax.all_to_all(filters, ("zl", "xc"), 0, 0, tiled=True)
+    pieces, filters = lax.optimization_barrier((pieces, filters))
+    filters = gathered(filters.reshape(1, -1), "zl")
     filters = filters.reshape(channels // chans, layers, chans, TAPS * TAPS + 1)
     filters = filters.transpose(1, 3, 0, 2).reshape(layers, TAPS * TAPS + 1, channels)
 
-    x = run_to_cells(pieces, halves * lats * slot, channels, tiles)
-    x = x.reshape(halves * lats, slot, channels)
+    cells = run_to_cells(pieces, halves * lats * slot, channels, tiles, 2 * REACH * slot)
+    x, north, south = [part.reshape(-1, slot, channels) for part in cells]
     pieces = run_blocks(
-        edges, x, halo_of(x, seg), filters, mods,
+        edges, x, halo_of(x, north, south, seg), filters, mods,
         expand_weight, expand_bias, project_weight, project_bias, layer_scale, tiles,
     )
     pieces = lax.all_to_all(pieces.reshape(shape), around, 0, 0, tiled=True).reshape(-1, LANES)

time: 194 us -> 197 us (1.015)
  the two profiles are of different devices: /device:TPU:41 before, /device:TPU:33 now
where the time goes in v2:
time: 197 us; the launch traced here: 196 us
  blocking collectives  58.5 us (30%)
  waiting for transfers between devices  47.4 us (24%)
  Pallas kernels  43.6 us (22%)
  starting transfers between devices  34.7 us (18%)
  local copies, waits for them, and re-layouts  8.67 us (4%)
  between operations  2.24 us (1%)
    all_to_all x1, blocking collectives, on_device(): lax.all_to_all(pieces.reshape(shape), around, 0, 0, tiled=True)  58.5 us
    all_to_all x1, waiting for transfers between devices, on_device(): lax.all_to_all(pieces.reshape(shape), around, 0, 0, tiled=True)  41.2 us
    pallas_call x1, Pallas kernels, run_blocks(): pl.pallas_call(lambda *refs: blocks_kernel(*refs, tiles=tiles), out_shape...  30.9 us
    all_to_all x1, starting transfers between devices, on_device(): lax.all_to_all(pieces.reshape(shape), around, 0, 0, tiled=True)  19.1 us
    all_to_all x2, starting transfers between devices, gathered(): return lax.all_to_all(copies, axis, 0, 0, tiled=True)  8.47 us
    pallas_call x1, Pallas kernels, run_paste(): pl.pallas_call(lambda *refs: paste_kernel(*refs, seg=seg, slot=slot), out...  5.44 us
    pallas_call x1, Pallas kernels, run_cut(): pl.pallas_call(lambda *refs: cut_kernel(*refs, seg=seg, slot=slot), out_s...  4.87 us
  transfers between devices with their start and end apart: 7, of which 4 were waited for; matrix products, arithmetic and copies ran while one was open for 2% of the time, Pallas kernels for 4%

profile of v2, /device:TPU:33, one launch (start us, length us, event | category | flops | bytes accessed | tf_op | source)
XLA Modules:
  0.0 196.2 jit_solution(9072806299347284422)
XLA Ops:
  0.0 0.0 copy-start
  0.0 0.0 copy-start.6
  0.0 0.7 copy-done.6
  0.7 0.1 copy.17
  0.8 0.8 copy.16
  1.6 0.1 reshape.51
  1.6 0.1 pad_maximum_fusion.2
  1.7 0.1 broadcast_in_dim.18
  1.8 0.6 broadcast_in_dim.19
  2.4 5.0 %all-to-all-start.1 = ((f32[8,1,400]{2,1,0:T(1,128)}), f32[8,1,400]{2,1,0:T(1,128)S(1)}, u32[]{:S(2)}, u32[]{:S(2)}) async-start(f32[8,1,400]{2,1,0:T(1,128)} %broadcast_in_dim.19), calls=%async_computation.1 | async-start | bytes 32768 | tf_op jit(solution)/shard_map/all_to_all | solution.py:345
  7.4 4.9 %cut.1 = bf16[3072,128]{1,0:T(8,128)(2,1)} custom-call(bf16[4,16,16,360]{3,2,1,0:T(8,128)(2,1)} %refs_0_.1), custom_call_target="tpu_custom_call" | custom-call | tf_op jit(solution)/shard_map/cut/pallas_call | solution.py:266
  12.3 0.0 all-to-all-done.1
  12.3 19.1 %all-to-all-start = ((bf16[128,24,128]{2,1,0:T(8,128)(2,1)}), bf16[128,24,128]{2,1,0:T(8,128)(2,1)S(1)}, u32[]{:S(2)}, u32[]{:S(2)}) async-start(bf16[128,24,128]{2,1,0:T(8,128)(2,1)} %bitcast.18), calls=%async_computation | async-start | bytes 1572864 | tf_op jit(solution)/shard_map/all_to_all | solution.py:373
  31.4 0.0 copy-start.7
  31.5 0.6 copy-done.7
  32.1 0.7 dynamic_slice.6
  34.9 41.2 %all-to-all-done = bf16[128,24,128]{2,1,0:T(8,128)(2,1)S(1)} async-done(((bf16[128,24,128]{2,1,0:T(8,128)(2,1)}), bf16[128,24,128]{2,1,0:T(8,128)(2,1)S(1)}, u32[]{:S(2)}, u32[]{:S(2)}) %all-to-all-start) | async-done | bytes 786464 | tf_op jit(solution)/shard_map/all_to_all | solution.py:373
  76.0 0.0 copy-start.1
  76.0 0.1 broadcast_in_dim.20
  76.1 0.8 broadcast_in_dim.21
  76.9 3.5 %all-to-all-start.2 = ((f32[8,1,3200]{2,1,0:T(1,128)}), f32[8,1,3200]{2,1,0:T(1,128)S(1)}, u32[]{:S(2)}, u32[]{:S(2)}) async-start(f32[8,1,3200]{2,1,0:T(1,128)} %broadcast_in_dim.21), calls=%async_computation.2 | async-start | bytes 204800 | tf_op jit(solution)/shard_map/all_to_all | solution.py:345
  80.4 0.0 copy-done.1
  80.4 2.4 %to_cells.1 = (bf16[1536,256]{1,0:T(8,128)(2,1)}, bf16[288,256]{1,0:T(8,128)(2,1)}, bf16[288,256]{1,0:T(8,128)(2,1)}) custom-call(bf16[3072,128]{1,0:T(8,128)(2,1)} %bitcast.17), custom_call_target="tpu_custom_call" | custom-call | tf_op jit(solution)/shard_map/to_cells/pallas_call | solution.py:292
  82.8 3.2 %collective-permute-start = (bf16[6,48,256]{2,1,0:T(8,128)(2,1)}, bf16[6,48,256]{2,1,0:T(8,128)(2,1)S(1)}, u32[]{:S(2)}, u32[]{:S(2)}) collective-permute-start(bf16[6,48,256]{2,1,0:T(8,128)(2,1)} %bitcast.27), channel_id=1, source_target_pairs={{0,128},{128,256},{256,384},{1,129},{129,257},{257,385},{2,130},{1... | collective-permute-start | bytes 442376 | tf_op jit(solution)/shard_map/ppermute | solution.py:328
  86.0 1.3 collective-permute-start.1
  87.3 1.1 fusion
  88.4 0.3 collective-permute-done.refs_2_
  88.7 0.0 copy-start.2
  88.7 3.4 %collective-permute-done.1.refs_3_ = bf16[6,48,256]{2,1,0:T(8,128)(2,1)S(1)} collective-permute-done((bf16[6,48,256]{2,1,0:T(8,128)(2,1)}, bf16[6,48,256]{2,1,0:T(8,128)(2,1)S(1)}, u32[]{:S(2)}, u32[]{:S(2)}) %collective-permute-start.1) | collective-permute-done | bytes 147488 | tf_op jit(solution)/shard_map/ppermute | solution.py:329
  92.1 0.0 copy-start.3
  92.2 0.0 copy-done.2
  92.2 0.6 copy-done.3
  92.8 2.6 %collective-permute-start.2 = (bf16[44,6,256]{2,1,0:T(8,128)(2,1)S(1)}, bf16[44,6,256]{2,1,0:T(8,128)(2,1)S(1)}, u32[]{:S(2)}, u32[]{:S(2)}) collective-permute-start(bf16[44,6,256]{2,1,0:T(8,128)(2,1)S(1)} %pad_maximum_fusion), channel_id=1, source_target_pairs={{0,1},{1,2},{2,3},{3,4},{4,5},{5,6},{6,7},{7,0},{8,9},{9,10},{10,1... | collective-permute-start | bytes 405512 | tf_op jit(solution)/shard_map/ppermute | solution.py:338
  95.4 0.0 collective-permute-start.3
  95.5 0.0 copy-done
  95.5 0.6 reshape_squeeze.3.refs_7_
  96.1 0.7 add_convert_fusion.refs_0_
  96.8 0.0 all-to-all-done.2
  96.8 0.2 reduce
  97.0 0.3 reshape.55
  97.4 0.8 copy.19.refs_6_
  98.2 0.0 collective-permute-done.2.refs_4_
  98.2 0.0 copy-start.4
  98.2 2.5 %collective-permute-done.3.refs_5_ = bf16[44,6,256]{2,1,0:T(8,128)(2,1)S(1)} collective-permute-done((bf16[44,6,256]{2,1,0:T(8,128)(2,1)S(1)}, bf16[44,6,256]{2,1,0:T(8,128)(2,1)S(1)}, u32[]{:S(2)}, u32[]{:S(2)}) %collective-permute-start.3) | collective-permute-done | bytes 135200 | tf_op jit(solution)/shard_map/ppermute | solution.py:339
  100.7 0.0 copy-done.4
  100.7 0.0 copy-start.5
  100.7 0.7 copy-done.5
  101.3 30.9 %blocks.1 = bf16[3072,128]{1,0:T(8,128)(2,1)} custom-call(s32[2]{0:T(128)} %add_convert_fusion.refs_0_, bf16[32,48,256]{2,1,0:T(8,128)(2,1)} %bitcast.21, bf16[6,48,256]{2,1,0:T(8,128)(2,1)} %copy-done.2, bf16[6,48,256]{2,1,0:T(8,128)(2,1)} %copy-done.3, bf16[44,6,256]{2,1,0:T(8,128)(2,1)} %copy-done.4, bf16[44,6,256]{2,1,0:T(8,128)(2,1)} %copy-done.5, ...), custom_call_target="tpu_custom_call" | custom-call | tf_op jit(solution)/shard_map/blocks/pallas_call | solution.py:307
  132.2 58.5 %all_to_all.25 = bf16[128,24,128]{2,1,0:T(8,128)(2,1)} all-to-all(bf16[128,24,128]{2,1,0:T(8,128)(2,1)} %bitcast.16), channel_id=1, replica_groups=mesh['y'=4,'zh'=2,'zl'=8,'xc'=8] {'zh','zl','xc'}, dimensions={0} | all-to-all | bytes 1572864 | tf_op jit(solution)/shard_map/all_to_all | solution.py:385
  190.8 5.4 %paste.1 = bf16[4,16,16,360]{3,2,1,0:T(8,128)(2,1)} custom-call(bf16[3072,128]{1,0:T(8,128)(2,1)} %bitcast.19), custom_call_target="tpu_custom_call" | custom-call | tf_op jit(solution)/shard_map/paste/pallas_call | solution.py:279
  (7 shorter events, 0.2 us)
Async XLA Ops:
  0.0 95.5 %copy-start = (f32[2,20,2,256]{3,2,1,0:T(2,128)S(1)}, f32[2,20,2,256]{3,2,1,0:T(2,128)}, u32[]{:S(2)}) copy-start(f32[2,20,2,256]{3,2,1,0:T(2,128)} %param.14) | copy-start | bytes 245764
  0.0 0.7 copy-start.6
  2.4 9.8 %all-to-all-start.1 = ((f32[8,1,400]{2,1,0:T(1,128)}), f32[8,1,400]{2,1,0:T(1,128)S(1)}, u32[]{:S(2)}, u32[]{:S(2)}) async-start(f32[8,1,400]{2,1,0:T(1,128)} %broadcast_in_dim.19), calls=%async_computation.1 | async-start | bytes 32768 | tf_op jit(solution)/shard_map/all_to_all | solution.py:345
  12.3 63.7 %all-to-all-start = ((bf16[128,24,128]{2,1,0:T(8,128)(2,1)}), bf16[128,24,128]{2,1,0:T(8,128)(2,1)S(1)}, u32[]{:S(2)}, u32[]{:S(2)}) async-start(bf16[128,24,128]{2,1,0:T(8,128)(2,1)} %bitcast.18), calls=%async_computation | async-start | bytes 1572864 | tf_op jit(solution)/shard_map/all_to_all | solution.py:373
  31.4 0.7 copy-start.7
  76.0 4.4 %copy-start.1 = (bf16[128,24,128]{2,1,0:T(8,128)(2,1)}, bf16[128,24,128]{2,1,0:T(8,128)(2,1)S(1)}, u32[]{:S(2)}) copy-start(bf16[128,24,128]{2,1,0:T(8,128)(2,1)S(1)} %all-to-all-done) | copy-start | bytes 2359300
  76.9 19.8 %all-to-all-start.2 = ((f32[8,1,3200]{2,1,0:T(1,128)}), f32[8,1,3200]{2,1,0:T(1,128)S(1)}, u32[]{:S(2)}, u32[]{:S(2)}) async-start(f32[8,1,3200]{2,1,0:T(1,128)} %broadcast_in_dim.21), calls=%async_computation.2 | async-start | bytes 204800 | tf_op jit(solution)/shard_map/all_to_all | solution.py:345
  82.8 5.9 %collective-permute-start = (bf16[6,48,256]{2,1,0:T(8,128)(2,1)}, bf16[6,48,256]{2,1,0:T(8,128)(2,1)S(1)}, u32[]{:S(2)}, u32[]{:S(2)}) collective-permute-start(bf16[6,48,256]{2,1,0:T(8,128)(2,1)} %bitcast.27), channel_id=1, source_target_pairs={{0,128},{128,256},{256,384},{1,129},{129,257},{257,385},{2,130},{1... | collective-permute-start | bytes 442376 | tf_op jit(solution)/shard_map/ppermute | solution.py:328
  86.0 6.1 %collective-permute-start.1 = (bf16[6,48,256]{2,1,0:T(8,128)(2,1)}, bf16[6,48,256]{2,1,0:T(8,128)(2,1)S(1)}, u32[]{:S(2)}, u32[]{:S(2)}) collective-permute-start(bf16[6,48,256]{2,1,0:T(8,128)(2,1)} %bitcast.26), channel_id=1, source_target_pairs={{128,0},{256,128},{384,256},{129,1},{257,129},{385,257},{130,2},{2... | collective-permute-start | bytes 442376 | tf_op jit(solution)/shard_map/ppermute | solution.py:329
  88.7 3.5 %copy-start.2 = (bf16[6,48,256]{2,1,0:T(8,128)(2,1)}, bf16[6,48,256]{2,1,0:T(8,128)(2,1)S(1)}, u32[]{:S(2)}) copy-start(bf16[6,48,256]{2,1,0:T(8,128)(2,1)S(1)} %collective-permute-done.refs_2_) | copy-start | bytes 442372
  92.1 0.7 copy-start.3
  92.8 5.4 %collective-permute-start.2 = (bf16[44,6,256]{2,1,0:T(8,128)(2,1)S(1)}, bf16[44,6,256]{2,1,0:T(8,128)(2,1)S(1)}, u32[]{:S(2)}, u32[]{:S(2)}) collective-permute-start(bf16[44,6,256]{2,1,0:T(8,128)(2,1)S(1)} %pad_maximum_fusion), channel_id=1, source_target_pairs={{0,1},{1,2},{2,3},{3,4},{4,5},{5,6},{6,7},{7,0},{8,9},{9,10},{10,1... | collective-permute-start | bytes 405512 | tf_op jit(solution)/shard_map/ppermute | solution.py:338
  95.4 5.2 %collective-permute-start.3 = (bf16[44,6,256]{2,1,0:T(8,128)(2,1)S(1)}, bf16[44,6,256]{2,1,0:T(8,128)(2,1)S(1)}, u32[]{:S(2)}, u32[]{:S(2)}) collective-permute-start(bf16[44,6,256]{2,1,0:T(8,128)(2,1)S(1)} %pad_maximum_fusion.1), channel_id=1, source_target_pairs={{1,0},{2,1},{3,2},{4,3},{5,4},{6,5},{7,6},{0,7},{9,8},{10,9},{11,1... | collective-permute-start | bytes 405512 | tf_op jit(solution)/shard_map/ppermute | solution.py:339
  98.2 2.5 %copy-start.4 = (bf16[44,6,256]{2,1,0:T(8,128)(2,1)}, bf16[44,6,256]{2,1,0:T(8,128)(2,1)S(1)}, u32[]{:S(2)}) copy-start(bf16[44,6,256]{2,1,0:T(8,128)(2,1)S(1)} %collective-permute-done.2.refs_4_) | copy-start | bytes 405508
  100.7 0.7 copy-start.5

commit v3 on v2

--- a/solution.py
+++ b/solution.py
@@ -133,15 +133,18 @@
         def step_of(step, carry):
             g = step // steps
             row = jnp.minimum((step % steps) * rows, lats - rows)
-            sums = [spread[layer, g, TAPS * TAPS]] * rows
-            for j in range(TAPS):
-                col = first_col + 8 * k + j
+            def column_of(j, sums):
+                sums = list(sums)
                 weights = [spread[layer, g, i * TAPS + j] for i in range(TAPS)]
                 for r in range(rows + TAPS - 1):
-                    value = source[g, row + r, col : col + 8, :]
+                    value = source[g, row + r, pl.ds(first_col + 8 * k + j, 8), :]
                     for i in range(TAPS):
                         if 0 <= r - i < rows:
                             sums[r - i] = sums[r - i] + weights[i] * value
+                return tuple(sums)
+
+            start = (spread[layer, g, TAPS * TAPS],) * rows
+            sums = lax.fori_loop(0, TAPS, column_of, start)
             for r in range(rows):
                 mixed[g, row + r, 8 * k : 8 * k + 8, :] = sums[r]
             return carry
@@ -215,7 +218,7 @@
     weights = (mod_ref, up_ref, up_bias_ref, down_ref, down_bias_ref, scale_ref)
 
     wide_slot = slot + 8
-    depthwise(first, spread, mixed, 0, wide, 13, wide_slot // 8, LEFT - reach)
+    depthwise(first, spread, mixed, 0, wide, 19, wide_slot // 8, LEFT - reach)
 
     def first_store(g, row, value):
         second[g, pl.ds(row, ROWS), :, :] = value
@@ -234,7 +237,7 @@
     def _():
         second[:, REACH + lats :, :, :] = jnp.zeros((groups, REACH, wide_slot, LANES), jnp.float32)
 
-    depthwise(second, spread, mixed, 1, lats, 16, slot // 8, 0)
+    depthwise(second, spread, mixed, 1, lats, 32, slot // 8, 0)
 
     def final_store(g, row, value):
         final[g, pl.ds(row, ROWS), :, :] = value
@@ -259,13 +262,17 @@
     out_ref[...] = rows32[...].astype(jnp.bfloat16)
 
 
+def near(x):
+    return pltpu.with_memory_space_constraint(x, pltpu.VMEM)
+
+
 def run_cut(field, seg, slot):
     chans, members, lats, lons = field.shape
     tiles = lats * slot // LANES
     rows = members * (lons // seg) * chans * tiles
     return pl.pallas_call(
         lambda *refs: cut_kernel(*refs, seg=seg, slot=slot),
-        out_shape=jax.ShapeDtypeStruct((rows, LANES), jnp.bfloat16),
+        out_shape=pltpu.VMEM((rows, LANES), jnp.bfloat16),
         scratch_shapes=[
             pltpu.VMEM((-(-lons // LANES), chans * members * lats, LANES), jnp.float32),
             pltpu.VMEM((rows, LANES), jnp.float32),
@@ -284,17 +291,17 @@
             pltpu.VMEM((-(-lons // LANES), chans * members * lats, LANES), jnp.float32),
         ],
         name="paste",
-    )(pieces)
+    )(near(pieces))
 
 
 def run_to_cells(pieces, cells, channels, tiles, edge):
     outs = [(cells, channels), (edge, channels), (edge, channels)]
     return pl.pallas_call(
         lambda *refs: to_cells_kernel(*refs, tiles=tiles),
-        out_shape=[jax.ShapeDtypeStruct(out, jnp.bfloat16) for out in outs],
+        out_shape=[pltpu.VMEM(out, jnp.bfloat16) for out in outs],
         scratch_shapes=[pltpu.VMEM(pieces.shape, jnp.float32)],
         name="to_cells",
-    )(pieces)
+    )(near(pieces))
 
 
 def run_blocks(edges, x, halos, taps, mods, up, up_bias, down, down_bias, scale, tiles):
@@ -306,7 +313,7 @@
     wide_slot = slot + 8
     return pl.pallas_call(
         lambda *refs: blocks_kernel(*refs, tiles=tiles),
-        out_shape=jax.ShapeDtypeStruct((rows, LANES), jnp.bfloat16),
+        out_shape=pltpu.VMEM((rows, LANES), jnp.bfloat16),
         in_specs=[pl.BlockSpec(memory_space=pltpu.SMEM)] + [vmem] * len(arrays),
         scratch_shapes=[
             pltpu.VMEM((groups, lats + 4 * REACH, LEFT + wide_slot, LANES), jnp.float32),
@@ -316,8 +323,9 @@
             pltpu.VMEM((groups, lats, slot, LANES), jnp.float32),
             pltpu.VMEM((rows, LANES), jnp.float32),
         ],
+        compiler_params=pltpu.CompilerParams(vmem_limit_bytes=40 * 2**20),
         name="blocks",
-    )(edges, *arrays)
+    )(edges, *[near(a) for a in arrays])
 
 
 def halo_of(x, north, south, seg):
@@ -338,11 +346,6 @@
     left = lax.ppermute(columns(seg - reach), "xc", east)
     right = lax.ppermute(columns(0), "xc", west)
     return top, bottom, left, right
-
-
-def gathered(row, axis):
-    copies = jnp.broadcast_to(row, (lax.axis_size(axis), row.shape[1]))
-    return lax.all_to_all(copies, axis, 0, 0, tiled=True)
 
 
 def on_device(
@@ -366,13 +369,13 @@
     filters = jnp.concatenate(
         [conv_kernel.reshape(layers, chans, TAPS * TAPS), conv_bias[:, :, None]], axis=2
     )
-    filters = gathered(filters.reshape(1, -1), "xc")
     pieces = run_cut(field, seg, slot)
+    pieces, filters = lax.optimization_barrier((pieces, filters))
     shape = (peers, chans * tiles, LANES)
     around = ("zh", "zl", "xc")
     pieces = lax.all_to_all(pieces.reshape(shape), around, 0, 0, tiled=True).reshape(-1, LANES)
-    pieces, filters = lax.optimization_barrier((pieces, filters))
-    filters = gathered(filters.reshape(1, -1), "zl")
+    filters = jnp.broadcast_to(filters.reshape(1, -1), (channels // chans, filters.size))
+    filters = lax.all_to_all(filters, ("zl", "xc"), 0, 0, tiled=True)
     filters = filters.reshape(channels // chans, layers, chans, TAPS * TAPS + 1)
     filters = filters.transpose(1, 3, 0, 2).reshape(layers, TAPS * TAPS + 1, channels)
 

time: 197 us -> 186 us (0.944)
  Pallas kernels: 43.6 us -> 36 us
  starting transfers between devices: 34.7 us -> 31.9 us
    pallas_call x1, Pallas kernels: 30.9 us -> 26.5 us  [run_blocks(): pl.pallas_call(lambda *refs: blocks_kernel(*refs, tiles=tiles), out_shape...]
    all_to_all x2 -> x1, starting transfers between devices: 8.47 us -> 5.48 us  [on_device(): filters = lax.all_to_all(filters, ('zl', 'xc'), 0, 0, tiled=True)]
    pallas_call x1, Pallas kernels: 2.41 us -> 0.32 us  [run_to_cells(): pl.pallas_call(lambda *refs: to_cells_kernel(*refs, tiles=tiles), out_sha...]
  transfers between devices with their start and end apart: 7 -> 6, of which waited for: 4 -> 4; matrix products, arithmetic and copies ran while one was open for 2% -> 3% of each run, Pallas kernels for 4% -> 0%
where the time goes in v3:
time: 186 us; the launch traced here: 185 us
  blocking collectives  58.1 us (31%)
  waiting for transfers between devices  48 us (26%)
  Pallas kernels  36 us (19%)
  starting transfers between devices  31.9 us (17%)
  local copies, waits for them, and re-layouts  6.78 us (4%)
  other arithmetic  2.58 us (1%)
    all_to_all x1, blocking collectives, on_device(): lax.all_to_all(pieces.reshape(shape), around, 0, 0, tiled=True)  58.1 us
    all_to_all x1, waiting for transfers between devices, on_device(): lax.all_to_all(pieces.reshape(shape), around, 0, 0, tiled=True)  41.6 us
    pallas_call x1, Pallas kernels, run_blocks(): pl.pallas_call(lambda *refs: blocks_kernel(*refs, tiles=tiles), out_shape...  26.5 us
    all_to_all x1, starting transfers between devices, on_device(): lax.all_to_all(pieces.reshape(shape), around, 0, 0, tiled=True)  19.3 us
    all_to_all x1, starting transfers between devices, on_device(): filters = lax.all_to_all(filters, ('zl', 'xc'), 0, 0, tiled=True)  5.48 us
    pallas_call x1, Pallas kernels, run_cut(): pl.pallas_call(lambda *refs: cut_kernel(*refs, seg=seg, slot=slot), out_s...  4.87 us
    pallas_call x1, Pallas kernels, run_paste(): pl.pallas_call(lambda *refs: paste_kernel(*refs, seg=seg, slot=slot), out...  4.3 us
    ppermute x1, waiting for transfers between devices, halo_of(): bottom = lax.ppermute(north, 'y', up)  3.79 us
  transfers between devices with their start and end apart: 6, of which 4 were waited for; matrix products, arithmetic and copies ran while one was open for 3% of the time, Pallas kernels for 0%

profile of v3, /device:TPU:33, one launch (start us, length us, event | category | flops | bytes accessed | tf_op | source)
XLA Modules:
  0.0 185.1 jit_solution(9739741506570629921)
XLA Ops:
  0.0 0.0 copy-start
  0.0 0.0 copy-start.6
  0.0 0.7 copy-done.6
  0.7 0.1 copy.17
  0.8 0.8 copy.16
  1.6 0.1 reshape.40
  1.6 4.9 %cut.1 = bf16[3072,128]{1,0:T(8,128)(2,1)} custom-call(bf16[4,16,16,360]{3,2,1,0:T(8,128)(2,1)} %refs_0_.1), custom_call_target="tpu_custom_call" | custom-call | tf_op jit(solution)/shard_map/cut/pallas_call | solution.py:273
  6.5 0.1 pad_maximum_fusion.2
  6.6 19.3 %all-to-all-start = ((bf16[128,24,128]{2,1,0:T(8,128)(2,1)}), bf16[128,24,128]{2,1,0:T(8,128)(2,1)S(1)}, u32[]{:S(2)}, u32[]{:S(2)}) async-start(bf16[128,24,128]{2,1,0:T(8,128)(2,1)} %bitcast.3), calls=%async_computation | async-start | bytes 1572864 | tf_op jit(solution)/shard_map/all_to_all | solution.py:376
  25.9 0.0 copy-start.7
  25.9 0.6 copy-done.7
  26.6 0.6 dynamic_slice.6
  28.2 0.1 broadcast_in_dim.11
  28.9 41.6 %all-to-all-done = bf16[128,24,128]{2,1,0:T(8,128)(2,1)S(1)} async-done(((bf16[128,24,128]{2,1,0:T(8,128)(2,1)}), bf16[128,24,128]{2,1,0:T(8,128)(2,1)S(1)}, u32[]{:S(2)}, u32[]{:S(2)}) %all-to-all-start) | async-done | bytes 786464 | tf_op jit(solution)/shard_map/all_to_all | solution.py:376
  70.5 0.7 broadcast_in_dim.12
  71.2 5.5 %all-to-all-start.1 = ((f32[64,1,400]{2,1,0:T(1,128)}), f32[64,1,400]{2,1,0:T(1,128)S(1)}, u32[]{:S(2)}, u32[]{:S(2)}) async-start(f32[64,1,400]{2,1,0:T(1,128)} %broadcast_in_dim.12), calls=%async_computation.1 | async-start | bytes 262144 | tf_op jit(solution)/shard_map/all_to_all | solution.py:378
  76.7 0.3 to_cells.1
  77.0 3.2 %collective-permute-start = (bf16[6,48,256]{2,1,0:T(8,128)(2,1)S(1)}, bf16[6,48,256]{2,1,0:T(8,128)(2,1)S(1)}, u32[]{:S(2)}, u32[]{:S(2)}) collective-permute-start(bf16[6,48,256]{2,1,0:T(8,128)(2,1)S(1)} %bitcast.19), channel_id=1, source_target_pairs={{0,128},{128,256},{256,384},{1,129},{129,257},{257,385},{2,130},{1... | collective-permute-start | bytes 442376 | tf_op jit(solution)/shard_map/ppermute | solution.py:336
  80.3 1.3 collective-permute-start.1
  81.6 1.5 collective-permute-done.refs_2_
  83.1 3.8 %collective-permute-done.1.refs_3_ = bf16[6,48,256]{2,1,0:T(8,128)(2,1)S(1)} collective-permute-done((bf16[6,48,256]{2,1,0:T(8,128)(2,1)S(1)}, bf16[6,48,256]{2,1,0:T(8,128)(2,1)S(1)}, u32[]{:S(2)}, u32[]{:S(2)}) %collective-permute-start.1) | collective-permute-done | bytes 147488 | tf_op jit(solution)/shard_map/ppermute | solution.py:337
  86.9 0.0 copy-start.2
  86.9 0.7 pad_maximum_fusion
  87.7 0.0 copy-start.1
  87.7 2.6 %collective-permute-start.2 = (bf16[44,6,256]{2,1,0:T(8,128)(2,1)}, bf16[44,6,256]{2,1,0:T(8,128)(2,1)}, u32[]{:S(2)}, u32[]{:S(2)}) collective-permute-start(bf16[44,6,256]{2,1,0:T(8,128)(2,1)} %pad_maximum_fusion), channel_id=1, source_target_pairs={{0,1},{1,2},{2,3},{3,4},{4,5},{5,6},{6,7},{7,0},{8,9},{9,10},{10,1... | collective-permute-start | bytes 405512 | tf_op jit(solution)/shard_map/ppermute | solution.py:346
  90.2 0.7 pad_maximum_fusion.1
  91.0 0.0 collective-permute-start.3
  91.0 0.0 copy-done
  91.0 0.1 add_convert_fusion.refs_0_
  91.1 0.0 all-to-all-done.1
  91.1 1.0 reduce
  92.1 1.2 reshape.46
  93.2 0.7 copy.18
  94.0 0.0 copy-start.3
  94.0 0.0 copy-start.4
  94.0 0.0 copy-start.5
  94.0 1.1 copy.19.refs_6_
  95.1 0.0 collective-permute-done.2.refs_4_
  95.1 1.1 collective-permute-done.3.refs_5_
  96.2 0.0 copy-done.2
  96.2 0.0 copy-done.1
  96.2 0.0 copy-done.3
  96.2 0.0 copy-done.4
  96.2 0.0 copy-done.5
  96.2 26.5 %blocks.1 = bf16[3072,128]{1,0:T(8,128)(2,1)S(1)} custom-call(s32[2]{0:T(128)S(1)} %add_convert_fusion.refs_0_, bf16[32,48,256]{2,1,0:T(8,128)(2,1)S(1)} %bitcast.17, bf16[6,48,256]{2,1,0:T(8,128)(2,1)S(1)} %collective-permute-done.refs_2_, bf16[6,48,256]{2,1,0:T(8,128)(2,1)S(1)} %collective-permute-done.1.refs_3_, ...), custom_call_target="tpu_custom_call" | custom-call | tf_op jit(solution)/shard_map/blocks/pallas_call | solution.py:314
  122.7 58.1 %all_to_all.16 = bf16[128,24,128]{2,1,0:T(8,128)(2,1)S(1)} all-to-all(bf16[128,24,128]{2,1,0:T(8,128)(2,1)S(1)} %bitcast.13), channel_id=1, replica_groups=mesh['y'=4,'zh'=2,'zl'=8,'xc'=8] {'zh','zl','xc'}, dimensions={0} | all-to-all | bytes 1572864 | tf_op jit(solution)/shard_map/all_to_all | solution.py:388
  180.8 4.3 %paste.1 = bf16[4,16,16,360]{3,2,1,0:T(8,128)(2,1)} custom-call(bf16[3072,128]{1,0:T(8,128)(2,1)S(1)} %bitcast.15), custom_call_target="tpu_custom_call" | custom-call | tf_op jit(solution)/shard_map/paste/pallas_call | solution.py:286
  (5 shorter events, 0.1 us)
Async XLA Ops:
  0.0 91.0 %copy-start = (f32[2,20,2,256]{3,2,1,0:T(2,128)S(1)}, f32[2,20,2,256]{3,2,1,0:T(2,128)}, u32[]{:S(2)}) copy-start(f32[2,20,2,256]{3,2,1,0:T(2,128)} %param.14) | copy-start | bytes 245764
  0.0 0.7 copy-start.6
  6.6 63.9 %all-to-all-start = ((bf16[128,24,128]{2,1,0:T(8,128)(2,1)}), bf16[128,24,128]{2,1,0:T(8,128)(2,1)S(1)}, u32[]{:S(2)}, u32[]{:S(2)}) async-start(bf16[128,24,128]{2,1,0:T(8,128)(2,1)} %bitcast.3), calls=%async_computation | async-start | bytes 1572864 | tf_op jit(solution)/shard_map/all_to_all | solution.py:376
  25.9 0.7 copy-start.7
  71.2 19.8 %all-to-all-start.1 = ((f32[64,1,400]{2,1,0:T(1,128)}), f32[64,1,400]{2,1,0:T(1,128)S(1)}, u32[]{:S(2)}, u32[]{:S(2)}) async-start(f32[64,1,400]{2,1,0:T(1,128)} %broadcast_in_dim.12), calls=%async_computation.1 | async-start | bytes 262144 | tf_op jit(solution)/shard_map/all_to_all | solution.py:378
  77.0 6.1 %collective-permute-start = (bf16[6,48,256]{2,1,0:T(8,128)(2,1)S(1)}, bf16[6,48,256]{2,1,0:T(8,128)(2,1)S(1)}, u32[]{:S(2)}, u32[]{:S(2)}) collective-permute-start(bf16[6,48,256]{2,1,0:T(8,128)(2,1)S(1)} %bitcast.19), channel_id=1, source_target_pairs={{0,128},{128,256},{256,384},{1,129},{129,257},{257,385},{2,130},{1... | collective-permute-start | bytes 442376 | tf_op jit(solution)/shard_map/ppermute | solution.py:336
  80.3 6.6 %collective-permute-start.1 = (bf16[6,48,256]{2,1,0:T(8,128)(2,1)S(1)}, bf16[6,48,256]{2,1,0:T(8,128)(2,1)S(1)}, u32[]{:S(2)}, u32[]{:S(2)}) collective-permute-start(bf16[6,48,256]{2,1,0:T(8,128)(2,1)S(1)} %bitcast.18), channel_id=1, source_target_pairs={{128,0},{256,128},{384,256},{129,1},{257,129},{385,257},{130,2},{2... | collective-permute-start | bytes 442376 | tf_op jit(solution)/shard_map/ppermute | solution.py:337
  86.9 9.3 %copy-start.2 = (bf16[2,1024,256]{2,1,0:T(8,128)(2,1)S(1)}, bf16[2,1024,256]{2,1,0:T(8,128)(2,1)}, u32[]{:S(2)}) copy-start(bf16[2,1024,256]{2,1,0:T(8,128)(2,1)} %refs_10_.1) | copy-start | bytes 3145732
  87.7 8.5 %copy-start.1 = (bf16[2,256,1024]{2,1,0:T(8,128)(2,1)S(1)}, bf16[2,256,1024]{2,1,0:T(8,128)(2,1)}, u32[]{:S(2)}) copy-start(bf16[2,256,1024]{2,1,0:T(8,128)(2,1)} %refs_8_.1) | copy-start | bytes 3145732
  87.7 7.4 %collective-permute-start.2 = (bf16[44,6,256]{2,1,0:T(8,128)(2,1)}, bf16[44,6,256]{2,1,0:T(8,128)(2,1)}, u32[]{:S(2)}, u32[]{:S(2)}) collective-permute-start(bf16[44,6,256]{2,1,0:T(8,128)(2,1)} %pad_maximum_fusion), channel_id=1, source_target_pairs={{0,1},{1,2},{2,3},{3,4},{4,5},{5,6},{6,7},{7,0},{8,9},{9,10},{10,1... | collective-permute-start | bytes 405512 | tf_op jit(solution)/shard_map/ppermute | solution.py:346
  91.0 5.2 %collective-permute-start.3 = (bf16[44,6,256]{2,1,0:T(8,128)(2,1)}, bf16[44,6,256]{2,1,0:T(8,128)(2,1)}, u32[]{:S(2)}, u32[]{:S(2)}) collective-permute-start(bf16[44,6,256]{2,1,0:T(8,128)(2,1)} %pad_maximum_fusion.1), channel_id=1, source_target_pairs={{1,0},{2,1},{3,2},{4,3},{5,4},{6,5},{7,6},{0,7},{9,8},{10,9},{11,1... | collective-permute-start | bytes 405512 | tf_op jit(solution)/shard_map/ppermute | solution.py:347
  94.0 2.2 %copy-start.3 = (f32[2,1024]{1,0:T(2,128)S(1)}, f32[2,1024]{1,0:T(2,128)}, u32[]{:S(2)}) copy-start(f32[2,1024]{1,0:T(2,128)} %refs_9_.1) | copy-start | bytes 24580
  94.0 2.2 %copy-start.4 = (f32[2,256]{1,0:T(2,128)S(1)}, f32[2,256]{1,0:T(2,128)}, u32[]{:S(2)}) copy-start(f32[2,256]{1,0:T(2,128)} %refs_11_.1) | copy-start | bytes 6148
  94.0 2.3 %copy-start.5 = (f32[2,256]{1,0:T(2,128)S(1)}, f32[2,256]{1,0:T(2,128)}, u32[]{:S(2)}) copy-start(f32[2,256]{1,0:T(2,128)} %refs_12_.1) | copy-start | bytes 6148

commit v4 on v3

--- a/solution.py
+++ b/solution.py
@@ -178,9 +178,9 @@
             jnp.dot(normed, up_ref[layer], preferred_element_type=jnp.float32)
             + up_bias_ref[layer : layer + 1, :]
         )
-        active = (0.5 * hidden * (1.0 + lax.erf(hidden * 0.7071067811865476))).astype(jnp.bfloat16)
+        doubled = (hidden * (1.0 + lax.erf(hidden * 0.7071067811865476))).astype(jnp.bfloat16)
         result = (
-            jnp.dot(active, down_ref[layer], preferred_element_type=jnp.float32)
+            0.5 * jnp.dot(doubled, down_ref[layer], preferred_element_type=jnp.float32)
             + down_bias_ref[layer : layer + 1, :]
         )
         branch = (scale_ref[layer : layer + 1, :] * result).astype(jnp.bfloat16).astype(jnp.float32)
@@ -304,12 +304,12 @@
     )(near(pieces))
 
 
-def run_blocks(edges, x, halos, taps, mods, up, up_bias, down, down_bias, scale, tiles):
+def run_blocks(edges, x, halos, mods, up, up_bias, down, down_bias, scale, tiles):
     lats, slot, channels = x.shape
     groups = channels // LANES
     rows = lats * slot * channels // LANES
     vmem = pl.BlockSpec(memory_space=pltpu.VMEM)
-    arrays = (x, *halos, taps, mods, up, up_bias, down, down_bias, scale)
+    arrays = (x, *halos, mods, up, up_bias, down, down_bias, scale)
     wide_slot = slot + 8
     return pl.pallas_call(
         lambda *refs: blocks_kernel(*refs, tiles=tiles),
@@ -318,23 +318,24 @@
         scratch_shapes=[
             pltpu.VMEM((groups, lats + 4 * REACH, LEFT + wide_slot, LANES), jnp.float32),
             pltpu.VMEM((groups, lats + 2 * REACH, wide_slot, LANES), jnp.float32),
-            pltpu.VMEM((taps.shape[0], groups, TAPS * TAPS + 1, 8, LANES), jnp.float32),
+            pltpu.VMEM((up.shape[0], groups, TAPS * TAPS + 1, 8, LANES), jnp.float32),
             pltpu.VMEM((groups, lats + 2 * REACH, wide_slot, LANES), jnp.float32),
             pltpu.VMEM((groups, lats, slot, LANES), jnp.float32),
             pltpu.VMEM((rows, LANES), jnp.float32),
         ],
-        compiler_params=pltpu.CompilerParams(vmem_limit_bytes=40 * 2**20),
+        compiler_params=pltpu.CompilerParams(vmem_limit_bytes=24 * 2**20),
         name="blocks",
     )(edges, *[near(a) for a in arrays])
 
 
-def halo_of(x, north, south, seg):
+def halo_of(x, north, south, filters, seg):
     rows, segs = lax.axis_size("y"), lax.axis_size("xc")
     reach = 2 * REACH
     down = [(i, i + 1) for i in range(rows - 1)]
     up = [(j, i) for i, j in down]
     top = lax.ppermute(south, "y", down)
     bottom = lax.ppermute(north, "y", up)
+    top, bottom, filters = lax.optimization_barrier((top, bottom, filters))
     east = [(i, (i + 1) % segs) for i in range(segs)]
     west = [(j, i) for i, j in east]
 
@@ -345,7 +346,7 @@
 
     left = lax.ppermute(columns(seg - reach), "xc", east)
     right = lax.ppermute(columns(0), "xc", west)
-    return top, bottom, left, right
+    return top, bottom, left, right, filters
 
 
 def on_device(
@@ -366,15 +367,16 @@
     band = lax.axis_index("y")
     edges = jnp.stack([band == 0, band == lax.axis_size("y") - 1]).astype(jnp.int32)
 
+    pieces = run_cut(field, seg, slot)
+    pieces, conv_kernel, conv_bias = lax.optimization_barrier((pieces, conv_kernel, conv_bias))
     filters = jnp.concatenate(
         [conv_kernel.reshape(layers, chans, TAPS * TAPS), conv_bias[:, :, None]], axis=2
     )
-    pieces = run_cut(field, seg, slot)
-    pieces, filters = lax.optimization_barrier((pieces, filters))
     shape = (peers, chans * tiles, LANES)
     around = ("zh", "zl", "xc")
     pieces = lax.all_to_all(pieces.reshape(shape), around, 0, 0, tiled=True).reshape(-1, LANES)
     filters = jnp.broadcast_to(filters.reshape(1, -1), (channels // chans, filters.size))
+    pieces, filters = lax.optimization_barrier((pieces, filters))
     filters = lax.all_to_all(filters, ("zl", "xc"), 0, 0, tiled=True)
     filters = filters.reshape(channels // chans, layers, chans, TAPS * TAPS + 1)
     filters = filters.transpose(1, 3, 0, 2).reshape(layers, TAPS * TAPS + 1, channels)
@@ -382,7 +384,7 @@
     cells = run_to_cells(pieces, halves * lats * slot, channels, tiles, 2 * REACH * slot)
     x, north, south = [part.reshape(-1, slot, channels) for part in cells]
     pieces = run_blocks(
-        edges, x, halo_of(x, north, south, seg), filters, mods,
+        edges, x, halo_of(x, north, south, filters, seg), mods,
         expand_weight, expand_bias, project_weight, project_bias, layer_scale, tiles,
     )
     pieces = lax.all_to_all(pieces.reshape(shape), around, 0, 0, tiled=True).reshape(-1, LANES)

time: 186 us -> 190 us (1.022)
  waiting for transfers between devices: 48 us -> 52 us
  starting transfers between devices: 31.9 us -> 29.9 us
    all_to_all x1, waiting for transfers between devices: 0.01 us -> 4.45 us  [on_device(): filters = lax.all_to_all(filters, ('zl', 'xc'), 0, 0, tiled=True)]
    ppermute x1, waiting for transfers between devices: 3.79 us -> 0.01 us  [halo_of(): bottom = lax.ppermute(north, 'y', up)]
    ppermute x1, waiting for transfers between devices: 1.11 us -> 3.97 us  [halo_of(): right = lax.ppermute(columns(0), 'xc', west)]
    ppermute x1, starting transfers between devices: 2.58 us -> 0.47 us  [halo_of(): left = lax.ppermute(columns(seg - reach), 'xc', east)]
    all_to_all x1, waiting for transfers between devices: 41.6 us -> 43.6 us  [on_device(): lax.all_to_all(pieces.reshape(shape), around, 0, 0, tiled=True)]
  transfers between devices with their start and end apart: 6 -> 6, of which waited for: 4 -> 3; matrix products, arithmetic and copies ran while one was open for 3% -> 4% of each run, Pallas kernels for 0% -> 1%
where the time goes in v4:
time: 190 us
  blocking collectives  58.3 us (31%)
  waiting for transfers between devices  52 us (27%)
  Pallas kernels  36.4 us (19%)
  starting transfers between devices  29.9 us (16%)
  local copies, waits for them, and re-layouts  7.45 us (4%)
  other arithmetic  3.7 us (2%)
    all_to_all x1, blocking collectives, on_device(): lax.all_to_all(pieces.reshape(shape), around, 0, 0, tiled=True)  58.3 us
    all_to_all x1, waiting for transfers between devices, on_device(): lax.all_to_all(pieces.reshape(shape), around, 0, 0, tiled=True)  43.6 us
    pallas_call x1, Pallas kernels, run_blocks(): pl.pallas_call(lambda *refs: blocks_kernel(*refs, tiles=tiles), out_shape...  26.2 us
    all_to_all x1, starting transfers between devices, on_device(): lax.all_to_all(pieces.reshape(shape), around, 0, 0, tiled=True)  19.4 us
    all_to_all x1, starting transfers between devices, on_device(): filters = lax.all_to_all(filters, ('zl', 'xc'), 0, 0, tiled=True)  5.48 us
    pallas_call x1, Pallas kernels, run_cut(): pl.pallas_call(lambda *refs: cut_kernel(*refs, seg=seg, slot=slot), out_s...  4.91 us
    all_to_all x1, waiting for transfers between devices, on_device(): filters = lax.all_to_all(filters, ('zl', 'xc'), 0, 0, tiled=True)  4.45 us
    pallas_call x1, Pallas kernels, run_paste(): pl.pallas_call(lambda *refs: paste_kernel(*refs, seg=seg, slot=slot), out...  4.3 us
  transfers between devices with their start and end apart: 6, of which 3 were waited for; matrix products, arithmetic and copies ran while one was open for 4% of the time, Pallas kernels for 1%

profile of v4, /device:TPU:33, one launch (start us, length us, event | category | flops | bytes accessed | tf_op | source)
XLA Modules:
  0.0 189.6 jit_solution(13723350538434805384)
XLA Ops:
  0.0 0.0 copy-start
  0.0 4.9 %cut.1 = bf16[3072,128]{1,0:T(8,128)(2,1)} custom-call(bf16[4,16,16,360]{3,2,1,0:T(8,128)(2,1)} %refs_0_.1), custom_call_target="tpu_custom_call" | custom-call | tf_op jit(solution)/shard_map/cut/pallas_call | solution.py:273
  4.9 0.0 copy-start.6
  4.9 19.4 %all-to-all-start = ((bf16[128,24,128]{2,1,0:T(8,128)(2,1)}), bf16[128,24,128]{2,1,0:T(8,128)(2,1)S(1)}, u32[]{:S(2)}, u32[]{:S(2)}) async-start(bf16[128,24,128]{2,1,0:T(8,128)(2,1)} %bitcast.2), calls=%async_computation | async-start | bytes 1572864 | tf_op jit(solution)/shard_map/all_to_all | solution.py:377
  24.4 0.0 copy-start.7
  24.4 0.7 copy-done.7
  25.0 0.1 copy.17
  25.1 0.0 copy-done.6
  25.2 0.1 reshape.37
  25.2 0.1 pad_maximum_fusion.2
  25.3 0.1 broadcast_in_dim.11
  25.4 43.6 %all-to-all-done = bf16[128,24,128]{2,1,0:T(8,128)(2,1)S(1)} async-done(((bf16[128,24,128]{2,1,0:T(8,128)(2,1)}), bf16[128,24,128]{2,1,0:T(8,128)(2,1)S(1)}, u32[]{:S(2)}, u32[]{:S(2)}) %all-to-all-start) | async-done | bytes 786464 | tf_op jit(solution)/shard_map/all_to_all | solution.py:377
  69.0 0.7 all_to_all.13
  69.7 5.5 %all-to-all-start.1 = ((f32[64,1,400]{2,1,0:T(1,128)}), f32[64,1,400]{2,1,0:T(1,128)S(1)}, u32[]{:S(2)}, u32[]{:S(2)}) async-start(f32[64,1,400]{2,1,0:T(1,128)} %all_to_all.13), calls=%async_computation.1 | async-start | bytes 262144 | tf_op jit(solution)/shard_map/all_to_all | solution.py:380
  75.2 0.0 copy-start.8
  75.2 0.6 copy-done.8
  75.9 0.6 dynamic_slice.6
  78.1 1.0 to_cells.1
  79.0 3.2 %collective-permute-start = (bf16[6,48,256]{2,1,0:T(8,128)(2,1)}, bf16[6,48,256]{2,1,0:T(8,128)(2,1)S(1)}, u32[]{:S(2)}, u32[]{:S(2)}) collective-permute-start(bf16[6,48,256]{2,1,0:T(8,128)(2,1)} %bitcast.6), channel_id=1, source_target_pairs={{0,128},{128,256},{256,384},{1,129},{129,257},{257,385},{2,130},{1... | collective-permute-start | bytes 442376 | tf_op jit(solution)/shard_map/ppermute | solution.py:336
  82.2 1.3 collective-permute-start.1
  83.5 0.7 fusion
  84.3 4.4 %all-to-all-done.1 = f32[64,1,400]{2,1,0:T(1,128)S(1)} async-done(((f32[64,1,400]{2,1,0:T(1,128)}), f32[64,1,400]{2,1,0:T(1,128)S(1)}, u32[]{:S(2)}, u32[]{:S(2)}) %all-to-all-start.1) | async-done | bytes 102432 | tf_op jit(solution)/shard_map/all_to_all | solution.py:380
  88.7 0.3 reduce
  89.0 0.0 copy-start.1
  89.0 0.0 copy-start.2
  89.1 1.0 reshape.41
  90.0 1.7 copy.18
  91.7 0.0 collective-permute-done.refs_2_
  91.7 0.0 collective-permute-done.1.refs_3_
  91.7 1.6 pad_maximum_fusion
  93.4 0.5 collective-permute-start.2
  93.8 1.6 pad_maximum_fusion.1
  95.4 0.0 collective-permute-start.3
  95.5 0.0 copy-done
  95.5 0.1 add_convert_fusion.refs_0_
  95.6 0.0 copy-start.3
  95.6 0.0 copy-start.4
  95.6 0.0 copy-start.5
  95.6 1.1 copy.19.refs_6_
  96.7 0.0 collective-permute-done.2.refs_4_
  96.7 4.0 %collective-permute-done.3.refs_5_ = bf16[44,6,256]{2,1,0:T(8,128)(2,1)} collective-permute-done((bf16[44,6,256]{2,1,0:T(8,128)(2,1)}, bf16[44,6,256]{2,1,0:T(8,128)(2,1)}, u32[]{:S(2)}, u32[]{:S(2)}) %collective-permute-start.3) | collective-permute-done | bytes 135200 | tf_op jit(solution)/shard_map/ppermute | solution.py:348
  100.7 0.0 copy-done.1
  100.7 0.0 copy-done.2
  100.7 0.0 copy-done.3
  100.7 0.0 copy-done.4
  100.7 0.0 copy-done.5
  100.7 26.2 %blocks.1 = bf16[3072,128]{1,0:T(8,128)(2,1)S(1)} custom-call(s32[2]{0:T(128)S(1)} %add_convert_fusion.refs_0_, bf16[32,48,256]{2,1,0:T(8,128)(2,1)S(1)} %bitcast.17, bf16[6,48,256]{2,1,0:T(8,128)(2,1)S(1)} %collective-permute-done.refs_2_, bf16[6,48,256]{2,1,0:T(8,128)(2,1)S(1)} %collective-permute-done.1.refs_3_, ...), custom_call_target="tpu_custom_call" | custom-call | tf_op jit(solution)/shard_map/blocks/pallas_call | solution.py:314
  126.9 58.3 %all_to_all.19 = bf16[128,24,128]{2,1,0:T(8,128)(2,1)S(1)} all-to-all(bf16[128,24,128]{2,1,0:T(8,128)(2,1)S(1)} %bitcast.13), channel_id=1, replica_groups=mesh['y'=4,'zh'=2,'zl'=8,'xc'=8] {'zh','zl','xc'}, dimensions={0} | all-to-all | bytes 1572864 | tf_op jit(solution)/shard_map/all_to_all | solution.py:390
  185.3 4.3 %paste.1 = bf16[4,16,16,360]{3,2,1,0:T(8,128)(2,1)} custom-call(bf16[3072,128]{1,0:T(8,128)(2,1)S(1)} %bitcast.15), custom_call_target="tpu_custom_call" | custom-call | tf_op jit(solution)/shard_map/paste/pallas_call | solution.py:286
  (5 shorter events, 0.1 us)
Async XLA Ops:
  0.0 95.5 %copy-start = (f32[2,20,2,256]{3,2,1,0:T(2,128)S(1)}, f32[2,20,2,256]{3,2,1,0:T(2,128)}, u32[]{:S(2)}) copy-start(f32[2,20,2,256]{3,2,1,0:T(2,128)} %param.14) | copy-start | bytes 245764
  4.9 20.2 %copy-start.6 = (f32[2,4,7,7]{3,1,2,0:T(4,128)S(1)}, f32[2,4,7,7]{3,1,2,0:T(4,128)}, u32[]{:S(2)}) copy-start(f32[2,4,7,7]{3,1,2,0:T(4,128)} %param.12) | copy-start | bytes 4708
  4.9 64.0 %all-to-all-start = ((bf16[128,24,128]{2,1,0:T(8,128)(2,1)}), bf16[128,24,128]{2,1,0:T(8,128)(2,1)S(1)}, u32[]{:S(2)}, u32[]{:S(2)}) async-start(bf16[128,24,128]{2,1,0:T(8,128)(2,1)} %bitcast.2), calls=%async_computation | async-start | bytes 1572864 | tf_op jit(solution)/shard_map/all_to_all | solution.py:377
  24.4 0.7 copy-start.7
  69.7 19.0 %all-to-all-start.1 = ((f32[64,1,400]{2,1,0:T(1,128)}), f32[64,1,400]{2,1,0:T(1,128)S(1)}, u32[]{:S(2)}, u32[]{:S(2)}) async-start(f32[64,1,400]{2,1,0:T(1,128)} %all_to_all.13), calls=%async_computation.1 | async-start | bytes 262144 | tf_op jit(solution)/shard_map/all_to_all | solution.py:380
  75.2 0.7 copy-start.8
  79.0 12.7 %collective-permute-start = (bf16[6,48,256]{2,1,0:T(8,128)(2,1)}, bf16[6,48,256]{2,1,0:T(8,128)(2,1)S(1)}, u32[]{:S(2)}, u32[]{:S(2)}) collective-permute-start(bf16[6,48,256]{2,1,0:T(8,128)(2,1)} %bitcast.6), channel_id=1, source_target_pairs={{0,128},{128,256},{256,384},{1,129},{129,257},{257,385},{2,130},{1... | collective-permute-start | bytes 442376 | tf_op jit(solution)/shard_map/ppermute | solution.py:336
  82.2 9.5 %collective-permute-start.1 = (bf16[6,48,256]{2,1,0:T(8,128)(2,1)S(1)}, bf16[6,48,256]{2,1,0:T(8,128)(2,1)S(1)}, u32[]{:S(2)}, u32[]{:S(2)}) collective-permute-start(bf16[6,48,256]{2,1,0:T(8,128)(2,1)S(1)} %bitcast.18), channel_id=1, source_target_pairs={{128,0},{256,128},{384,256},{129,1},{257,129},{385,257},{130,2},{2... | collective-permute-start | bytes 442376 | tf_op jit(solution)/shard_map/ppermute | solution.py:337
  89.0 11.7 %copy-start.1 = (bf16[2,256,1024]{2,1,0:T(8,128)(2,1)S(1)}, bf16[2,256,1024]{2,1,0:T(8,128)(2,1)}, u32[]{:S(2)}) copy-start(bf16[2,256,1024]{2,1,0:T(8,128)(2,1)} %refs_8_.1) | copy-start | bytes 3145732
  89.0 11.6 %copy-start.2 = (bf16[2,1024,256]{2,1,0:T(8,128)(2,1)S(1)}, bf16[2,1024,256]{2,1,0:T(8,128)(2,1)}, u32[]{:S(2)}) copy-start(bf16[2,1024,256]{2,1,0:T(8,128)(2,1)} %refs_10_.1) | copy-start | bytes 3145732
  93.4 3.4 %collective-permute-start.2 = (bf16[44,6,256]{2,1,0:T(8,128)(2,1)}, bf16[44,6,256]{2,1,0:T(8,128)(2,1)}, u32[]{:S(2)}, u32[]{:S(2)}) collective-permute-start(bf16[44,6,256]{2,1,0:T(8,128)(2,1)} %pad_maximum_fusion), channel_id=1, source_target_pairs={{0,1},{1,2},{2,3},{3,4},{4,5},{5,6},{6,7},{7,0},{8,9},{9,10},{10,1... | collective-permute-start | bytes 405512 | tf_op jit(solution)/shard_map/ppermute | solution.py:347
  95.4 5.2 %collective-permute-start.3 = (bf16[44,6,256]{2,1,0:T(8,128)(2,1)}, bf16[44,6,256]{2,1,0:T(8,128)(2,1)}, u32[]{:S(2)}, u32[]{:S(2)}) collective-permute-start(bf16[44,6,256]{2,1,0:T(8,128)(2,1)} %pad_maximum_fusion.1), channel_id=1, source_target_pairs={{1,0},{2,1},{3,2},{4,3},{5,4},{6,5},{7,6},{0,7},{9,8},{10,9},{11,1... | collective-permute-start | bytes 405512 | tf_op jit(solution)/shard_map/ppermute | solution.py:348
  95.6 5.1 %copy-start.3 = (f32[2,1024]{1,0:T(2,128)S(1)}, f32[2,1024]{1,0:T(2,128)}, u32[]{:S(2)}) copy-start(f32[2,1024]{1,0:T(2,128)} %refs_9_.1) | copy-start | bytes 24580
  95.6 5.1 %copy-start.4 = (f32[2,256]{1,0:T(2,128)S(1)}, f32[2,256]{1,0:T(2,128)}, u32[]{:S(2)}) copy-start(f32[2,256]{1,0:T(2,128)} %refs_11_.1) | copy-start | bytes 6148
  95.6 5.1 %copy-start.5 = (f32[2,256]{1,0:T(2,128)S(1)}, f32[2,256]{1,0:T(2,128)}, u32[]{:S(2)}) copy-start(f32[2,256]{1,0:T(2,128)} %refs_12_.1) | copy-start | bytes 6148

commit v5 on v3

--- a/solution.py
+++ b/solution.py
@@ -11,6 +11,8 @@
 REACH = 3
 LEFT = 8
 ROWS = 8
+HALF_LANES = 64
+TAP_ROWS = 56
 
 
 def lane_iota(rows):
@@ -46,12 +48,18 @@
     return spans
 
 
-def cut_kernel(field_ref, out_ref, wide, cut, *, seg, slot):
+def cut_kernel(field_ref, filter_ref, out_ref, wide, cut, *, seg, slot):
     chans, members, lats, lons = field_ref.shape
     rows = chans * members
     parts = -(-lons // LANES)
     segs = lons // seg
     tiles = lats * slot // LANES
+    extra = filter_ref.shape[0]
+    piece_rows = chans * tiles + extra
+    for e in range(extra):
+        cut[pl.ds(chans * tiles + e, members * segs, stride=piece_rows), :] = jnp.broadcast_to(
+            filter_ref[e : e + 1, :], (members * segs, LANES)
+        )
     for a in range(parts):
         lo, hi = a * LANES, min((a + 1) * LANES, lons)
         piece = field_ref[:, :, :, lo:hi].astype(jnp.float32).reshape(rows * lats, hi - lo)
@@ -68,8 +76,8 @@
 
             tile = moved_lanes(load, spans, rows, rolled)
             for c in range(chans):
-                start = s * chans * tiles + c * tiles + t
-                cut[pl.ds(start, members, stride=segs * chans * tiles), :] = tile[
+                start = s * piece_rows + c * tiles + t
+                cut[pl.ds(start, members, stride=segs * piece_rows), :] = tile[
                     c * members : (c + 1) * members
                 ]
     out_ref[...] = cut[...].astype(jnp.bfloat16)
@@ -111,10 +119,19 @@
         )
 
 
-def to_cells_kernel(in_ref, out_ref, north_ref, south_ref, rows32, *, tiles):
+def to_cells_kernel(
+    in_ref, out_ref, north_ref, south_ref, taps_ref, raw, rows32, *, tiles, sources
+):
     cells, channels = out_ref.shape
-    halves = in_ref.shape[0] // (channels * tiles)
-    rows32[...] = in_ref[...].astype(jnp.float32)
+    halves = taps_ref.shape[0]
+    data = rows32.shape[0]
+    piece_rows = in_ref.shape[0] // sources
+    data_rows = data // sources
+    raw[...] = in_ref[...].astype(jnp.float32)
+    for src in range(sources):
+        rows32[src * data_rows : (src + 1) * data_rows, :] = raw[
+            src * piece_rows : src * piece_rows + data_rows, :
+        ]
     for half in range(halves):
         for t in range(tiles):
             block = rows32[pl.ds(half * channels * tiles + t, channels, stride=tiles), :]
@@ -123,6 +140,23 @@
     edge = north_ref.shape[0]
     north_ref[...] = out_ref[0:edge, :]
     south_ref[...] = out_ref[cells - edge :, :]
+    owners = sources // halves
+    chans = channels // owners
+    taps = taps_ref.shape[1]
+    owner = lax.broadcasted_iota(jnp.int32, (owners, channels), 0)
+    channel = lax.broadcasted_iota(jnp.int32, (owners, channels), 1)
+    for half in range(halves):
+        total = jnp.zeros((taps, channels), jnp.float32)
+        for e in range(piece_rows - data_rows):
+            start = half * owners * piece_rows + data_rows + e
+            lines = raw[pl.ds(start, owners, stride=piece_rows), :].T.astype(jnp.bfloat16)
+            for k in range(2):
+                place = (channel == owner * chans + 2 * e + k).astype(jnp.float32)
+                spread = jnp.dot(
+                    lines, place.astype(jnp.bfloat16), preferred_element_type=jnp.float32
+                )
+                total = total + spread[k * HALF_LANES : k * HALF_LANES + taps, :]
+        taps_ref[half] = total
 
 
 def depthwise(source, spread, mixed, layer, lats, rows, col_tiles, first_col):
@@ -178,9 +212,9 @@
             jnp.dot(normed, up_ref[layer], preferred_element_type=jnp.float32)
             + up_bias_ref[layer : layer + 1, :]
         )
-        active = (0.5 * hidden * (1.0 + lax.erf(hidden * 0.7071067811865476))).astype(jnp.bfloat16)
+        doubled = (hidden * (1.0 + lax.erf(hidden * 0.7071067811865476))).astype(jnp.bfloat16)
         result = (
-            jnp.dot(active, down_ref[layer], preferred_element_type=jnp.float32)
+            0.5 * jnp.dot(doubled, down_ref[layer], preferred_element_type=jnp.float32)
             + down_bias_ref[layer : layer + 1, :]
         )
         branch = (scale_ref[layer : layer + 1, :] * result).astype(jnp.bfloat16).astype(jnp.float32)
@@ -266,10 +300,10 @@
     return pltpu.with_memory_space_constraint(x, pltpu.VMEM)
 
 
-def run_cut(field, seg, slot):
+def run_cut(field, filters, seg, slot):
     chans, members, lats, lons = field.shape
     tiles = lats * slot // LANES
-    rows = members * (lons // seg) * chans * tiles
+    rows = members * (lons // seg) * (chans * tiles + filters.shape[0])
     return pl.pallas_call(
         lambda *refs: cut_kernel(*refs, seg=seg, slot=slot),
         out_shape=pltpu.VMEM((rows, LANES), jnp.bfloat16),
@@ -278,7 +312,7 @@
             pltpu.VMEM((rows, LANES), jnp.float32),
         ],
         name="cut",
-    )(field)
+    )(field, filters)
 
 
 def run_paste(pieces, shape, seg, slot):
@@ -294,12 +328,16 @@
     )(near(pieces))
 
 
-def run_to_cells(pieces, cells, channels, tiles, edge):
+def run_to_cells(pieces, cells, channels, tiles, edge, sources, layers):
     outs = [(cells, channels), (edge, channels), (edge, channels)]
     return pl.pallas_call(
-        lambda *refs: to_cells_kernel(*refs, tiles=tiles),
-        out_shape=[pltpu.VMEM(out, jnp.bfloat16) for out in outs],
-        scratch_shapes=[pltpu.VMEM(pieces.shape, jnp.float32)],
+        lambda *refs: to_cells_kernel(*refs, tiles=tiles, sources=sources),
+        out_shape=[pltpu.VMEM(out, jnp.bfloat16) for out in outs]
+        + [pltpu.VMEM((layers, TAP_ROWS, channels), jnp.float32)],
+        scratch_shapes=[
+            pltpu.VMEM(pieces.shape, jnp.float32),
+            pltpu.VMEM((cells * channels // LANES, LANES), jnp.float32),
+        ],
         name="to_cells",
     )(near(pieces))
 
@@ -366,21 +404,26 @@
     band = lax.axis_index("y")
     edges = jnp.stack([band == 0, band == lax.axis_size("y") - 1]).astype(jnp.int32)
 
+    layer = lax.axis_index("zh")
     filters = jnp.concatenate(
-        [conv_kernel.reshape(layers, chans, TAPS * TAPS), conv_bias[:, :, None]], axis=2
-    )
-    pieces = run_cut(field, seg, slot)
-    pieces, filters = lax.optimization_barrier((pieces, filters))
+        [
+            conv_kernel.reshape(layers, chans, TAPS * TAPS),
+            conv_bias[:, :, None],
+            jnp.zeros((layers, chans, HALF_LANES - TAPS * TAPS - 1), jnp.float32),
+        ],
+        axis=2,
+    )
+    filters = lax.dynamic_index_in_dim(filters, layer, 0, False).reshape(-1, LANES)
+    pieces = run_cut(field, filters, seg, slot)
+    around = ("zh", "zl", "xc")
+    pairs = pieces.reshape(peers, -1, 2, LANES)
+    pieces = lax.all_to_all(pairs, around, 0, 0, tiled=True).reshape(-1, LANES)
     shape = (peers, chans * tiles, LANES)
-    around = ("zh", "zl", "xc")
-    pieces = lax.all_to_all(pieces.reshape(shape), around, 0, 0, tiled=True).reshape(-1, LANES)
-    filters = jnp.broadcast_to(filters.reshape(1, -1), (channels // chans, filters.size))
-    filters = lax.all_to_all(filters, ("zl", "xc"), 0, 0, tiled=True)
-    filters = filters.reshape(channels // chans, layers, chans, TAPS * TAPS + 1)
-    filters = filters.transpose(1, 3, 0, 2).reshape(layers, TAPS * TAPS + 1, channels)
-
-    cells = run_to_cells(pieces, halves * lats * slot, channels, tiles, 2 * REACH * slot)
-    x, north, south = [part.reshape(-1, slot, channels) for part in cells]
+    cells = run_to_cells(
+        pieces, halves * lats * slot, channels, tiles, 2 * REACH * slot, peers, layers
+    )
+    x, north, south = [part.reshape(-1, slot, channels) for part in cells[:3]]
+    filters = cells[3]
     pieces = run_blocks(
         edges, x, halo_of(x, north, south, seg), filters, mods,
         expand_weight, expand_bias, project_weight, project_bias, layer_scale, tiles,

time: 186 us -> 175 us (0.941)
  starting transfers between devices: 31.9 us -> 25.1 us
  waiting for transfers between devices: 48 us -> 54.3 us
  blocking collectives: 58.1 us -> 53.5 us
  other arithmetic: 2.58 us -> 0.25 us
    all_to_all x2 -> x1, starting transfers between devices: 24.8 us -> 19.3 us  [on_device(): pieces = lax.all_to_all(pairs, around, 0, 0, tiled=True).reshape(-1, LANES)]
    all_to_all x1, blocking collectives: 58.1 us -> 53.5 us  [on_device(): lax.all_to_all(pieces.reshape(shape), around, 0, 0, tiled=True)]
    all_to_all x2 -> x1, waiting for transfers between devices: 41.6 us -> 44.2 us  [on_device(): pieces = lax.all_to_all(pairs, around, 0, 0, tiled=True).reshape(-1, LANES)]
    ppermute x1, starting transfers between devices: 2.58 us -> 0.41 us  [halo_of(): left = lax.ppermute(columns(seg - reach), 'xc', east)]
  transfers between devices with their start and end apart: 6 -> 5, of which waited for: 4 -> 5; matrix products, arithmetic and copies ran while one was open for 3% -> 0% of each run, Pallas kernels for 0% -> 0%
where the time goes in v5:
time: 175 us
  waiting for transfers between devices  54.3 us (31%)
  blocking collectives  53.5 us (31%)
  Pallas kernels  34.9 us (20%)
  starting transfers between devices  25.1 us (14%)
  local copies, waits for them, and re-layouts  4.93 us (3%)
  between operations  2.08 us (1%)
    all_to_all x1, blocking collectives, on_device(): lax.all_to_all(pieces.reshape(shape), around, 0, 0, tiled=True)  53.5 us
    all_to_all x1, waiting for transfers between devices, on_device(): pieces = lax.all_to_all(pairs, around, 0, 0, tiled=True).reshape(-1, LANES)  44.2 us
    pallas_call x1, Pallas kernels, run_blocks(): pl.pallas_call(lambda *refs: blocks_kernel(*refs, tiles=tiles), out_shape...  25.8 us
    all_to_all x1, starting transfers between devices, on_device(): pieces = lax.all_to_all(pairs, around, 0, 0, tiled=True).reshape(-1, LANES)  19.3 us
    pallas_call x1, Pallas kernels, run_paste(): pl.pallas_call(lambda *refs: paste_kernel(*refs, seg=seg, slot=slot), out...  4.3 us
    pallas_call x1, Pallas kernels, run_cut(): pl.pallas_call(lambda *refs: cut_kernel(*refs, seg=seg, slot=slot), out_s...  4.23 us
    ppermute x1, waiting for transfers between devices, halo_of(): bottom = lax.ppermute(north, 'y', up)  3.78 us
  transfers between devices with their start and end apart: 5, of which 5 were waited for; matrix products, arithmetic and copies ran while one was open for 0% of the time, Pallas kernels for 0%

profile of v5, /device:TPU:33, one launch (start us, length us, event | category | flops | bytes accessed | tf_op | source)
XLA Modules:
  0.0 175.0 jit_solution(392072876018420843)
XLA Ops:
  0.0 0.0 copy-start
  0.0 0.0 copy-start.6
  0.0 0.7 copy-done.6
  0.7 0.1 copy.13
  0.8 0.8 copy.12
  1.6 0.1 reshape.28
  1.7 0.1 pad.8.clone
  1.7 0.1 fusion.1
  1.8 0.6 reshape.29.refs_1_
  2.5 4.2 %cut.1 = bf16[3328,128]{1,0:T(8,128)(2,1)} custom-call(bf16[4,16,16,360]{3,2,1,0:T(8,128)(2,1)} %refs_0_.1, f32[2,128]{1,0:T(2,128)} %reshape.29.refs_1_), custom_call_target="tpu_custom_call" | custom-call | tf_op jit(solution)/shard_map/cut/pallas_call | solution.py:307
  6.7 19.3 %all-to-all-start = ((bf16[128,13,2,128]{3,2,1,0:T(2,128)(2,1)}), bf16[128,13,2,128]{3,2,1,0:T(2,128)(2,1)S(1)}, u32[]{:S(2)}, u32[]{:S(2)}) async-start(bf16[128,13,2,128]{3,2,1,0:T(2,128)(2,1)} %bitcast.3), calls=%async_computation | async-start | bytes 1703936 | tf_op jit(solution)/shard_map/all_to_all | solution.py:420
  26.0 0.0 copy-start.7
  26.0 0.6 copy-done.7
  26.7 0.6 dynamic_slice.11
  29.2 44.2 %all-to-all-done = bf16[128,13,2,128]{3,2,1,0:T(2,128)(2,1)S(1)} async-done(((bf16[128,13,2,128]{3,2,1,0:T(2,128)(2,1)}), bf16[128,13,2,128]{3,2,1,0:T(2,128)(2,1)S(1)}, u32[]{:S(2)}, u32[]{:S(2)}) %all-to-all-start) | async-done | bytes 852000 | tf_op jit(solution)/shard_map/all_to_all | solution.py:420
  73.4 0.6 to_cells.1
  74.0 0.0 copy-start.1
  74.0 3.3 %collective-permute-start = (bf16[6,48,256]{2,1,0:T(8,128)(2,1)S(1)}, bf16[6,48,256]{2,1,0:T(8,128)(2,1)S(1)}, u32[]{:S(2)}, u32[]{:S(2)}) collective-permute-start(bf16[6,48,256]{2,1,0:T(8,128)(2,1)S(1)} %bitcast.17), channel_id=1, source_target_pairs={{0,128},{128,256},{256,384},{1,129},{129,257},{257,385},{2,130},{1... | collective-permute-start | bytes 442376 | tf_op jit(solution)/shard_map/ppermute | solution.py:374
  77.3 1.3 collective-permute-start.1
  78.7 1.9 %collective-permute-done.refs_2_ = bf16[6,48,256]{2,1,0:T(8,128)(2,1)S(1)} collective-permute-done((bf16[6,48,256]{2,1,0:T(8,128)(2,1)S(1)}, bf16[6,48,256]{2,1,0:T(8,128)(2,1)S(1)}, u32[]{:S(2)}, u32[]{:S(2)}) %collective-permute-start) | collective-permute-done | bytes 147488 | tf_op jit(solution)/shard_map/ppermute | solution.py:374
  80.6 3.8 %collective-permute-done.1.refs_3_ = bf16[6,48,256]{2,1,0:T(8,128)(2,1)S(1)} collective-permute-done((bf16[6,48,256]{2,1,0:T(8,128)(2,1)S(1)}, bf16[6,48,256]{2,1,0:T(8,128)(2,1)S(1)}, u32[]{:S(2)}, u32[]{:S(2)}) %collective-permute-start.1) | collective-permute-done | bytes 147488 | tf_op jit(solution)/shard_map/ppermute | solution.py:375
  84.5 0.4 collective-permute-start.2
  84.9 0.7 collective-permute-start.3
  85.6 0.0 copy-done
  85.6 0.0 copy-start.3
  85.7 0.0 copy-start.5
  85.7 0.0 copy-start.4
  85.7 0.1 add_convert_fusion.refs_0_
  85.8 1.6 collective-permute-done.2.refs_4_
  87.3 2.8 %collective-permute-done.3.refs_5_ = bf16[44,6,256]{2,1,0:T(8,128)(2,1)S(1)} collective-permute-done((bf16[44,6,256]{2,1,0:T(8,128)(2,1)S(1)}, bf16[44,6,256]{2,1,0:T(8,128)(2,1)S(1)}, u32[]{:S(2)}, u32[]{:S(2)}) %collective-permute-start.3) | collective-permute-done | bytes 135200 | tf_op jit(solution)/shard_map/ppermute | solution.py:385
  90.1 0.0 copy-done.1
  90.2 0.0 copy-done.3
  90.2 0.0 copy-done.5
  90.2 0.0 copy-done.4
  90.2 0.0 copy-start.2
  90.2 1.2 copy-done.2
  91.4 25.8 %blocks.1 = bf16[3072,128]{1,0:T(8,128)(2,1)S(1)} custom-call(s32[2]{0:T(128)S(1)} %add_convert_fusion.refs_0_, bf16[32,48,256]{2,1,0:T(8,128)(2,1)S(1)} %bitcast.15, bf16[6,48,256]{2,1,0:T(8,128)(2,1)S(1)} %collective-permute-done.refs_2_, bf16[6,48,256]{2,1,0:T(8,128)(2,1)S(1)} %collective-permute-done.1.refs_3_, ...), custom_call_target="tpu_custom_call" | custom-call | tf_op jit(solution)/shard_map/blocks/pallas_call | solution.py:352
  117.2 53.5 %all_to_all.10 = bf16[128,24,128]{2,1,0:T(8,128)(2,1)S(1)} all-to-all(bf16[128,24,128]{2,1,0:T(8,128)(2,1)S(1)} %bitcast.12), channel_id=1, replica_groups=mesh['y'=4,'zh'=2,'zl'=8,'xc'=8] {'zh','zl','xc'}, dimensions={0} | all-to-all | bytes 1572864 | tf_op jit(solution)/shard_map/all_to_all | solution.py:431
  170.7 4.3 %paste.1 = bf16[4,16,16,360]{3,2,1,0:T(8,128)(2,1)} custom-call(bf16[3072,128]{1,0:T(8,128)(2,1)S(1)} %bitcast.13), custom_call_target="tpu_custom_call" | custom-call | tf_op jit(solution)/shard_map/paste/pallas_call | solution.py:320
  (8 shorter events, 0.2 us)
Async XLA Ops:
  0.0 85.6 %copy-start = (f32[2,20,2,256]{3,2,1,0:T(2,128)S(1)}, f32[2,20,2,256]{3,2,1,0:T(2,128)}, u32[]{:S(2)}) copy-start(f32[2,20,2,256]{3,2,1,0:T(2,128)} %param.14) | copy-start | bytes 245764
  0.0 0.7 copy-start.6
  6.7 66.7 %all-to-all-start = ((bf16[128,13,2,128]{3,2,1,0:T(2,128)(2,1)}), bf16[128,13,2,128]{3,2,1,0:T(2,128)(2,1)S(1)}, u32[]{:S(2)}, u32[]{:S(2)}) async-start(bf16[128,13,2,128]{3,2,1,0:T(2,128)(2,1)} %bitcast.3), calls=%async_computation | async-start | bytes 1703936 | tf_op jit(solution)/shard_map/all_to_all | solution.py:420
  26.0 0.7 copy-start.7
  74.0 16.2 %copy-start.1 = (bf16[2,256,1024]{2,1,0:T(8,128)(2,1)S(1)}, bf16[2,256,1024]{2,1,0:T(8,128)(2,1)}, u32[]{:S(2)}) copy-start(bf16[2,256,1024]{2,1,0:T(8,128)(2,1)} %refs_8_.1) | copy-start | bytes 3145732
  74.0 6.6 %collective-permute-start = (bf16[6,48,256]{2,1,0:T(8,128)(2,1)S(1)}, bf16[6,48,256]{2,1,0:T(8,128)(2,1)S(1)}, u32[]{:S(2)}, u32[]{:S(2)}) collective-permute-start(bf16[6,48,256]{2,1,0:T(8,128)(2,1)S(1)} %bitcast.17), channel_id=1, source_target_pairs={{0,128},{128,256},{256,384},{1,129},{129,257},{257,385},{2,130},{1... | collective-permute-start | bytes 442376 | tf_op jit(solution)/shard_map/ppermute | solution.py:374
  77.3 7.1 %collective-permute-start.1 = (bf16[6,48,256]{2,1,0:T(8,128)(2,1)S(1)}, bf16[6,48,256]{2,1,0:T(8,128)(2,1)S(1)}, u32[]{:S(2)}, u32[]{:S(2)}) collective-permute-start(bf16[6,48,256]{2,1,0:T(8,128)(2,1)S(1)} %bitcast.16), channel_id=1, source_target_pairs={{128,0},{256,128},{384,256},{129,1},{257,129},{385,257},{130,2},{2... | collective-permute-start | bytes 442376 | tf_op jit(solution)/shard_map/ppermute | solution.py:375
  84.5 2.8 %collective-permute-start.2 = (bf16[44,6,256]{2,1,0:T(8,128)(2,1)S(1)}, bf16[44,6,256]{2,1,0:T(8,128)(2,1)S(1)}, u32[]{:S(2)}, u32[]{:S(2)}) collective-permute-start(bf16[44,6,256]{2,1,0:T(8,128)(2,1)S(1)} %pad_maximum_fusion), channel_id=1, source_target_pairs={{0,1},{1,2},{2,3},{3,4},{4,5},{5,6},{6,7},{7,0},{8,9},{9,10},{10,1... | collective-permute-start | bytes 405512 | tf_op jit(solution)/shard_map/ppermute | solution.py:384
  84.9 5.2 %collective-permute-start.3 = (bf16[44,6,256]{2,1,0:T(8,128)(2,1)S(1)}, bf16[44,6,256]{2,1,0:T(8,128)(2,1)S(1)}, u32[]{:S(2)}, u32[]{:S(2)}) collective-permute-start(bf16[44,6,256]{2,1,0:T(8,128)(2,1)S(1)} %pad_maximum_fusion.1), channel_id=1, source_target_pairs={{1,0},{2,1},{3,2},{4,3},{5,4},{6,5},{7,6},{0,7},{9,8},{10,9},{11,1... | collective-permute-start | bytes 405512 | tf_op jit(solution)/shard_map/ppermute | solution.py:385
  85.6 4.5 %copy-start.3 = (f32[2,1024]{1,0:T(2,128)S(1)}, f32[2,1024]{1,0:T(2,128)}, u32[]{:S(2)}) copy-start(f32[2,1024]{1,0:T(2,128)} %refs_9_.1) | copy-start | bytes 24580
  85.7 4.5 %copy-start.5 = (f32[2,256]{1,0:T(2,128)S(1)}, f32[2,256]{1,0:T(2,128)}, u32[]{:S(2)}) copy-start(f32[2,256]{1,0:T(2,128)} %refs_12_.1) | copy-start | bytes 6148
  85.7 4.5 %copy-start.4 = (f32[2,256]{1,0:T(2,128)S(1)}, f32[2,256]{1,0:T(2,128)}, u32[]{:S(2)}) copy-start(f32[2,256]{1,0:T(2,128)} %refs_11_.1) | copy-start | bytes 6148
  90.2 1.2 copy-start.2

commit v6 on v5

--- a/solution.py
+++ b/solution.py
@@ -159,31 +159,63 @@
         taps_ref[half] = total
 
 
-def depthwise(source, spread, mixed, layer, lats, rows, col_tiles, first_col):
-    groups = source.shape[0]
-    steps = -(-lats // rows)
-    for k in range(col_tiles):
-
-        def step_of(step, carry):
-            g = step // steps
-            row = jnp.minimum((step % steps) * rows, lats - rows)
+def depthwise(source, spread, mixed, layer, bands, tiles, first_col):
+    packed = mixed.shape[1] == sum(count for _, count in bands)
+    for k in tiles:
+
+        def step_of(g, carry):
             def column_of(j, sums):
                 sums = list(sums)
                 weights = [spread[layer, g, i * TAPS + j] for i in range(TAPS)]
-                for r in range(rows + TAPS - 1):
-                    value = source[g, row + r, pl.ds(first_col + 8 * k + j, 8), :]
-                    for i in range(TAPS):
-                        if 0 <= r - i < rows:
-                            sums[r - i] = sums[r - i] + weights[i] * value
+                at = 0
+                for start, count in bands:
+                    for r in range(count + TAPS - 1):
+                        value = source[g, start + r, pl.ds(first_col + 8 * k + j, 8), :]
+                        for i in range(TAPS):
+                            if 0 <= r - i < count:
+                                sums[at + r - i] = sums[at + r - i] + weights[i] * value
+                    at += count
                 return tuple(sums)
 
-            start = (spread[layer, g, TAPS * TAPS],) * rows
-            sums = lax.fori_loop(0, TAPS, column_of, start)
-            for r in range(rows):
-                mixed[g, row + r, 8 * k : 8 * k + 8, :] = sums[r]
+            total = sum(count for _, count in bands)
+            sums = lax.fori_loop(0, TAPS, column_of, (spread[layer, g, TAPS * TAPS],) * total)
+            at = 0
+            for start, count in bands:
+                for r in range(count):
+                    row = at if packed else start + r
+                    mixed[g, row, 8 * k : 8 * k + 8, :] = sums[at]
+                    at += 1
             return carry
 
-        lax.fori_loop(0, groups * steps, step_of, 0)
+        lax.fori_loop(0, source.shape[0], step_of, 0)
+
+
+def spread_taps(spread, taps_ref, layers):
+    for g in range(spread.shape[1]):
+        ch = slice(g * LANES, (g + 1) * LANES)
+        for layer in range(layers):
+            for k in range(TAPS * TAPS + 1):
+                spread[layer, g, k] = jnp.broadcast_to(taps_ref[layer, k : k + 1, ch], (8, LANES))
+
+
+def middle_kernel(*refs, bands, tiles):
+    *part_refs, taps_ref, out_ref, source, spread = refs
+    for g in range(source.shape[0]):
+        row = 0
+        for part_ref, lo, hi in part_refs_of(part_refs, source.shape[1]):
+            ch = slice(g * LANES, (g + 1) * LANES)
+            source[g, row : row + hi - lo, :, :] = part_ref[lo:hi, :, ch].astype(jnp.float32)
+            row += hi - lo
+    spread_taps(spread, taps_ref, 1)
+    depthwise(source, spread, out_ref, 0, bands, range(tiles), 8 - 2 * REACH)
+
+
+def part_refs_of(part_refs, rows):
+    if len(part_refs) == 1:
+        return [(part_refs[0], 0, rows)]
+    top_ref, x_ref, bottom_ref = part_refs
+    edge, lats = top_ref.shape[0], x_ref.shape[0]
+    return [(top_ref, 0, edge), (x_ref, 0, edge), (x_ref, lats - edge, lats), (bottom_ref, 0, edge)]
 
 
 def pointwise(mixed, layer, lats, slot, residual, store, weights):
@@ -227,15 +259,21 @@
 
 
 def blocks_kernel(
-    edge_ref, x_ref, top_ref, bottom_ref, left_ref, right_ref, taps_ref, mod_ref,
-    up_ref, up_bias_ref, down_ref, down_bias_ref, scale_ref,
-    out_ref, first, second, spread, mixed, final, rows32, *, tiles,
+    edge_ref, x_ref, top_ref, bottom_ref, left_ref, right_ref, taps_ref, inner_ref, outer_ref, mod_ref,
+    up_bias_ref, down_bias_ref, scale_ref, up_hbm, down_hbm,
+    out_ref, first, second, spread, mixed, final, rows32, up_ref, down_ref, arrived, *, tiles,
 ):
     lats, slot, channels = x_ref.shape
     groups = channels // LANES
     reach = 2 * REACH
     wide = lats + reach
     right_at = LEFT + slot - REACH
+    copies = [
+        pltpu.make_async_copy(up_hbm, up_ref, arrived.at[0]),
+        pltpu.make_async_copy(down_hbm, down_ref, arrived.at[1]),
+    ]
+    for copy in copies:
+        copy.start()
     for g in range(groups):
         ch = slice(g * LANES, (g + 1) * LANES)
         first[g, 0:reach, LEFT : LEFT + slot, :] = top_ref[:, :, ch].astype(jnp.float32)
@@ -246,13 +284,21 @@
         )
         first[g, :, LEFT - reach : LEFT, :] = left_ref[:, :, ch].astype(jnp.float32)
         first[g, :, right_at : right_at + reach, :] = right_ref[:, :, ch].astype(jnp.float32)
-        for layer in range(taps_ref.shape[0]):
-            for k in range(TAPS * TAPS + 1):
-                spread[layer, g, k] = jnp.broadcast_to(taps_ref[layer, k : k + 1, ch], (8, LANES))
+        middle = slice(8, 8 + inner_ref.shape[2])
+        mixed[g, 0:reach, middle, :] = outer_ref[g, 0:reach]
+        mixed[g, reach:lats, middle, :] = inner_ref[g]
+        mixed[g, lats:wide, middle, :] = outer_ref[g, reach:]
+    spread_taps(spread, taps_ref, taps_ref.shape[0])
     weights = (mod_ref, up_ref, up_bias_ref, down_ref, down_bias_ref, scale_ref)
 
     wide_slot = slot + 8
-    depthwise(first, spread, mixed, 0, wide, 19, wide_slot // 8, LEFT - reach)
+    covered = inner_ref.shape[2] // 8
+    sides = [k for k in range(wide_slot // 8) if not 1 <= k <= covered]
+    depthwise(first, spread, mixed, 0, [(0, wide // 2)], sides, LEFT - reach)
+    depthwise(first, spread, mixed, 0, [(wide // 2, wide - wide // 2)], sides, LEFT - reach)
+
+    for copy in copies:
+        copy.wait()
 
     def first_store(g, row, value):
         second[g, pl.ds(row, ROWS), :, :] = value
@@ -271,7 +317,7 @@
     def _():
         second[:, REACH + lats :, :, :] = jnp.zeros((groups, REACH, wide_slot, LANES), jnp.float32)
 
-    depthwise(second, spread, mixed, 1, lats, 32, slot // 8, 0)
+    depthwise(second, spread, mixed, 1, [(0, lats)], range(slot // 8), 0)
 
     def final_store(g, row, value):
         final[g, pl.ds(row, ROWS), :, :] = value
@@ -300,6 +346,10 @@
     return pltpu.with_memory_space_constraint(x, pltpu.VMEM)
 
 
+def far(x):
+    return pltpu.with_memory_space_constraint(x, pltpu.HBM)
+
+
 def run_cut(field, filters, seg, slot):
     chans, members, lats, lons = field.shape
     tiles = lats * slot // LANES
@@ -342,37 +392,59 @@
     )(near(pieces))
 
 
-def run_blocks(edges, x, halos, taps, mods, up, up_bias, down, down_bias, scale, tiles):
+def run_middle(parts, taps, rows, bands, cols):
+    slot, channels = parts[0].shape[1:]
+    groups = channels // LANES
+    total = sum(count for _, count in bands)
+    return pl.pallas_call(
+        lambda *refs: middle_kernel(*refs, bands=bands, tiles=cols // 8),
+        out_shape=pltpu.VMEM((groups, total, cols, LANES), jnp.float32),
+        scratch_shapes=[
+            pltpu.VMEM((groups, rows, slot, LANES), jnp.float32),
+            pltpu.VMEM((1, groups, TAPS * TAPS + 1, 8, LANES), jnp.float32),
+        ],
+        compiler_params=pltpu.CompilerParams(vmem_limit_bytes=16 * 2**20),
+        name="middle",
+    )(*[near(part) for part in parts], near(taps))
+
+
+def run_blocks(edges, x, halos, taps, middles, mods, up, up_bias, down, down_bias, scale, tiles):
     lats, slot, channels = x.shape
     groups = channels // LANES
     rows = lats * slot * channels // LANES
     vmem = pl.BlockSpec(memory_space=pltpu.VMEM)
-    arrays = (x, *halos, taps, mods, up, up_bias, down, down_bias, scale)
+    arrays = (x, *halos, taps, *middles, mods, up_bias, down_bias, scale)
     wide_slot = slot + 8
     return pl.pallas_call(
         lambda *refs: blocks_kernel(*refs, tiles=tiles),
         out_shape=pltpu.VMEM((rows, LANES), jnp.bfloat16),
-        in_specs=[pl.BlockSpec(memory_space=pltpu.SMEM)] + [vmem] * len(arrays),
+        in_specs=[pl.BlockSpec(memory_space=pltpu.SMEM)]
+        + [vmem] * len(arrays)
+        + [pl.BlockSpec(memory_space=pltpu.HBM)] * 2,
         scratch_shapes=[
             pltpu.VMEM((groups, lats + 4 * REACH, LEFT + wide_slot, LANES), jnp.float32),
             pltpu.VMEM((groups, lats + 2 * REACH, wide_slot, LANES), jnp.float32),
-            pltpu.VMEM((taps.shape[0], groups, TAPS * TAPS + 1, 8, LANES), jnp.float32),
+            pltpu.VMEM((up.shape[0], groups, TAPS * TAPS + 1, 8, LANES), jnp.float32),
             pltpu.VMEM((groups, lats + 2 * REACH, wide_slot, LANES), jnp.float32),
             pltpu.VMEM((groups, lats, slot, LANES), jnp.float32),
             pltpu.VMEM((rows, LANES), jnp.float32),
+            pltpu.VMEM(up.shape, up.dtype),
+            pltpu.VMEM(down.shape, down.dtype),
+            pltpu.SemaphoreType.DMA((2,)),
         ],
         compiler_params=pltpu.CompilerParams(vmem_limit_bytes=40 * 2**20),
         name="blocks",
-    )(edges, *[near(a) for a in arrays])
-
-
-def halo_of(x, north, south, seg):
+    )(edges, *[near(a) for a in arrays], far(up), far(down))
+
+
+def halo_of(x, north, south, inner, seg):
     rows, segs = lax.axis_size("y"), lax.axis_size("xc")
     reach = 2 * REACH
     down = [(i, i + 1) for i in range(rows - 1)]
     up = [(j, i) for i, j in down]
     top = lax.ppermute(south, "y", down)
     bottom = lax.ppermute(north, "y", up)
+    top, bottom, inner = lax.optimization_barrier((top, bottom, inner))
     east = [(i, (i + 1) % segs) for i in range(segs)]
     west = [(j, i) for i, j in east]
 
@@ -383,7 +455,7 @@
 
     left = lax.ppermute(columns(seg - reach), "xc", east)
     right = lax.ppermute(columns(0), "xc", west)
-    return top, bottom, left, right
+    return (top, bottom, left, right), inner
 
 
 def on_device(
@@ -424,8 +496,15 @@
     )
     x, north, south = [part.reshape(-1, slot, channels) for part in cells[:3]]
     filters = cells[3]
+    edge = 2 * REACH
+    reads = x.shape[0] - edge
+    cols = slot - 2 * 8
+    inner = run_middle([x], filters, x.shape[0], [(0, reads)], cols)
+    halos, inner = halo_of(x, north, south, inner, seg)
+    parts = [halos[0], x, halos[1]]
+    outer = run_middle(parts, filters, 4 * edge, [(0, edge), (2 * edge, edge)], cols)
     pieces = run_blocks(
-        edges, x, halo_of(x, north, south, seg), filters, mods,
+        edges, x, halos, filters, (inner, outer), mods,
         expand_weight, expand_bias, project_weight, project_bias, layer_scale, tiles,
     )
     pieces = lax.all_to_all(pieces.reshape(shape), around, 0, 0, tiled=True).reshape(-1, LANES)

time: 175 us -> 169 us (0.966)
  waiting for transfers between devices: 54.3 us -> 49.1 us
    pallas_call x1, Pallas kernels: 25.8 us -> 20.6 us  [run_blocks(): pl.pallas_call(lambda *refs: blocks_kernel(*refs, tiles=tiles), out_shape...]
    pallas_call x0 -> x2, Pallas kernels: none -> 5.13 us  [run_middle(): pl.pallas_call(lambda *refs: middle_kernel(*refs, bands=bands, tiles=cols...]
    ppermute x1, waiting for transfers between devices: 1.92 us -> 0.01 us  [halo_of(): top = lax.ppermute(south, 'y', down)]
  transfers between devices with their start and end apart: 5 -> 5, of which waited for: 5 -> 3; matrix products, arithmetic and copies ran while one was open for 0% -> 0% of each run, Pallas kernels for 0% -> 3%
where the time goes in v6:
time: 169 us; the launch traced here: 168 us
  blocking collectives  53.5 us (32%)
  waiting for transfers between devices  49.1 us (29%)
  Pallas kernels  34.9 us (21%)
  starting transfers between devices  24.9 us (15%)
  local copies, waits for them, and re-layouts  3.7 us (2%)
  between operations  2.07 us (1%)
    all_to_all x1, blocking collectives, on_device(): lax.all_to_all(pieces.reshape(shape), around, 0, 0, tiled=True)  53.5 us
    all_to_all x1, waiting for transfers between devices, on_device(): pieces = lax.all_to_all(pairs, around, 0, 0, tiled=True).reshape(-1, LANES)  44.2 us
    pallas_call x1, Pallas kernels, run_blocks(): pl.pallas_call(lambda *refs: blocks_kernel(*refs, tiles=tiles), out_shape...  20.6 us
    all_to_all x1, starting transfers between devices, on_device(): pieces = lax.all_to_all(pairs, around, 0, 0, tiled=True).reshape(-1, LANES)  19.3 us
    pallas_call x2, Pallas kernels, run_middle(): pl.pallas_call(lambda *refs: middle_kernel(*refs, bands=bands, tiles=cols...  5.13 us
    pallas_call x1, Pallas kernels, run_paste(): pl.pallas_call(lambda *refs: paste_kernel(*refs, seg=seg, slot=slot), out...  4.3 us
    pallas_call x1, Pallas kernels, run_cut(): pl.pallas_call(lambda *refs: cut_kernel(*refs, seg=seg, slot=slot), out_s...  4.24 us
  transfers between devices with their start and end apart: 5, of which 3 were waited for; matrix products, arithmetic and copies ran while one was open for 0% of the time, Pallas kernels for 3%

profile of v6, /device:TPU:33, one launch (start us, length us, event | category | flops | bytes accessed | tf_op | source)
XLA Modules:
  0.0 168.4 jit_solution(13012118555893645860)
XLA Ops:
  0.0 0.0 copy-start
  0.0 0.0 copy-start.4
  0.0 0.7 copy-done.4
  0.7 0.1 copy.13
  0.8 0.8 copy.12
  1.6 0.1 reshape.28
  1.7 0.1 pad.8.clone
  1.7 0.1 fusion.1
  1.8 0.6 reshape.29.refs_1_
  2.5 4.2 %cut.1 = bf16[3328,128]{1,0:T(8,128)(2,1)} custom-call(bf16[4,16,16,360]{3,2,1,0:T(8,128)(2,1)} %refs_0_.1, f32[2,128]{1,0:T(2,128)} %reshape.29.refs_1_), custom_call_target="tpu_custom_call" | custom-call | tf_op jit(solution)/shard_map/cut/pallas_call | solution.py:357
  6.7 19.3 %all-to-all-start = ((bf16[128,13,2,128]{3,2,1,0:T(2,128)(2,1)}), bf16[128,13,2,128]{3,2,1,0:T(2,128)(2,1)S(1)}, u32[]{:S(2)}, u32[]{:S(2)}) async-start(bf16[128,13,2,128]{3,2,1,0:T(2,128)(2,1)} %bitcast.3), calls=%async_computation | async-start | bytes 1703936 | tf_op jit(solution)/shard_map/all_to_all | solution.py:492
  26.0 0.0 copy-start.5
  26.0 0.6 copy-done.5
  26.7 0.6 dynamic_slice.11
  29.2 44.2 %all-to-all-done = bf16[128,13,2,128]{3,2,1,0:T(2,128)(2,1)S(1)} async-done(((bf16[128,13,2,128]{3,2,1,0:T(2,128)(2,1)}), bf16[128,13,2,128]{3,2,1,0:T(2,128)(2,1)S(1)}, u32[]{:S(2)}, u32[]{:S(2)}) %all-to-all-start) | async-done | bytes 852000 | tf_op jit(solution)/shard_map/all_to_all | solution.py:492
  73.4 0.6 to_cells.1
  74.0 3.2 %collective-permute-start = (bf16[6,48,256]{2,1,0:T(8,128)(2,1)S(1)}, bf16[6,48,256]{2,1,0:T(8,128)(2,1)S(1)}, u32[]{:S(2)}, u32[]{:S(2)}) collective-permute-start(bf16[6,48,256]{2,1,0:T(8,128)(2,1)S(1)} %bitcast.19), channel_id=1, source_target_pairs={{0,128},{128,256},{256,384},{1,129},{129,257},{257,385},{2,130},{1... | collective-permute-start | bytes 442376 | tf_op jit(solution)/shard_map/ppermute | solution.py:445
  77.2 1.3 collective-permute-start.1
  78.5 3.4 %middle.2.refs_7_ = f32[2,26,32,128]{3,2,1,0:T(8,128)S(1)} custom-call(bf16[32,48,256]{2,1,0:T(8,128)(2,1)S(1)} %bitcast.11, f32[2,56,256]{2,1,0:T(8,128)S(1)} %get-tuple-element.15.refs_1_.refs_3_.refs_6_), custom_call_target="tpu_custom_call" | custom-call | tf_op jit(solution)/shard_map/middle/pallas_call | solution.py:399
  81.9 0.0 collective-permute-done.refs_0_.refs_2_
  82.0 2.3 %collective-permute-done.1.refs_2_.refs_3_ = bf16[6,48,256]{2,1,0:T(8,128)(2,1)S(1)} collective-permute-done((bf16[6,48,256]{2,1,0:T(8,128)(2,1)S(1)}, bf16[6,48,256]{2,1,0:T(8,128)(2,1)S(1)}, u32[]{:S(2)}, u32[]{:S(2)}) %collective-permute-start.1) | collective-permute-done | bytes 147488 | tf_op jit(solution)/shard_map/ppermute | solution.py:446
  84.4 0.4 collective-permute-start.2
  84.8 0.7 collective-permute-start.3
  85.5 0.0 copy-done
  85.5 0.1 add_convert_fusion.refs_0_
  85.6 0.0 copy-start.1
  85.6 0.0 copy-start.2
  85.6 0.0 copy-start.3
  85.6 1.7 %middle.3.refs_8_ = f32[2,12,32,128]{3,2,1,0:T(8,128)S(1)} custom-call(bf16[6,48,256]{2,1,0:T(8,128)(2,1)S(1)} %collective-permute-done.refs_0_.refs_2_, bf16[32,48,256]{2,1,0:T(8,128)(2,1)S(1)} %bitcast.13, bf16[6,48,256]{2,1,0:T(8,128)(2,1)S(1)} %collective-permute-done.1.refs_2_.refs_3_, f32[2,56,256]{2,1,0:T(8,128)S(1)} %get-tuple-element.15.refs_1_.refs_3_.refs_6_), custom_call_target="tpu_custom_call" | custom-call | tf_op jit(solution)/shard_map/middle/pallas_call | solution.py:399
  87.4 0.0 collective-permute-done.2.refs_4_
  87.4 2.6 %collective-permute-done.3.refs_5_ = bf16[44,6,256]{2,1,0:T(8,128)(2,1)S(1)} collective-permute-done((bf16[44,6,256]{2,1,0:T(8,128)(2,1)S(1)}, bf16[44,6,256]{2,1,0:T(8,128)(2,1)S(1)}, u32[]{:S(2)}, u32[]{:S(2)}) %collective-permute-start.3) | collective-permute-done | bytes 135200 | tf_op jit(solution)/shard_map/ppermute | solution.py:457
  90.0 0.0 copy-done.1
  90.0 0.0 copy-done.2
  90.0 0.0 copy-done.3
  90.0 20.6 %blocks.1 = bf16[3072,128]{1,0:T(8,128)(2,1)S(1)} custom-call(s32[2]{0:T(128)S(1)} %add_convert_fusion.refs_0_, bf16[32,48,256]{2,1,0:T(8,128)(2,1)S(1)} %bitcast.14, bf16[6,48,256]{2,1,0:T(8,128)(2,1)S(1)} %collective-permute-done.refs_0_.refs_2_, bf16[6,48,256]{2,1,0:T(8,128)(2,1)S(1)} %collective-permute-done.1.refs_2_.refs_3_, ...), custom_call_target="tpu_custom_call" | custom-call | tf_op jit(solution)/shard_map/blocks/pallas_call | solution.py:418
  110.6 53.5 %all_to_all.10 = bf16[128,24,128]{2,1,0:T(8,128)(2,1)S(1)} all-to-all(bf16[128,24,128]{2,1,0:T(8,128)(2,1)S(1)} %bitcast.17), channel_id=1, replica_groups=mesh['y'=4,'zh'=2,'zl'=8,'xc'=8] {'zh','zl','xc'}, dimensions={0} | all-to-all | bytes 1572864 | tf_op jit(solution)/shard_map/all_to_all | solution.py:510
  164.1 4.3 %paste.1 = bf16[4,16,16,360]{3,2,1,0:T(8,128)(2,1)} custom-call(bf16[3072,128]{1,0:T(8,128)(2,1)S(1)} %bitcast.16), custom_call_target="tpu_custom_call" | custom-call | tf_op jit(solution)/shard_map/paste/pallas_call | solution.py:370
  (7 shorter events, 0.2 us)
Async XLA Ops:
  0.0 85.5 %copy-start = (f32[2,20,2,256]{3,2,1,0:T(2,128)S(1)}, f32[2,20,2,256]{3,2,1,0:T(2,128)}, u32[]{:S(2)}) copy-start(f32[2,20,2,256]{3,2,1,0:T(2,128)} %param.14) | copy-start | bytes 245764
  0.0 0.7 copy-start.4
  6.7 66.7 %all-to-all-start = ((bf16[128,13,2,128]{3,2,1,0:T(2,128)(2,1)}), bf16[128,13,2,128]{3,2,1,0:T(2,128)(2,1)S(1)}, u32[]{:S(2)}, u32[]{:S(2)}) async-start(bf16[128,13,2,128]{3,2,1,0:T(2,128)(2,1)} %bitcast.3), calls=%async_computation | async-start | bytes 1703936 | tf_op jit(solution)/shard_map/all_to_all | solution.py:492
  26.0 0.7 copy-start.5
  74.0 8.0 %collective-permute-start = (bf16[6,48,256]{2,1,0:T(8,128)(2,1)S(1)}, bf16[6,48,256]{2,1,0:T(8,128)(2,1)S(1)}, u32[]{:S(2)}, u32[]{:S(2)}) collective-permute-start(bf16[6,48,256]{2,1,0:T(8,128)(2,1)S(1)} %bitcast.19), channel_id=1, source_target_pairs={{0,128},{128,256},{256,384},{1,129},{129,257},{257,385},{2,130},{1... | collective-permute-start | bytes 442376 | tf_op jit(solution)/shard_map/ppermute | solution.py:445
  77.2 7.1 %collective-permute-start.1 = (bf16[6,48,256]{2,1,0:T(8,128)(2,1)S(1)}, bf16[6,48,256]{2,1,0:T(8,128)(2,1)S(1)}, u32[]{:S(2)}, u32[]{:S(2)}) collective-permute-start(bf16[6,48,256]{2,1,0:T(8,128)(2,1)S(1)} %bitcast.18), channel_id=1, source_target_pairs={{128,0},{256,128},{384,256},{129,1},{257,129},{385,257},{130,2},{2... | collective-permute-start | bytes 442376 | tf_op jit(solution)/shard_map/ppermute | solution.py:446
  84.4 3.0 %collective-permute-start.2 = (bf16[44,6,256]{2,1,0:T(8,128)(2,1)S(1)}, bf16[44,6,256]{2,1,0:T(8,128)(2,1)S(1)}, u32[]{:S(2)}, u32[]{:S(2)}) collective-permute-start(bf16[44,6,256]{2,1,0:T(8,128)(2,1)S(1)} %pad_maximum_fusion), channel_id=1, source_target_pairs={{0,1},{1,2},{2,3},{3,4},{4,5},{5,6},{6,7},{7,0},{8,9},{9,10},{10,1... | collective-permute-start | bytes 405512 | tf_op jit(solution)/shard_map/ppermute | solution.py:456
  84.8 5.2 %collective-permute-start.3 = (bf16[44,6,256]{2,1,0:T(8,128)(2,1)S(1)}, bf16[44,6,256]{2,1,0:T(8,128)(2,1)S(1)}, u32[]{:S(2)}, u32[]{:S(2)}) collective-permute-start(bf16[44,6,256]{2,1,0:T(8,128)(2,1)S(1)} %pad_maximum_fusion.1), channel_id=1, source_target_pairs={{1,0},{2,1},{3,2},{4,3},{5,4},{6,5},{7,6},{0,7},{9,8},{10,9},{11,1... | collective-permute-start | bytes 405512 | tf_op jit(solution)/shard_map/ppermute | solution.py:457
  85.6 4.4 %copy-start.1 = (f32[2,1024]{1,0:T(2,128)S(1)}, f32[2,1024]{1,0:T(2,128)}, u32[]{:S(2)}) copy-start(f32[2,1024]{1,0:T(2,128)} %refs_10_.1) | copy-start | bytes 24580
  85.6 4.4 %copy-start.2 = (f32[2,256]{1,0:T(2,128)S(1)}, f32[2,256]{1,0:T(2,128)}, u32[]{:S(2)}) copy-start(f32[2,256]{1,0:T(2,128)} %refs_11_.1) | copy-start | bytes 6148
  85.6 4.4 %copy-start.3 = (f32[2,256]{1,0:T(2,128)S(1)}, f32[2,256]{1,0:T(2,128)}, u32[]{:S(2)}) copy-start(f32[2,256]{1,0:T(2,128)} %refs_12_.1) | copy-start | bytes 6148

commit v7 on v6

--- a/solution.py
+++ b/solution.py
@@ -48,17 +48,42 @@
     return spans
 
 
-def cut_kernel(field_ref, filter_ref, out_ref, wide, cut, *, seg, slot):
+def filter_lines(taps, bias):
+    chans = bias.shape[1]
+    lines = jnp.zeros((chans, LANES), jnp.float32)
+    column = lax.broadcasted_iota(jnp.int32, (TAPS, LANES), 0)
+    lane = lax.broadcasted_iota(jnp.int32, (TAPS, LANES), 1)
+    for i in range(TAPS):
+        place = (lane == i * TAPS + column).astype(jnp.float32).astype(jnp.bfloat16)
+        lines = lines + jnp.dot(
+            taps[i].astype(jnp.bfloat16), place, preferred_element_type=jnp.float32
+        )
+    square = (chans, chans)
+    same = lax.broadcasted_iota(jnp.int32, square, 0) == lax.broadcasted_iota(jnp.int32, square, 1)
+    diagonal = jnp.where(same, jnp.broadcast_to(bias, square), 0.0)
+    own = jnp.sum(diagonal, axis=1, keepdims=True)
+    lanes = lane_iota(chans)
+    lines = jnp.where(lanes == TAPS * TAPS, jnp.broadcast_to(own, lines.shape), lines)
+    turned = pltpu.roll(lines, HALF_LANES, 1)
+    first = lane_iota(1) < HALF_LANES
+    return [
+        jnp.where(first, lines[c : c + 1], turned[c + 1 : c + 2]) for c in range(0, chans, 2)
+    ]
+
+
+def cut_kernel(layer_ref, field_ref, taps_ref, bias_ref, out_ref, wide, cut, *, seg, slot):
     chans, members, lats, lons = field_ref.shape
     rows = chans * members
     parts = -(-lons // LANES)
     segs = lons // seg
     tiles = lats * slot // LANES
-    extra = filter_ref.shape[0]
-    piece_rows = chans * tiles + extra
-    for e in range(extra):
+    layer = layer_ref[0]
+    bias = jnp.where(layer == 0, bias_ref[0:1, :], bias_ref[1:2, :])
+    lines = filter_lines([taps_ref[layer, i] for i in range(TAPS)], bias)
+    piece_rows = chans * tiles + len(lines)
+    for e, line in enumerate(lines):
         cut[pl.ds(chans * tiles + e, members * segs, stride=piece_rows), :] = jnp.broadcast_to(
-            filter_ref[e : e + 1, :], (members * segs, LANES)
+            line, (members * segs, LANES)
         )
     for a in range(parts):
         lo, hi = a * LANES, min((a + 1) * LANES, lons)
@@ -232,11 +257,7 @@
         rounded = jnp.concatenate(parts, axis=1).astype(jnp.bfloat16)
         average = jnp.dot(rounded, average_matrix, preferred_element_type=jnp.float32)
         centered = rounded.astype(jnp.float32) - average
-        variance = jnp.dot(
-            (centered * centered).astype(jnp.bfloat16),
-            average_matrix,
-            preferred_element_type=jnp.float32,
-        )
+        variance = jnp.mean(centered * centered, axis=1, keepdims=True)
         gain = 1.0 + mod_ref[2 * layer : 2 * layer + 1, :]
         shift = mod_ref[2 * layer + 1 : 2 * layer + 2, :]
         normed = (centered * lax.rsqrt(variance + EPS) * gain + shift).astype(jnp.bfloat16)
@@ -350,19 +371,21 @@
     return pltpu.with_memory_space_constraint(x, pltpu.HBM)
 
 
-def run_cut(field, filters, seg, slot):
+def run_cut(layer, field, taps, bias, seg, slot):
     chans, members, lats, lons = field.shape
     tiles = lats * slot // LANES
-    rows = members * (lons // seg) * (chans * tiles + filters.shape[0])
+    rows = members * (lons // seg) * (chans * tiles + chans // 2)
     return pl.pallas_call(
         lambda *refs: cut_kernel(*refs, seg=seg, slot=slot),
         out_shape=pltpu.VMEM((rows, LANES), jnp.bfloat16),
+        in_specs=[pl.BlockSpec(memory_space=pltpu.SMEM)]
+        + [pl.BlockSpec(memory_space=pltpu.VMEM)] * 3,
         scratch_shapes=[
             pltpu.VMEM((-(-lons // LANES), chans * members * lats, LANES), jnp.float32),
             pltpu.VMEM((rows, LANES), jnp.float32),
         ],
         name="cut",
-    )(field, filters)
+    )(layer, field, taps, bias)
 
 
 def run_paste(pieces, shape, seg, slot):
@@ -476,17 +499,8 @@
     band = lax.axis_index("y")
     edges = jnp.stack([band == 0, band == lax.axis_size("y") - 1]).astype(jnp.int32)
 
-    layer = lax.axis_index("zh")
-    filters = jnp.concatenate(
-        [
-            conv_kernel.reshape(layers, chans, TAPS * TAPS),
-            conv_bias[:, :, None],
-            jnp.zeros((layers, chans, HALF_LANES - TAPS * TAPS - 1), jnp.float32),
-        ],
-        axis=2,
-    )
-    filters = lax.dynamic_index_in_dim(filters, layer, 0, False).reshape(-1, LANES)
-    pieces = run_cut(field, filters, seg, slot)
+    layer = lax.axis_index("zh").astype(jnp.int32).reshape(1)
+    pieces = run_cut(layer, field, conv_kernel.transpose(0, 2, 1, 3), conv_bias, seg, slot)
     around = ("zh", "zl", "xc")
     pairs = pieces.reshape(peers, -1, 2, LANES)
     pieces = lax.all_to_all(pairs, around, 0, 0, tiled=True).reshape(-1, LANES)

time: 169 us -> 166 us (0.982)
  local copies, waits for them, and re-layouts: 3.7 us -> 1.33 us
where the time goes in v7:
time: 166 us; the launch traced here: 165 us
  blocking collectives  53.5 us (32%)
  waiting for transfers between devices  49.1 us (30%)
  Pallas kernels  34.2 us (21%)
  starting transfers between devices  24.9 us (15%)
  between operations  2.07 us (1%)
    all_to_all x1, blocking collectives, on_device(): lax.all_to_all(pieces.reshape(shape), around, 0, 0, tiled=True)  53.5 us
    all_to_all x1, waiting for transfers between devices, on_device(): pieces = lax.all_to_all(pairs, around, 0, 0, tiled=True).reshape(-1, LANES)  44.2 us
    pallas_call x1, Pallas kernels, run_blocks(): pl.pallas_call(lambda *refs: blocks_kernel(*refs, tiles=tiles), out_shape...  19.9 us
    all_to_all x1, starting transfers between devices, on_device(): pieces = lax.all_to_all(pairs, around, 0, 0, tiled=True).reshape(-1, LANES)  19.3 us
    pallas_call x2, Pallas kernels, run_middle(): pl.pallas_call(lambda *refs: middle_kernel(*refs, bands=bands, tiles=cols...  5.13 us
    pallas_call x1, Pallas kernels, run_paste(): pl.pallas_call(lambda *refs: paste_kernel(*refs, seg=seg, slot=slot), out...  4.3 us
    pallas_call x1, Pallas kernels, run_cut(): pl.pallas_call(lambda *refs: cut_kernel(*refs, seg=seg, slot=slot), out_s...  4.22 us
  transfers between devices with their start and end apart: 5, of which 3 were waited for; matrix products, arithmetic and copies ran while one was open for 0% of the time, Pallas kernels for 3%

profile of v7, /device:TPU:33, one launch (start us, length us, event | category | flops | bytes accessed | tf_op | source)
XLA Modules:
  0.0 165.3 jit_solution(14228548519572584257)
XLA Ops:
  0.0 0.0 copy-start
  0.0 4.2 %cut.1 = bf16[3328,128]{1,0:T(8,128)(2,1)} custom-call(s32[1]{0:T(128)} %bitcast.2.refs_0_, bf16[4,16,16,360]{3,2,1,0:T(8,128)(2,1)} %refs_1_.1, f32[2,7,4,7]{3,2,1,0:T(4,128)} %bitcast.21, f32[2,4]{1,0:T(2,128)} %refs_3_.1), custom_call_target="tpu_custom_call" | custom-call | tf_op jit(solution)/shard_map/cut/pallas_call | solution.py:378
  4.2 19.3 %all-to-all-start = ((bf16[128,13,2,128]{3,2,1,0:T(2,128)(2,1)}), bf16[128,13,2,128]{3,2,1,0:T(2,128)(2,1)S(1)}, u32[]{:S(2)}, u32[]{:S(2)}) async-start(bf16[128,13,2,128]{3,2,1,0:T(2,128)(2,1)} %bitcast.4), calls=%async_computation | async-start | bytes 1703936 | tf_op jit(solution)/shard_map/all_to_all | solution.py:506
  23.6 0.0 copy-start.4
  23.6 0.6 copy-done.4
  24.2 0.6 dynamic_slice.6
  26.7 44.2 %all-to-all-done = bf16[128,13,2,128]{3,2,1,0:T(2,128)(2,1)S(1)} async-done(((bf16[128,13,2,128]{3,2,1,0:T(2,128)(2,1)}), bf16[128,13,2,128]{3,2,1,0:T(2,128)(2,1)S(1)}, u32[]{:S(2)}, u32[]{:S(2)}) %all-to-all-start) | async-done | bytes 852000 | tf_op jit(solution)/shard_map/all_to_all | solution.py:506
  70.9 0.6 to_cells.1
  71.5 3.2 %collective-permute-start = (bf16[6,48,256]{2,1,0:T(8,128)(2,1)S(1)}, bf16[6,48,256]{2,1,0:T(8,128)(2,1)S(1)}, u32[]{:S(2)}, u32[]{:S(2)}) collective-permute-start(bf16[6,48,256]{2,1,0:T(8,128)(2,1)S(1)} %bitcast.20), channel_id=1, source_target_pairs={{0,128},{128,256},{256,384},{1,129},{129,257},{257,385},{2,130},{1... | collective-permute-start | bytes 442376 | tf_op jit(solution)/shard_map/ppermute | solution.py:468
  74.7 1.3 collective-permute-start.1
  76.0 3.4 %middle.2.refs_7_ = f32[2,26,32,128]{3,2,1,0:T(8,128)S(1)} custom-call(bf16[32,48,256]{2,1,0:T(8,128)(2,1)S(1)} %bitcast.12, f32[2,56,256]{2,1,0:T(8,128)S(1)} %get-tuple-element.15.refs_1_.refs_3_.refs_6_), custom_call_target="tpu_custom_call" | custom-call | tf_op jit(solution)/shard_map/middle/pallas_call | solution.py:422
  79.5 0.0 collective-permute-done.refs_0_.refs_2_
  79.5 2.3 %collective-permute-done.1.refs_2_.refs_3_ = bf16[6,48,256]{2,1,0:T(8,128)(2,1)S(1)} collective-permute-done((bf16[6,48,256]{2,1,0:T(8,128)(2,1)S(1)}, bf16[6,48,256]{2,1,0:T(8,128)(2,1)S(1)}, u32[]{:S(2)}, u32[]{:S(2)}) %collective-permute-start.1) | collective-permute-done | bytes 147488 | tf_op jit(solution)/shard_map/ppermute | solution.py:469
  81.9 0.4 collective-permute-start.2
  82.3 0.7 collective-permute-start.3
  83.0 0.0 copy-done
  83.1 0.1 add_convert_fusion.refs_0_
  83.1 0.0 copy-start.1
  83.1 0.0 copy-start.2
  83.1 0.0 copy-start.3
  83.1 1.7 %middle.3.refs_8_ = f32[2,12,32,128]{3,2,1,0:T(8,128)S(1)} custom-call(bf16[6,48,256]{2,1,0:T(8,128)(2,1)S(1)} %collective-permute-done.refs_0_.refs_2_, bf16[32,48,256]{2,1,0:T(8,128)(2,1)S(1)} %bitcast.14, bf16[6,48,256]{2,1,0:T(8,128)(2,1)S(1)} %collective-permute-done.1.refs_2_.refs_3_, f32[2,56,256]{2,1,0:T(8,128)S(1)} %get-tuple-element.15.refs_1_.refs_3_.refs_6_), custom_call_target="tpu_custom_call" | custom-call | tf_op jit(solution)/shard_map/middle/pallas_call | solution.py:422
  84.9 0.0 collective-permute-done.2.refs_4_
  84.9 2.6 %collective-permute-done.3.refs_5_ = bf16[44,6,256]{2,1,0:T(8,128)(2,1)S(1)} collective-permute-done((bf16[44,6,256]{2,1,0:T(8,128)(2,1)S(1)}, bf16[44,6,256]{2,1,0:T(8,128)(2,1)S(1)}, u32[]{:S(2)}, u32[]{:S(2)}) %collective-permute-start.3) | collective-permute-done | bytes 135200 | tf_op jit(solution)/shard_map/ppermute | solution.py:480
  87.6 0.0 copy-done.1
  87.6 0.0 copy-done.2
  87.6 0.0 copy-done.3
  87.6 19.9 %blocks.1 = bf16[3072,128]{1,0:T(8,128)(2,1)S(1)} custom-call(s32[2]{0:T(128)S(1)} %add_convert_fusion.refs_0_, bf16[32,48,256]{2,1,0:T(8,128)(2,1)S(1)} %bitcast.15, bf16[6,48,256]{2,1,0:T(8,128)(2,1)S(1)} %collective-permute-done.refs_0_.refs_2_, bf16[6,48,256]{2,1,0:T(8,128)(2,1)S(1)} %collective-permute-done.1.refs_2_.refs_3_, ...), custom_call_target="tpu_custom_call" | custom-call | tf_op jit(solution)/shard_map/blocks/pallas_call | solution.py:441
  107.5 53.5 %all_to_all.10 = bf16[128,24,128]{2,1,0:T(8,128)(2,1)S(1)} all-to-all(bf16[128,24,128]{2,1,0:T(8,128)(2,1)S(1)} %bitcast.18), channel_id=1, replica_groups=mesh['y'=4,'zh'=2,'zl'=8,'xc'=8] {'zh','zl','xc'}, dimensions={0} | all-to-all | bytes 1572864 | tf_op jit(solution)/shard_map/all_to_all | solution.py:524
  161.0 4.3 %paste.1 = bf16[4,16,16,360]{3,2,1,0:T(8,128)(2,1)} custom-call(bf16[3072,128]{1,0:T(8,128)(2,1)S(1)} %bitcast.17), custom_call_target="tpu_custom_call" | custom-call | tf_op jit(solution)/shard_map/paste/pallas_call | solution.py:393
  (6 shorter events, 0.2 us)
Async XLA Ops:
  0.0 83.0 %copy-start = (f32[2,20,2,256]{3,2,1,0:T(2,128)S(1)}, f32[2,20,2,256]{3,2,1,0:T(2,128)}, u32[]{:S(2)}) copy-start(f32[2,20,2,256]{3,2,1,0:T(2,128)} %param.14) | copy-start | bytes 245764
  4.2 66.7 %all-to-all-start = ((bf16[128,13,2,128]{3,2,1,0:T(2,128)(2,1)}), bf16[128,13,2,128]{3,2,1,0:T(2,128)(2,1)S(1)}, u32[]{:S(2)}, u32[]{:S(2)}) async-start(bf16[128,13,2,128]{3,2,1,0:T(2,128)(2,1)} %bitcast.4), calls=%async_computation | async-start | bytes 1703936 | tf_op jit(solution)/shard_map/all_to_all | solution.py:506
  23.6 0.7 copy-start.4
  71.5 8.0 %collective-permute-start = (bf16[6,48,256]{2,1,0:T(8,128)(2,1)S(1)}, bf16[6,48,256]{2,1,0:T(8,128)(2,1)S(1)}, u32[]{:S(2)}, u32[]{:S(2)}) collective-permute-start(bf16[6,48,256]{2,1,0:T(8,128)(2,1)S(1)} %bitcast.20), channel_id=1, source_target_pairs={{0,128},{128,256},{256,384},{1,129},{129,257},{257,385},{2,130},{1... | collective-permute-start | bytes 442376 | tf_op jit(solution)/shard_map/ppermute | solution.py:468
  74.7 7.1 %collective-permute-start.1 = (bf16[6,48,256]{2,1,0:T(8,128)(2,1)S(1)}, bf16[6,48,256]{2,1,0:T(8,128)(2,1)S(1)}, u32[]{:S(2)}, u32[]{:S(2)}) collective-permute-start(bf16[6,48,256]{2,1,0:T(8,128)(2,1)S(1)} %bitcast.19), channel_id=1, source_target_pairs={{128,0},{256,128},{384,256},{129,1},{257,129},{385,257},{130,2},{2... | collective-permute-start | bytes 442376 | tf_op jit(solution)/shard_map/ppermute | solution.py:469
  81.9 3.0 %collective-permute-start.2 = (bf16[44,6,256]{2,1,0:T(8,128)(2,1)S(1)}, bf16[44,6,256]{2,1,0:T(8,128)(2,1)S(1)}, u32[]{:S(2)}, u32[]{:S(2)}) collective-permute-start(bf16[44,6,256]{2,1,0:T(8,128)(2,1)S(1)} %pad_maximum_fusion), channel_id=1, source_target_pairs={{0,1},{1,2},{2,3},{3,4},{4,5},{5,6},{6,7},{7,0},{8,9},{9,10},{10,1... | collective-permute-start | bytes 405512 | tf_op jit(solution)/shard_map/ppermute | solution.py:479
  82.3 5.2 %collective-permute-start.3 = (bf16[44,6,256]{2,1,0:T(8,128)(2,1)S(1)}, bf16[44,6,256]{2,1,0:T(8,128)(2,1)S(1)}, u32[]{:S(2)}, u32[]{:S(2)}) collective-permute-start(bf16[44,6,256]{2,1,0:T(8,128)(2,1)S(1)} %pad_maximum_fusion.1), channel_id=1, source_target_pairs={{1,0},{2,1},{3,2},{4,3},{5,4},{6,5},{7,6},{0,7},{9,8},{10,9},{11,1... | collective-permute-start | bytes 405512 | tf_op jit(solution)/shard_map/ppermute | solution.py:480
  83.1 4.4 %copy-start.1 = (f32[2,1024]{1,0:T(2,128)S(1)}, f32[2,1024]{1,0:T(2,128)}, u32[]{:S(2)}) copy-start(f32[2,1024]{1,0:T(2,128)} %refs_10_.1) | copy-start | bytes 24580
  83.1 4.4 %copy-start.2 = (f32[2,256]{1,0:T(2,128)S(1)}, f32[2,256]{1,0:T(2,128)}, u32[]{:S(2)}) copy-start(f32[2,256]{1,0:T(2,128)} %refs_11_.1) | copy-start | bytes 6148
  83.1 4.4 %copy-start.3 = (f32[2,256]{1,0:T(2,128)S(1)}, f32[2,256]{1,0:T(2,128)}, u32[]{:S(2)}) copy-start(f32[2,256]{1,0:T(2,128)} %refs_12_.1) | copy-start | bytes 6148

commit v8 on v7

--- a/solution.py
+++ b/solution.py
@@ -10,7 +10,6 @@
 TAPS = 7
 REACH = 3
 LEFT = 8
-ROWS = 8
 HALF_LANES = 64
 TAP_ROWS = 56
 
@@ -243,17 +242,17 @@
     return [(top_ref, 0, edge), (x_ref, 0, edge), (x_ref, lats - edge, lats), (bottom_ref, 0, edge)]
 
 
-def pointwise(mixed, layer, lats, slot, residual, store, weights):
+def pointwise(mixed, layer, lats, rows, slot, residual, store, weights):
     mod_ref, up_ref, up_bias_ref, down_ref, down_bias_ref, scale_ref = weights
     groups = mixed.shape[0]
     channels = groups * LANES
-    cells = ROWS * slot
-    steps = -(-lats // ROWS)
+    cells = rows * slot
+    steps = -(-lats // rows)
     average_matrix = jnp.full((channels, channels), 1.0 / channels, jnp.bfloat16)
 
     def step_of(step, carry):
-        row = jnp.minimum(step * ROWS, lats - ROWS)
-        parts = [mixed[g, pl.ds(row, ROWS), 0:slot, :].reshape(cells, LANES) for g in range(groups)]
+        row = jnp.minimum(step * rows, lats - rows)
+        parts = [mixed[g, pl.ds(row, rows), 0:slot, :].reshape(cells, LANES) for g in range(groups)]
         rounded = jnp.concatenate(parts, axis=1).astype(jnp.bfloat16)
         average = jnp.dot(rounded, average_matrix, preferred_element_type=jnp.float32)
         centered = rounded.astype(jnp.float32) - average
@@ -272,7 +271,7 @@
         )
         branch = (scale_ref[layer : layer + 1, :] * result).astype(jnp.bfloat16).astype(jnp.float32)
         for g in range(groups):
-            part = branch[:, g * LANES : (g + 1) * LANES].reshape(ROWS, slot, LANES)
+            part = branch[:, g * LANES : (g + 1) * LANES].reshape(rows, slot, LANES)
             store(g, row, (residual(g, row) + part).astype(jnp.bfloat16).astype(jnp.float32))
         return carry
 
@@ -322,11 +321,11 @@
         copy.wait()
 
     def first_store(g, row, value):
-        second[g, pl.ds(row, ROWS), :, :] = value
+        second[g, pl.ds(row, 19), :, :] = value
 
     pointwise(
-        mixed, 0, wide, wide_slot,
-        lambda g, row: first[g, pl.ds(row + REACH, ROWS), LEFT - REACH : LEFT - REACH + wide_slot, :],
+        mixed, 0, wide, 19, wide_slot,
+        lambda g, row: first[g, pl.ds(row + REACH, 19), LEFT - REACH : LEFT - REACH + wide_slot, :],
         first_store, weights,
     )
 
@@ -341,11 +340,11 @@
     depthwise(second, spread, mixed, 1, [(0, lats)], range(slot // 8), 0)
 
     def final_store(g, row, value):
-        final[g, pl.ds(row, ROWS), :, :] = value
+        final[g, pl.ds(row, 32), :, :] = value
 
     pointwise(
-        mixed, 1, lats, slot,
-        lambda g, row: second[g, pl.ds(row + REACH, ROWS), REACH : REACH + slot, :],
+        mixed, 1, lats, 32, slot,
+        lambda g, row: second[g, pl.ds(row + REACH, 32), REACH : REACH + slot, :],
         final_store, weights,
     )
     flat = lats * slot // tiles // LANES

time: 166 us -> 163 us (0.982)
  Pallas kernels: 34.2 us -> 31.6 us
    pallas_call x1, Pallas kernels: 19.9 us -> 17.4 us  [run_blocks(): pl.pallas_call(lambda *refs: blocks_kernel(*refs, tiles=tiles), out_shape...]
where the time goes in v8:
time: 163 us
  blocking collectives  53.6 us (33%)
  waiting for transfers between devices  49.1 us (30%)
  Pallas kernels  31.6 us (19%)
  starting transfers between devices  24.9 us (15%)
  between operations  2.07 us (1%)
    all_to_all x1, blocking collectives, on_device(): lax.all_to_all(pieces.reshape(shape), around, 0, 0, tiled=True)  53.6 us
    all_to_all x1, waiting for transfers between devices, on_device(): pieces = lax.all_to_all(pairs, around, 0, 0, tiled=True).reshape(-1, LANES)  44.2 us
    all_to_all x1, starting transfers between devices, on_device(): pieces = lax.all_to_all(pairs, around, 0, 0, tiled=True).reshape(-1, LANES)  19.3 us
    pallas_call x1, Pallas kernels, run_blocks(): pl.pallas_call(lambda *refs: blocks_kernel(*refs, tiles=tiles), out_shape...  17.4 us
    pallas_call x2, Pallas kernels, run_middle(): pl.pallas_call(lambda *refs: middle_kernel(*refs, bands=bands, tiles=cols...  5.13 us
    pallas_call x1, Pallas kernels, run_paste(): pl.pallas_call(lambda *refs: paste_kernel(*refs, seg=seg, slot=slot), out...  4.3 us
    pallas_call x1, Pallas kernels, run_cut(): pl.pallas_call(lambda *refs: cut_kernel(*refs, seg=seg, slot=slot), out_s...  4.22 us
  transfers between devices with their start and end apart: 5, of which 3 were waited for; matrix products, arithmetic and copies ran while one was open for 0% of the time, Pallas kernels for 3%

profile of v8, /device:TPU:33, one launch (start us, length us, event | category | flops | bytes accessed | tf_op | source)
XLA Modules:
  0.0 162.9 jit_solution(11611647909825237379)
XLA Ops:
  0.0 0.0 copy-start
  0.0 4.2 %cut.1 = bf16[3328,128]{1,0:T(8,128)(2,1)} custom-call(s32[1]{0:T(128)} %bitcast.2.refs_0_, bf16[4,16,16,360]{3,2,1,0:T(8,128)(2,1)} %refs_1_.1, f32[2,7,4,7]{3,2,1,0:T(4,128)} %bitcast.21, f32[2,4]{1,0:T(2,128)} %refs_3_.1), custom_call_target="tpu_custom_call" | custom-call | tf_op jit(solution)/shard_map/cut/pallas_call | solution.py:377
  4.2 19.3 %all-to-all-start = ((bf16[128,13,2,128]{3,2,1,0:T(2,128)(2,1)}), bf16[128,13,2,128]{3,2,1,0:T(2,128)(2,1)S(1)}, u32[]{:S(2)}, u32[]{:S(2)}) async-start(bf16[128,13,2,128]{3,2,1,0:T(2,128)(2,1)} %bitcast.4), calls=%async_computation | async-start | bytes 1703936 | tf_op jit(solution)/shard_map/all_to_all | solution.py:505
  23.6 0.0 copy-start.4
  23.6 0.6 copy-done.4
  24.2 0.6 dynamic_slice.6
  26.7 44.2 %all-to-all-done = bf16[128,13,2,128]{3,2,1,0:T(2,128)(2,1)S(1)} async-done(((bf16[128,13,2,128]{3,2,1,0:T(2,128)(2,1)}), bf16[128,13,2,128]{3,2,1,0:T(2,128)(2,1)S(1)}, u32[]{:S(2)}, u32[]{:S(2)}) %all-to-all-start) | async-done | bytes 852000 | tf_op jit(solution)/shard_map/all_to_all | solution.py:505
  70.9 0.6 to_cells.1
  71.5 3.2 %collective-permute-start = (bf16[6,48,256]{2,1,0:T(8,128)(2,1)S(1)}, bf16[6,48,256]{2,1,0:T(8,128)(2,1)S(1)}, u32[]{:S(2)}, u32[]{:S(2)}) collective-permute-start(bf16[6,48,256]{2,1,0:T(8,128)(2,1)S(1)} %bitcast.20), channel_id=1, source_target_pairs={{0,128},{128,256},{256,384},{1,129},{129,257},{257,385},{2,130},{1... | collective-permute-start | bytes 442376 | tf_op jit(solution)/shard_map/ppermute | solution.py:467
  74.7 1.3 collective-permute-start.1
  76.0 3.4 %middle.2.refs_7_ = f32[2,26,32,128]{3,2,1,0:T(8,128)S(1)} custom-call(bf16[32,48,256]{2,1,0:T(8,128)(2,1)S(1)} %bitcast.12, f32[2,56,256]{2,1,0:T(8,128)S(1)} %get-tuple-element.15.refs_1_.refs_3_.refs_6_), custom_call_target="tpu_custom_call" | custom-call | tf_op jit(solution)/shard_map/middle/pallas_call | solution.py:421
  79.5 0.0 collective-permute-done.refs_0_.refs_2_
  79.5 2.3 %collective-permute-done.1.refs_2_.refs_3_ = bf16[6,48,256]{2,1,0:T(8,128)(2,1)S(1)} collective-permute-done((bf16[6,48,256]{2,1,0:T(8,128)(2,1)S(1)}, bf16[6,48,256]{2,1,0:T(8,128)(2,1)S(1)}, u32[]{:S(2)}, u32[]{:S(2)}) %collective-permute-start.1) | collective-permute-done | bytes 147488 | tf_op jit(solution)/shard_map/ppermute | solution.py:468
  81.9 0.4 collective-permute-start.2
  82.3 0.7 collective-permute-start.3
  83.0 0.0 copy-done
  83.1 0.1 add_convert_fusion.refs_0_
  83.1 0.0 copy-start.1
  83.1 0.0 copy-start.2
  83.1 0.0 copy-start.3
  83.1 1.7 %middle.3.refs_8_ = f32[2,12,32,128]{3,2,1,0:T(8,128)S(1)} custom-call(bf16[6,48,256]{2,1,0:T(8,128)(2,1)S(1)} %collective-permute-done.refs_0_.refs_2_, bf16[32,48,256]{2,1,0:T(8,128)(2,1)S(1)} %bitcast.14, bf16[6,48,256]{2,1,0:T(8,128)(2,1)S(1)} %collective-permute-done.1.refs_2_.refs_3_, f32[2,56,256]{2,1,0:T(8,128)S(1)} %get-tuple-element.15.refs_1_.refs_3_.refs_6_), custom_call_target="tpu_custom_call" | custom-call | tf_op jit(solution)/shard_map/middle/pallas_call | solution.py:421
  84.9 0.0 collective-permute-done.2.refs_4_
  84.9 2.6 %collective-permute-done.3.refs_5_ = bf16[44,6,256]{2,1,0:T(8,128)(2,1)S(1)} collective-permute-done((bf16[44,6,256]{2,1,0:T(8,128)(2,1)S(1)}, bf16[44,6,256]{2,1,0:T(8,128)(2,1)S(1)}, u32[]{:S(2)}, u32[]{:S(2)}) %collective-permute-start.3) | collective-permute-done | bytes 135200 | tf_op jit(solution)/shard_map/ppermute | solution.py:479
  87.6 0.0 copy-done.1
  87.6 0.0 copy-done.2
  87.6 0.0 copy-done.3
  87.6 17.4 %blocks.1 = bf16[3072,128]{1,0:T(8,128)(2,1)S(1)} custom-call(s32[2]{0:T(128)S(1)} %add_convert_fusion.refs_0_, bf16[32,48,256]{2,1,0:T(8,128)(2,1)S(1)} %bitcast.15, bf16[6,48,256]{2,1,0:T(8,128)(2,1)S(1)} %collective-permute-done.refs_0_.refs_2_, bf16[6,48,256]{2,1,0:T(8,128)(2,1)S(1)} %collective-permute-done.1.refs_2_.refs_3_, ...), custom_call_target="tpu_custom_call" | custom-call | tf_op jit(solution)/shard_map/blocks/pallas_call | solution.py:440
  104.9 53.6 %all_to_all.10 = bf16[128,24,128]{2,1,0:T(8,128)(2,1)S(1)} all-to-all(bf16[128,24,128]{2,1,0:T(8,128)(2,1)S(1)} %bitcast.18), channel_id=1, replica_groups=mesh['y'=4,'zh'=2,'zl'=8,'xc'=8] {'zh','zl','xc'}, dimensions={0} | all-to-all | bytes 1572864 | tf_op jit(solution)/shard_map/all_to_all | solution.py:523
  158.6 4.3 %paste.1 = bf16[4,16,16,360]{3,2,1,0:T(8,128)(2,1)} custom-call(bf16[3072,128]{1,0:T(8,128)(2,1)S(1)} %bitcast.17), custom_call_target="tpu_custom_call" | custom-call | tf_op jit(solution)/shard_map/paste/pallas_call | solution.py:392
  (6 shorter events, 0.2 us)
Async XLA Ops:
  0.0 83.0 %copy-start = (f32[2,20,2,256]{3,2,1,0:T(2,128)S(1)}, f32[2,20,2,256]{3,2,1,0:T(2,128)}, u32[]{:S(2)}) copy-start(f32[2,20,2,256]{3,2,1,0:T(2,128)} %param.14) | copy-start | bytes 245764
  4.2 66.7 %all-to-all-start = ((bf16[128,13,2,128]{3,2,1,0:T(2,128)(2,1)}), bf16[128,13,2,128]{3,2,1,0:T(2,128)(2,1)S(1)}, u32[]{:S(2)}, u32[]{:S(2)}) async-start(bf16[128,13,2,128]{3,2,1,0:T(2,128)(2,1)} %bitcast.4), calls=%async_computation | async-start | bytes 1703936 | tf_op jit(solution)/shard_map/all_to_all | solution.py:505
  23.6 0.7 copy-start.4
  71.5 8.0 %collective-permute-start = (bf16[6,48,256]{2,1,0:T(8,128)(2,1)S(1)}, bf16[6,48,256]{2,1,0:T(8,128)(2,1)S(1)}, u32[]{:S(2)}, u32[]{:S(2)}) collective-permute-start(bf16[6,48,256]{2,1,0:T(8,128)(2,1)S(1)} %bitcast.20), channel_id=1, source_target_pairs={{0,128},{128,256},{256,384},{1,129},{129,257},{257,385},{2,130},{1... | collective-permute-start | bytes 442376 | tf_op jit(solution)/shard_map/ppermute | solution.py:467
  74.7 7.1 %collective-permute-start.1 = (bf16[6,48,256]{2,1,0:T(8,128)(2,1)S(1)}, bf16[6,48,256]{2,1,0:T(8,128)(2,1)S(1)}, u32[]{:S(2)}, u32[]{:S(2)}) collective-permute-start(bf16[6,48,256]{2,1,0:T(8,128)(2,1)S(1)} %bitcast.19), channel_id=1, source_target_pairs={{128,0},{256,128},{384,256},{129,1},{257,129},{385,257},{130,2},{2... | collective-permute-start | bytes 442376 | tf_op jit(solution)/shard_map/ppermute | solution.py:468
  81.9 3.0 %collective-permute-start.2 = (bf16[44,6,256]{2,1,0:T(8,128)(2,1)S(1)}, bf16[44,6,256]{2,1,0:T(8,128)(2,1)S(1)}, u32[]{:S(2)}, u32[]{:S(2)}) collective-permute-start(bf16[44,6,256]{2,1,0:T(8,128)(2,1)S(1)} %pad_maximum_fusion), channel_id=1, source_target_pairs={{0,1},{1,2},{2,3},{3,4},{4,5},{5,6},{6,7},{7,0},{8,9},{9,10},{10,1... | collective-permute-start | bytes 405512 | tf_op jit(solution)/shard_map/ppermute | solution.py:478
  82.3 5.2 %collective-permute-start.3 = (bf16[44,6,256]{2,1,0:T(8,128)(2,1)S(1)}, bf16[44,6,256]{2,1,0:T(8,128)(2,1)S(1)}, u32[]{:S(2)}, u32[]{:S(2)}) collective-permute-start(bf16[44,6,256]{2,1,0:T(8,128)(2,1)S(1)} %pad_maximum_fusion.1), channel_id=1, source_target_pairs={{1,0},{2,1},{3,2},{4,3},{5,4},{6,5},{7,6},{0,7},{9,8},{10,9},{11,1... | collective-permute-start | bytes 405512 | tf_op jit(solution)/shard_map/ppermute | solution.py:479
  83.1 4.4 %copy-start.1 = (f32[2,1024]{1,0:T(2,128)S(1)}, f32[2,1024]{1,0:T(2,128)}, u32[]{:S(2)}) copy-start(f32[2,1024]{1,0:T(2,128)} %refs_10_.1) | copy-start | bytes 24580
  83.1 4.4 %copy-start.2 = (f32[2,256]{1,0:T(2,128)S(1)}, f32[2,256]{1,0:T(2,128)}, u32[]{:S(2)}) copy-start(f32[2,256]{1,0:T(2,128)} %refs_11_.1) | copy-start | bytes 6148
  83.1 4.4 %copy-start.3 = (f32[2,256]{1,0:T(2,128)S(1)}, f32[2,256]{1,0:T(2,128)}, u32[]{:S(2)}) copy-start(f32[2,256]{1,0:T(2,128)} %refs_12_.1) | copy-start | bytes 6148

commit v9 on v8

--- a/solution.py
+++ b/solution.py
@@ -314,18 +314,17 @@
     wide_slot = slot + 8
     covered = inner_ref.shape[2] // 8
     sides = [k for k in range(wide_slot // 8) if not 1 <= k <= covered]
-    depthwise(first, spread, mixed, 0, [(0, wide // 2)], sides, LEFT - reach)
-    depthwise(first, spread, mixed, 0, [(wide // 2, wide - wide // 2)], sides, LEFT - reach)
+    depthwise(first, spread, mixed, 0, [(0, wide)], sides, LEFT - reach)
 
     for copy in copies:
         copy.wait()
 
     def first_store(g, row, value):
-        second[g, pl.ds(row, 19), :, :] = value
+        second[g, pl.ds(row, 38), :, :] = value
 
     pointwise(
-        mixed, 0, wide, 19, wide_slot,
-        lambda g, row: first[g, pl.ds(row + REACH, 19), LEFT - REACH : LEFT - REACH + wide_slot, :],
+        mixed, 0, wide, 38, wide_slot,
+        lambda g, row: first[g, pl.ds(row + REACH, 38), LEFT - REACH : LEFT - REACH + wide_slot, :],
         first_store, weights,
     )
 

time: 163 us -> 163 us (level)
  no operation moved by 1% of the time
where the time goes in v9:
time: 163 us; the launch traced here: 162 us
  blocking collectives  53.5 us (33%)
  waiting for transfers between devices  49.1 us (30%)
  Pallas kernels  31.2 us (19%)
  starting transfers between devices  24.9 us (15%)
  between operations  2.07 us (1%)
    all_to_all x1, blocking collectives, on_device(): lax.all_to_all(pieces.reshape(shape), around, 0, 0, tiled=True)  53.5 us
    all_to_all x1, waiting for transfers between devices, on_device(): pieces = lax.all_to_all(pairs, around, 0, 0, tiled=True).reshape(-1, LANES)  44.2 us
    all_to_all x1, starting transfers between devices, on_device(): pieces = lax.all_to_all(pairs, around, 0, 0, tiled=True).reshape(-1, LANES)  19.3 us
    pallas_call x1, Pallas kernels, run_blocks(): pl.pallas_call(lambda *refs: blocks_kernel(*refs, tiles=tiles), out_shape...  16.9 us
    pallas_call x2, Pallas kernels, run_middle(): pl.pallas_call(lambda *refs: middle_kernel(*refs, bands=bands, tiles=cols...  5.13 us
    pallas_call x1, Pallas kernels, run_paste(): pl.pallas_call(lambda *refs: paste_kernel(*refs, seg=seg, slot=slot), out...  4.3 us
    pallas_call x1, Pallas kernels, run_cut(): pl.pallas_call(lambda *refs: cut_kernel(*refs, seg=seg, slot=slot), out_s...  4.22 us
  transfers between devices with their start and end apart: 5, of which 3 were waited for; matrix products, arithmetic and copies ran while one was open for 0% of the time, Pallas kernels for 3%

profile of v9, /device:TPU:33, one launch (start us, length us, event | category | flops | bytes accessed | tf_op | source)
XLA Modules:
  0.0 162.3 jit_solution(1976699269517564251)
XLA Ops:
  0.0 0.0 copy-start
  0.0 4.2 %cut.1 = bf16[3328,128]{1,0:T(8,128)(2,1)} custom-call(s32[1]{0:T(128)} %bitcast.2.refs_0_, bf16[4,16,16,360]{3,2,1,0:T(8,128)(2,1)} %refs_1_.1, f32[2,7,4,7]{3,2,1,0:T(4,128)} %bitcast.21, f32[2,4]{1,0:T(2,128)} %refs_3_.1), custom_call_target="tpu_custom_call" | custom-call | tf_op jit(solution)/shard_map/cut/pallas_call | solution.py:376
  4.2 19.3 %all-to-all-start = ((bf16[128,13,2,128]{3,2,1,0:T(2,128)(2,1)}), bf16[128,13,2,128]{3,2,1,0:T(2,128)(2,1)S(1)}, u32[]{:S(2)}, u32[]{:S(2)}) async-start(bf16[128,13,2,128]{3,2,1,0:T(2,128)(2,1)} %bitcast.4), calls=%async_computation | async-start | bytes 1703936 | tf_op jit(solution)/shard_map/all_to_all | solution.py:504
  23.6 0.0 copy-start.4
  23.6 0.6 copy-done.4
  24.2 0.6 dynamic_slice.6
  26.7 44.2 %all-to-all-done = bf16[128,13,2,128]{3,2,1,0:T(2,128)(2,1)S(1)} async-done(((bf16[128,13,2,128]{3,2,1,0:T(2,128)(2,1)}), bf16[128,13,2,128]{3,2,1,0:T(2,128)(2,1)S(1)}, u32[]{:S(2)}, u32[]{:S(2)}) %all-to-all-start) | async-done | bytes 852000 | tf_op jit(solution)/shard_map/all_to_all | solution.py:504
  70.9 0.6 to_cells.1
  71.5 3.2 %collective-permute-start = (bf16[6,48,256]{2,1,0:T(8,128)(2,1)S(1)}, bf16[6,48,256]{2,1,0:T(8,128)(2,1)S(1)}, u32[]{:S(2)}, u32[]{:S(2)}) collective-permute-start(bf16[6,48,256]{2,1,0:T(8,128)(2,1)S(1)} %bitcast.20), channel_id=1, source_target_pairs={{0,128},{128,256},{256,384},{1,129},{129,257},{257,385},{2,130},{1... | collective-permute-start | bytes 442376 | tf_op jit(solution)/shard_map/ppermute | solution.py:466
  74.7 1.3 collective-permute-start.1
  76.0 3.4 %middle.2.refs_7_ = f32[2,26,32,128]{3,2,1,0:T(8,128)S(1)} custom-call(bf16[32,48,256]{2,1,0:T(8,128)(2,1)S(1)} %bitcast.12, f32[2,56,256]{2,1,0:T(8,128)S(1)} %get-tuple-element.15.refs_1_.refs_3_.refs_6_), custom_call_target="tpu_custom_call" | custom-call | tf_op jit(solution)/shard_map/middle/pallas_call | solution.py:420
  79.5 0.0 collective-permute-done.refs_0_.refs_2_
  79.5 2.3 %collective-permute-done.1.refs_2_.refs_3_ = bf16[6,48,256]{2,1,0:T(8,128)(2,1)S(1)} collective-permute-done((bf16[6,48,256]{2,1,0:T(8,128)(2,1)S(1)}, bf16[6,48,256]{2,1,0:T(8,128)(2,1)S(1)}, u32[]{:S(2)}, u32[]{:S(2)}) %collective-permute-start.1) | collective-permute-done | bytes 147488 | tf_op jit(solution)/shard_map/ppermute | solution.py:467
  81.9 0.4 collective-permute-start.2
  82.3 0.7 collective-permute-start.3
  83.0 0.0 copy-done
  83.1 0.1 add_convert_fusion.refs_0_
  83.1 0.0 copy-start.1
  83.1 0.0 copy-start.2
  83.1 0.0 copy-start.3
  83.1 1.7 %middle.3.refs_8_ = f32[2,12,32,128]{3,2,1,0:T(8,128)S(1)} custom-call(bf16[6,48,256]{2,1,0:T(8,128)(2,1)S(1)} %collective-permute-done.refs_0_.refs_2_, bf16[32,48,256]{2,1,0:T(8,128)(2,1)S(1)} %bitcast.14, bf16[6,48,256]{2,1,0:T(8,128)(2,1)S(1)} %collective-permute-done.1.refs_2_.refs_3_, f32[2,56,256]{2,1,0:T(8,128)S(1)} %get-tuple-element.15.refs_1_.refs_3_.refs_6_), custom_call_target="tpu_custom_call" | custom-call | tf_op jit(solution)/shard_map/middle/pallas_call | solution.py:420
  84.9 0.0 collective-permute-done.2.refs_4_
  84.9 2.6 %collective-permute-done.3.refs_5_ = bf16[44,6,256]{2,1,0:T(8,128)(2,1)S(1)} collective-permute-done((bf16[44,6,256]{2,1,0:T(8,128)(2,1)S(1)}, bf16[44,6,256]{2,1,0:T(8,128)(2,1)S(1)}, u32[]{:S(2)}, u32[]{:S(2)}) %collective-permute-start.3) | collective-permute-done | bytes 135200 | tf_op jit(solution)/shard_map/ppermute | solution.py:478
  87.6 0.0 copy-done.1
  87.6 0.0 copy-done.2
  87.6 0.0 copy-done.3
  87.6 16.9 %blocks.1 = bf16[3072,128]{1,0:T(8,128)(2,1)S(1)} custom-call(s32[2]{0:T(128)S(1)} %add_convert_fusion.refs_0_, bf16[32,48,256]{2,1,0:T(8,128)(2,1)S(1)} %bitcast.15, bf16[6,48,256]{2,1,0:T(8,128)(2,1)S(1)} %collective-permute-done.refs_0_.refs_2_, bf16[6,48,256]{2,1,0:T(8,128)(2,1)S(1)} %collective-permute-done.1.refs_2_.refs_3_, ...), custom_call_target="tpu_custom_call" | custom-call | tf_op jit(solution)/shard_map/blocks/pallas_call | solution.py:439
  104.5 53.5 %all_to_all.10 = bf16[128,24,128]{2,1,0:T(8,128)(2,1)S(1)} all-to-all(bf16[128,24,128]{2,1,0:T(8,128)(2,1)S(1)} %bitcast.18), channel_id=1, replica_groups=mesh['y'=4,'zh'=2,'zl'=8,'xc'=8] {'zh','zl','xc'}, dimensions={0} | all-to-all | bytes 1572864 | tf_op jit(solution)/shard_map/all_to_all | solution.py:522
  158.0 4.3 %paste.1 = bf16[4,16,16,360]{3,2,1,0:T(8,128)(2,1)} custom-call(bf16[3072,128]{1,0:T(8,128)(2,1)S(1)} %bitcast.17), custom_call_target="tpu_custom_call" | custom-call | tf_op jit(solution)/shard_map/paste/pallas_call | solution.py:391
  (6 shorter events, 0.2 us)
Async XLA Ops:
  0.0 83.0 %copy-start = (f32[2,20,2,256]{3,2,1,0:T(2,128)S(1)}, f32[2,20,2,256]{3,2,1,0:T(2,128)}, u32[]{:S(2)}) copy-start(f32[2,20,2,256]{3,2,1,0:T(2,128)} %param.14) | copy-start | bytes 245764
  4.2 66.7 %all-to-all-start = ((bf16[128,13,2,128]{3,2,1,0:T(2,128)(2,1)}), bf16[128,13,2,128]{3,2,1,0:T(2,128)(2,1)S(1)}, u32[]{:S(2)}, u32[]{:S(2)}) async-start(bf16[128,13,2,128]{3,2,1,0:T(2,128)(2,1)} %bitcast.4), calls=%async_computation | async-start | bytes 1703936 | tf_op jit(solution)/shard_map/all_to_all | solution.py:504
  23.6 0.7 copy-start.4
  71.5 8.0 %collective-permute-start = (bf16[6,48,256]{2,1,0:T(8,128)(2,1)S(1)}, bf16[6,48,256]{2,1,0:T(8,128)(2,1)S(1)}, u32[]{:S(2)}, u32[]{:S(2)}) collective-permute-start(bf16[6,48,256]{2,1,0:T(8,128)(2,1)S(1)} %bitcast.20), channel_id=1, source_target_pairs={{0,128},{128,256},{256,384},{1,129},{129,257},{257,385},{2,130},{1... | collective-permute-start | bytes 442376 | tf_op jit(solution)/shard_map/ppermute | solution.py:466
  74.7 7.1 %collective-permute-start.1 = (bf16[6,48,256]{2,1,0:T(8,128)(2,1)S(1)}, bf16[6,48,256]{2,1,0:T(8,128)(2,1)S(1)}, u32[]{:S(2)}, u32[]{:S(2)}) collective-permute-start(bf16[6,48,256]{2,1,0:T(8,128)(2,1)S(1)} %bitcast.19), channel_id=1, source_target_pairs={{128,0},{256,128},{384,256},{129,1},{257,129},{385,257},{130,2},{2... | collective-permute-start | bytes 442376 | tf_op jit(solution)/shard_map/ppermute | solution.py:467
  81.9 3.0 %collective-permute-start.2 = (bf16[44,6,256]{2,1,0:T(8,128)(2,1)S(1)}, bf16[44,6,256]{2,1,0:T(8,128)(2,1)S(1)}, u32[]{:S(2)}, u32[]{:S(2)}) collective-permute-start(bf16[44,6,256]{2,1,0:T(8,128)(2,1)S(1)} %pad_maximum_fusion), channel_id=1, source_target_pairs={{0,1},{1,2},{2,3},{3,4},{4,5},{5,6},{6,7},{7,0},{8,9},{9,10},{10,1... | collective-permute-start | bytes 405512 | tf_op jit(solution)/shard_map/ppermute | solution.py:477
  82.3 5.2 %collective-permute-start.3 = (bf16[44,6,256]{2,1,0:T(8,128)(2,1)S(1)}, bf16[44,6,256]{2,1,0:T(8,128)(2,1)S(1)}, u32[]{:S(2)}, u32[]{:S(2)}) collective-permute-start(bf16[44,6,256]{2,1,0:T(8,128)(2,1)S(1)} %pad_maximum_fusion.1), channel_id=1, source_target_pairs={{1,0},{2,1},{3,2},{4,3},{5,4},{6,5},{7,6},{0,7},{9,8},{10,9},{11,1... | collective-permute-start | bytes 405512 | tf_op jit(solution)/shard_map/ppermute | solution.py:478
  83.1 4.4 %copy-start.1 = (f32[2,1024]{1,0:T(2,128)S(1)}, f32[2,1024]{1,0:T(2,128)}, u32[]{:S(2)}) copy-start(f32[2,1024]{1,0:T(2,128)} %refs_10_.1) | copy-start | bytes 24580
  83.1 4.4 %copy-start.2 = (f32[2,256]{1,0:T(2,128)S(1)}, f32[2,256]{1,0:T(2,128)}, u32[]{:S(2)}) copy-start(f32[2,256]{1,0:T(2,128)} %refs_11_.1) | copy-start | bytes 6148
  83.1 4.4 %copy-start.3 = (f32[2,256]{1,0:T(2,128)S(1)}, f32[2,256]{1,0:T(2,128)}, u32[]{:S(2)}) copy-start(f32[2,256]{1,0:T(2,128)} %refs_12_.1) | copy-start | bytes 6148
